TPU v7x, 32 devices: a whole 2x2x4 slice. The times are simulated.
32 devices in a mesh: clips: 2 (over y), tile: 4 (over x, core), tm: 4 (over z).
Axes of the slice: x: 2, y: 2, z: 4, core: 2. Of those that a mesh axis runs over, the one named last changes fastest.
Arguments:
- frames: bfloat16 [8, 120, 32, 128], P(('clips', 'tm'), None, 'tile'), parts along dimension 0, may hold values from -6 to 6
- ln_gain: float32 [2, 2, 120], replicated, may hold values from 0.5 to 1.5
- qkv_weight: bfloat16 [2, 120, 360], replicated, may hold values from -4 to 4
- out_weight: bfloat16 [2, 120, 120], replicated, may hold values from -0.5 to 0.5
- gate_weight: bfloat16 [2, 120, 240], replicated, may hold values from -0.5 to 0.5
- up_weight: bfloat16 [2, 120, 240], replicated, may hold values from -0.5 to 0.5
- down_weight: bfloat16 [2, 240, 120], replicated, may hold values from -0.375 to 0.375
- conv_weight: bfloat16 [2, 9, 120, 120], replicated, may hold values from -0.1875 to 0.1875
- conv_bias: float32 [2, 120], replicated, may hold values from -3 to 3
Outputs:
- restored: bfloat16 [8, 120, 32, 128], P(('clips', 'tm'), None, 'tile'), parts along dimension 0
There are 2 independent parts, one for each index of `clips`. A program takes and returns all parts, laid end to end along the dimension named above; an argument that names none is the same for every part. Nothing has to cross between parts.
All inputs are finite; a program needn't handle non-finite values.
Results may differ from a plain program's by a relative error of at most 0.0084.
Values may be sent and summed in bfloat16 or wider, within the bound.
No kernel may reach another device: no remote copies, remote signals or barrier semaphores. Data moves between devices by JAX's collectives and lax.ppermute only.
A program may use at most 64 MiB of HBM per device.

v0:
```python
import jax
import jax.numpy as jnp
from jax import lax
from jax.experimental import pallas as pl
from jax.experimental.pallas import tpu as pltpu
from jax.sharding import PartitionSpec as P

HEADS = 6
HD = 20
LAYERS = 2
WIN = 8
LANES = 128
BF = jnp.bfloat16
F32 = jnp.float32
NT = (((1,), (1,)), ((), ()))


def up(n):
    return -(-n // LANES) * LANES


def dot(a, b):
    return jnp.dot(a, b, preferred_element_type=F32)


def dot_nt(a, b):
    return lax.dot_general(a, b, NT, preferred_element_type=F32)


def norm(x, gain, channels):
    lane = lax.broadcasted_iota(jnp.int32, x.shape, x.ndim - 1)
    mean = jnp.sum(x, axis=-1, keepdims=True) * (1.0 / channels)
    center = jnp.where(lane < channels, x - mean, 0.0)
    spread = jnp.sum(center * center, axis=-1, keepdims=True) * (1.0 / channels)
    return center * lax.rsqrt(spread + 1e-05) * gain


def to_positions(ref):
    x = ref[0].astype(F32)
    channels, rows, cols = x.shape
    x = jnp.concatenate([x, jnp.zeros((LANES - channels, rows, cols), F32)], axis=0)
    x = jnp.swapaxes(x, 0, 1)
    return jnp.stack([x[r].T for r in range(rows)], axis=0)


def windows(x):
    rows, cols, lanes = x.shape
    x = x.reshape(rows, cols // WIN, WIN, lanes)
    return jnp.swapaxes(x, 0, 1).reshape(cols // WIN, rows * WIN, lanes)


def unwindows(x, rows):
    count, _, lanes = x.shape
    x = jnp.swapaxes(x.reshape(count, rows, WIN, lanes), 0, 1)
    return x.reshape(rows, count * WIN, lanes)


def pad2(x, rows, cols):
    x = x.astype(F32)
    if x.shape[1] < cols:
        x = jnp.concatenate([x, jnp.zeros((x.shape[0], cols - x.shape[1]), F32)], axis=1)
    if x.shape[0] < rows:
        x = jnp.concatenate([x, jnp.zeros((rows - x.shape[0], cols), F32)], axis=0)
    return x


def weights_body(gain, qkv, out, gate, upw, down, conv, bias, o_gain, o_qk, o_vt, o_out, o_gu, o_down, o_conv, o_bias):
    layers, channels, _ = out.shape
    hidden = gate.shape[2]
    hp = up(hidden)
    for l in range(layers):
        o_gain[l] = pad2(gain[l], 2, LANES)
        o_bias[l] = pad2(bias[l : l + 1], 1, LANES)
        w = qkv[l].astype(F32)
        o_qk[l, :, :LANES] = pad2(w[:, :channels], LANES, LANES).astype(BF)
        o_qk[l, :, LANES:] = pad2(w[:, channels : 2 * channels], LANES, LANES).astype(BF)
        o_vt[l] = pad2(w[:, 2 * channels :], LANES, LANES).T.astype(BF)
        o_out[l] = pad2(out[l], LANES, LANES).astype(BF)
        o_gu[l, :, :hp] = pad2(gate[l], LANES, hp).astype(BF)
        o_gu[l, :, hp:] = pad2(upw[l], LANES, hp).astype(BF)
        o_down[l] = pad2(down[l], hp, LANES).astype(BF)
        for tap in range(9):
            a, b = divmod(tap, 3)
            o_conv[l, a, b * LANES : (b + 1) * LANES, :] = pad2(conv[l, tap], LANES, LANES).astype(BF)


def own_body(channels, x_ref, gain, qk, o_x, o_xn, o_q, o_k):
    x = to_positions(x_ref)
    own_tail(channels, windows(x), gain, qk, o_x, o_xn, o_q, o_k)


def own_tail(channels, x, gain, qk, o_x, o_xn, o_q, o_k):
    o_x[...] = x
    xn = norm(x, gain[0:1], channels).astype(BF)
    o_xn[...] = xn
    count, size, _ = xn.shape
    both = dot(xn.reshape(count * size, LANES), qk[...]).astype(BF)
    o_q[...] = both[:, :LANES].reshape(count, size, LANES)
    o_k[...] = both[:, LANES:].reshape(count, size, LANES)


def mutual(channels, far, x_ref, xn_ref, q_ref, k_ref, gain, qk, vt, wo, wgu, wd, emit):
    fn = norm(far, gain[0:1], channels).astype(BF)
    count, size, _ = fn.shape
    hp = wd.shape[0]
    fk = dot(fn.reshape(count * size, LANES), qk[:, LANES:]).astype(BF).reshape(count, size, LANES)
    head_of = lax.broadcasted_iota(jnp.int32, (size, LANES), 1) // HD
    sub = lax.broadcasted_iota(jnp.int32, (LANES, LANES), 0) // HD
    half = lax.broadcasted_iota(jnp.int32, (LANES, LANES), 1) // size
    pick = [sub == 2 * j + half for j in range(HEADS // 2)]
    scale = HD ** (-0.5) * 1.4426950408889634
    group = 4
    for g in range(count // group):
        mixed = []
        for w in range(g * group, (g + 1) * group):
            keys = jnp.concatenate([k_ref[w], fk[w]], axis=0)
            xall = jnp.concatenate([xn_ref[w], fn[w]], axis=0)
            vals = dot_nt(vt[...], xall).astype(BF)
            q = q_ref[w]
            qm = jnp.concatenate([jnp.where(head_of == h, q, jnp.zeros_like(q)) for h in range(HEADS)], axis=0)
            s = dot_nt(keys, qm)
            top = jnp.max(s, axis=0, keepdims=True)
            p = jnp.exp2((s - top) * scale)
            p = (p * (1.0 / jnp.sum(p, axis=0, keepdims=True))).astype(BF)
            o = dot(vals, p)
            r = jnp.where(pick[0], o[:, :LANES], 0.0)
            for j in range(1, HEADS // 2):
                r = jnp.where(pick[j], o[:, j * LANES : (j + 1) * LANES], r)
            r = r.T
            mixed.append(r[:size] + r[size:])
        mixed = jnp.concatenate(mixed, axis=0).astype(BF)
        att = x_ref[g * group : (g + 1) * group].reshape(group * size, LANES) + dot(mixed, wo[...])
        nf = norm(att, gain[1:2], channels).astype(BF)
        gu = dot(nf, wgu[...])
        gate = gu[:, :hp]
        act = 0.5 * gate * (1.0 + lax.erf(gate * (0.5**0.5))) * gu[:, hp:]
        fed = att + dot(act.astype(BF), wd[...])
        emit(g * group, fed.reshape(group, size, LANES))


def conv_rows(x, shift, origin, drop, wc, bias):
    cols = x.shape[1]
    col = (lax.broadcasted_iota(jnp.int32, (cols, 1), 0) + origin) % cols
    rows = x.shape[0] - 2
    parts = []
    center = None
    for b in range(3):
        turn = (shift + 1 - b) % cols
        moved = pltpu.roll(x, turn, 1) if turn else x
        if b == 1:
            center = moved
        else:
            moved = jnp.where(col == (0 if b == 0 else cols - 1), 0.0, moved)
        parts.append(moved.astype(BF))
    cat = jnp.concatenate(parts, axis=2)
    total = center[1 : 1 + rows] + bias[...]
    total = total.reshape(rows * x.shape[1], LANES)
    for a in range(3):
        part = drop(a, cat[a : a + rows])
        total = total + dot(part.reshape(rows * x.shape[1], 3 * LANES), wc[a])
    return total.reshape(rows, x.shape[1], LANES)


def wrap_drop(last, edge):
    def drop(a, part):
        if a == 1:
            return part
        at = edge if a == 0 else edge - 1
        row = jnp.where(last, 0.0, part[at : at + 1].astype(F32)).astype(BF)
        return jnp.concatenate([part[:at], row, part[at + 1 :]], axis=0)

    return drop


def layer0_body(channels, far_ref, x_ref, xn_ref, q_ref, k_ref, gain, qk, vt, wo, wgu, wd, o_fed, o_low, o_high, buf):
    far = windows(to_positions(far_ref))
    rows = buf.shape[0]
    keep = o_low.shape[0]

    def emit(at, fed):
        buf[:, at * WIN : (at + fed.shape[0]) * WIN, :] = unwindows(fed, rows)

    mutual(channels, far, x_ref, xn_ref, q_ref, k_ref, gain, qk, vt, wo, wgu, wd, emit)
    o_fed[...] = buf[rows - keep :]
    o_low[...] = buf[:keep].astype(BF)
    o_high[...] = buf[rows - keep :].astype(BF)


def shifted_stream(last, high, low, wc, bias):
    x = jnp.concatenate([high, low], axis=0)
    x = conv_rows(x, -(WIN // 2), WIN // 2, wrap_drop(last, WIN // 2), wc, bias)
    return windows(x)


def own1_body(channels, last_ref, high, low, wc, bias, gain, qk, o_x, o_xn, o_q, o_k):
    x = shifted_stream(last_ref[0] == 1, high[...], low[...].astype(F32), wc, bias)
    own_tail(channels, x, gain, qk, o_x, o_xn, o_q, o_k)


def layer1_body(channels, last_ref, high, low, x_ref, xn_ref, q_ref, k_ref, wc, bias, gain, qk, vt, wo, wgu, wd, o_fed, o_send, buf):
    far = shifted_stream(last_ref[0] == 1, high[...].astype(F32), low[...].astype(F32), wc, bias)
    rows = buf.shape[0]
    keep = o_send.shape[0]

    def emit(at, fed):
        buf[:, at * WIN : (at + fed.shape[0]) * WIN, :] = unwindows(fed, rows)

    mutual(channels, far, x_ref, xn_ref, q_ref, k_ref, gain, qk, vt, wo, wgu, wd, emit)
    o_fed[...] = buf[:keep]
    o_send[...] = buf[rows - keep :].astype(BF)


def final_body(channels, last_ref, high, own, wc, bias, o_ref):
    first, last = last_ref[1] == 1, last_ref[0] == 1
    high = high[...].astype(F32)
    own = own[...]
    top = jnp.where(first, 0.0, high[:1])
    low = jnp.where(last, 0.0, own[-1:])
    x = jnp.concatenate([top, high[1:], own[:-1], low], axis=0)
    y = conv_rows(x, WIN // 2, 0, lambda a, part: part, wc, bias)
    y = jnp.stack([y[r].T for r in range(y.shape[0])], axis=0)
    y = jnp.swapaxes(y, 0, 1)[:channels]
    o_ref[0] = y.astype(BF)


def call(body, outs, *args, scratch=(), scalars=0):
    vm = pl.BlockSpec(memory_space=pltpu.VMEM)
    sm = pl.BlockSpec(memory_space=pltpu.SMEM)
    return pl.pallas_call(
        body,
        out_shape=[jax.ShapeDtypeStruct(s, d) for s, d in outs],
        in_specs=[sm] * scalars + [vm] * (len(args) - scalars),
        out_specs=[vm] * len(outs),
        scratch_shapes=list(scratch),
        compiler_params=pltpu.CompilerParams(vmem_limit_bytes=24 * 1024 * 1024),
    )(*args)


def on_device(frames, ln_gain, qkv_weight, out_weight, gate_weight, up_weight, down_weight, conv_weight, conv_bias):
    _, channels, rows, cols = frames.shape
    layers = ln_gain.shape[0]
    hp = up(gate_weight.shape[2])
    tiles, depth = lax.axis_size("tile"), lax.axis_size("tm")
    where = lax.axis_index("tile")
    ends = jnp.stack([where == tiles - 1, where == 0]).astype(jnp.int32)
    axes = ("tile", "tm")

    def odd(f):
        return (f + 1) % depth if f % 2 else (f - 1) % depth

    def send(x, target):
        pairs = []
        for t in range(tiles):
            for f in range(depth):
                to_t, to_f = target(t, f)
                pairs.append((t * depth + f, to_t * depth + to_f))
        return lax.ppermute(x, axes, pairs)

    far_frames = send(frames, lambda t, f: (t, f ^ 1))
    gain, qk, vt, wo, wgu, wd, wc, bias = call(
        weights_body,
        [
            ((layers, 2, LANES), F32),
            ((layers, LANES, 2 * LANES), BF),
            ((layers, LANES, LANES), BF),
            ((layers, LANES, LANES), BF),
            ((layers, LANES, 2 * hp), BF),
            ((layers, hp, LANES), BF),
            ((layers, 3, 3 * LANES, LANES), BF),
            ((layers, 1, LANES), F32),
        ],
        ln_gain, qkv_weight, out_weight, gate_weight, up_weight, down_weight, conv_weight, conv_bias,
    )
    count = cols // WIN
    own_outs = [
        ((count, rows * WIN, LANES), F32),
        ((count, rows * WIN, LANES), BF),
        ((count, rows * WIN, LANES), BF),
        ((count, rows * WIN, LANES), BF),
    ]
    half = (rows // 2 + 1, cols, LANES)
    buf = pltpu.VMEM((rows, cols, LANES), F32)

    def bind(body):
        def wrapped(*refs):
            return body(channels, *refs)
        wrapped.__name__ = body.__name__
        return wrapped

    x, xn, q, k = call(bind(own_body), own_outs, frames, gain[0], qk[0])
    fed, low, high = call(
        bind(layer0_body),
        [(half, F32), (half, BF), (half, BF)],
        far_frames, x, xn, q, k, gain[0], qk[0], vt[0], wo[0], wgu[0], wd[0],
        scratch=[buf],
    )
    below = send(low, lambda t, f: ((t - 1) % tiles, f))
    far_high = send(high, lambda t, f: (t, odd(f)))
    far_low = send(low, lambda t, f: ((t - 1) % tiles, odd(f)))
    x, xn, q, k = call(bind(own1_body), own_outs, ends, fed, below, wc[0], bias[0], gain[1], qk[1], scalars=1)
    fed, down = call(
        bind(layer1_body),
        [(half, F32), (half, BF)],
        ends, far_high, far_low, x, xn, q, k, wc[0], bias[0], gain[1], qk[1], vt[1], wo[1], wgu[1], wd[1],
        scratch=[buf], scalars=1,
    )
    above = send(down, lambda t, f: ((t + 1) % tiles, f))
    (out,) = call(bind(final_body), [((1, channels, rows, cols), BF)], ends, above, fed, wc[1], bias[1], scalars=1)
    return out


def solution(mesh):
    in_specs = (P(("clips", "tm"), None, "tile", None), P(), P(), P(), P(), P(), P(), P(), P())
    out_specs = P(("clips", "tm"), None, "tile", None)
    return jax.shard_map(
        on_device, mesh=mesh, in_specs=in_specs, out_specs=out_specs, check_vma=False
    )
```

profile of v0, /device:TPU:16, one launch (start us, length us, event | category | flops | bytes accessed | tf_op | source)
XLA Modules:
  0.0 51.2 jit_solution(14477237643905284891)
XLA Ops:
  0.0 1.6 %collective-permute-start = (bf16[1,120,8,128]{3,2,1,0:T(8,128)(2,1)}, bf16[1,120,8,128]{3,2,1,0:T(8,128)(2,1)S(1)}, u32[]{:S(2)}, u32[]{:S(2)}) collective-permute-start(bf16[1,120,8,128]{3,2,1,0:T(8,128)(2,1)} %refs_0_.1), channel_id=1, source_target_pairs={{0,1},{1,0},{2,3},{3,2},{4,5},{5,4},{6,7},{7,6},{8,9},{9,8},{10,11... | collective-permute-start | bytes 737288 | tf_op jit(solution)/shard_map/ppermute | solution.py:257
  1.6 0.0 copy-start
  1.6 1.0 %copy-done = bf16[2,9,120,120]{3,2,1,0:T(8,128)(2,1)S(1)} copy-done((bf16[2,9,120,120]{3,2,1,0:T(8,128)(2,1)S(1)}, bf16[2,9,120,120]{3,2,1,0:T(8,128)(2,1)}, u32[]{:S(2)}) %copy-start) | copy-done | bytes 518424
  2.6 0.0 copy-start.2
  2.6 0.9 %copy-done.2 = bf16[2,120,360]{2,1,0:T(8,128)(2,1)S(1)} copy-done((bf16[2,120,360]{2,1,0:T(8,128)(2,1)S(1)}, bf16[2,120,360]{2,1,0:T(8,128)(2,1)}, u32[]{:S(2)}) %copy-start.2) | copy-done | bytes 172824
  3.6 0.0 copy-start.3
  3.6 0.9 %copy-done.3 = bf16[2,120,240]{2,1,0:T(8,128)(2,1)S(1)} copy-done((bf16[2,120,240]{2,1,0:T(8,128)(2,1)S(1)}, bf16[2,120,240]{2,1,0:T(8,128)(2,1)}, u32[]{:S(2)}) %copy-start.3) | copy-done | bytes 115224
  4.5 0.0 copy-start.4
  4.5 0.9 %copy-done.4 = bf16[2,120,240]{2,1,0:T(8,128)(2,1)S(1)} copy-done((bf16[2,120,240]{2,1,0:T(8,128)(2,1)S(1)}, bf16[2,120,240]{2,1,0:T(8,128)(2,1)}, u32[]{:S(2)}) %copy-start.4) | copy-done | bytes 115224
  5.4 0.0 copy-start.5
  5.4 0.9 %copy-done.5 = bf16[2,240,120]{2,1,0:T(8,128)(2,1)S(1)} copy-done((bf16[2,240,120]{2,1,0:T(8,128)(2,1)S(1)}, bf16[2,240,120]{2,1,0:T(8,128)(2,1)}, u32[]{:S(2)}) %copy-start.5) | copy-done | bytes 115224
  6.3 0.0 copy-start.6
  6.3 0.8 %copy-done.6 = bf16[2,120,120]{2,1,0:T(8,128)(2,1)S(1)} copy-done((bf16[2,120,120]{2,1,0:T(8,128)(2,1)S(1)}, bf16[2,120,120]{2,1,0:T(8,128)(2,1)}, u32[]{:S(2)}) %copy-start.6) | copy-done | bytes 57624
  7.1 0.0 copy-start.7
  7.1 0.7 %copy-done.7 = f32[2,2,120]{2,1,0:T(2,128)S(1)} copy-done((f32[2,2,120]{2,1,0:T(2,128)S(1)}, f32[2,2,120]{2,1,0:T(2,128)}, u32[]{:S(2)}) %copy-start.7) | copy-done | bytes 1944
  7.8 0.0 copy-start.8
  7.8 0.7 %copy-done.8 = f32[2,120]{1,0:T(2,128)S(1)} copy-done((f32[2,120]{1,0:T(2,128)S(1)}, f32[2,120]{1,0:T(2,128)}, u32[]{:S(2)}) %copy-start.8) | copy-done | bytes 984
  8.4 0.3 shard_map.91
  8.8 0.0 copy-start.1
  8.8 0.9 %copy-done.1 = bf16[1,120,8,128]{3,2,1,0:T(8,128)(2,1)S(1)} copy-done((bf16[1,120,8,128]{3,2,1,0:T(8,128)(2,1)S(1)}, bf16[1,120,8,128]{3,2,1,0:T(8,128)(2,1)}, u32[]{:S(2)}) %copy-start.1) | copy-done | bytes 245784
  9.8 0.7 %shard_map.92 = (f32[16,64,128]{2,1,0:T(8,128)S(1)}, bf16[16,64,128]{2,1,0:T(8,128)(2,1)S(1)}, bf16[16,64,128]{2,1,0:T(8,128)(2,1)S(1)}, bf16[16,64,128]{2,1,0:T(8,128)(2,1)S(1)}) custom-call(bf16[1,120,8,128]{3,2,1,0:T(8,128)(2,1)S(1)} %copy-done.1, f32[2,128]{1,0:T(2,128)S(1)} %get-tuple-element.60.refs_1_.refs_5_, ...), custom_call_target="tpu_custom_call" | custom-call | tf_op jit(solution)/shard_map/pallas_call | solution.py:229
  10.6 0.0 collective-permute-done.refs_0_
  10.6 7.4 %shard_map.93 = (f32[5,128,128]{2,1,0:T(8,128)S(1)}, bf16[5,128,128]{2,1,0:T(8,128)(2,1)S(1)}, bf16[5,128,128]{2,1,0:T(8,128)(2,1)S(1)}) custom-call(bf16[1,120,8,128]{3,2,1,0:T(8,128)(2,1)S(1)} %collective-permute-done.refs_0_, f32[16,64,128]{2,1,0:T(8,128)S(1)} %get-tuple-element.28.refs_1_, bf16[16,64,128]{2,1,0:T(8,128)(2,1)S(1)} %get-tuple-element.29.refs_2_, ...), custom_call_target="tpu_custom_call" | custom-call | tf_op jit(solution)/shard_map/pallas_call | solution.py:229
  18.0 0.7 %collective-permute-start.3 = (bf16[5,128,128]{2,1,0:T(8,128)(2,1)S(1)}, bf16[5,128,128]{2,1,0:T(8,128)(2,1)S(1)}, u32[]{:S(2)}, u32[]{:S(2)}) collective-permute-start(bf16[5,128,128]{2,1,0:T(8,128)(2,1)S(1)} %get-tuple-element.37), channel_id=1, source_target_pairs={{0,12},{1,13},{2,14},{3,15},{4,0},{5,1},{6,2},{7,3},{8,4},{9,5},{1... | collective-permute-start | bytes 491528 | tf_op jit(solution)/shard_map/ppermute | solution.py:257
  18.7 0.0 collective-permute-start.2
  18.7 2.4 %collective-permute-start.1 = (bf16[5,128,128]{2,1,0:T(8,128)(2,1)S(1)}, bf16[5,128,128]{2,1,0:T(8,128)(2,1)S(1)}, u32[]{:S(2)}, u32[]{:S(2)}) collective-permute-start(bf16[5,128,128]{2,1,0:T(8,128)(2,1)S(1)} %get-tuple-element.36), channel_id=1, source_target_pairs={{0,3},{1,2},{2,1},{3,0},{4,7},{5,6},{6,5},{7,4},{8,11},{9,10},{10,... | collective-permute-start | bytes 491528 | tf_op jit(solution)/shard_map/ppermute | solution.py:257
  21.1 0.1 add_convert_fusion.refs_0_
  21.2 0.3 collective-permute-done.3.refs_2_
  21.6 2.2 %shard_map.94 = (f32[16,64,128]{2,1,0:T(8,128)S(1)}, bf16[16,64,128]{2,1,0:T(8,128)(2,1)S(1)}, bf16[16,64,128]{2,1,0:T(8,128)(2,1)S(1)}, bf16[16,64,128]{2,1,0:T(8,128)(2,1)S(1)}) custom-call(s32[2]{0:T(128)S(1)} %add_convert_fusion.refs_0_, f32[5,128,128]{2,1,0:T(8,128)S(1)} %get-tuple-element.38.refs_1_, ...), custom_call_target="tpu_custom_call" | custom-call | tf_op jit(solution)/shard_map/pallas_call | solution.py:229
  23.7 12.0 %collective-permute-done.1.refs_1_ = bf16[5,128,128]{2,1,0:T(8,128)(2,1)S(1)} collective-permute-done((bf16[5,128,128]{2,1,0:T(8,128)(2,1)S(1)}, bf16[5,128,128]{2,1,0:T(8,128)(2,1)S(1)}, u32[]{:S(2)}, u32[]{:S(2)}) %collective-permute-start.1) | collective-permute-done | bytes 163872 | tf_op jit(solution)/shard_map/ppermute | solution.py:257
  35.7 0.0 collective-permute-done.2.refs_2_
  35.8 8.5 %shard_map.95 = (f32[5,128,128]{2,1,0:T(8,128)S(1)}, bf16[5,128,128]{2,1,0:T(8,128)(2,1)S(1)}) custom-call(s32[2]{0:T(128)S(1)} %add_convert_fusion.refs_0_, bf16[5,128,128]{2,1,0:T(8,128)(2,1)S(1)} %collective-permute-done.1.refs_1_, bf16[5,128,128]{2,1,0:T(8,128)(2,1)S(1)} %collective-permute-done.2.refs_2_, f32[16,64,128]{2,1,0:T(8,128)S(1)} %get-tuple-element.41.refs_3_, ...), custom_call_target="tpu_custom_call" | custom-call | tf_op jit(solution)/shard_map/pallas_call | solution.py:229
  44.2 0.1 collective-permute-start.4
  44.3 4.7 %collective-permute-done.4.refs_1_ = bf16[5,128,128]{2,1,0:T(8,128)(2,1)S(1)} collective-permute-done((bf16[5,128,128]{2,1,0:T(8,128)(2,1)S(1)}, bf16[5,128,128]{2,1,0:T(8,128)(2,1)S(1)}, u32[]{:S(2)}, u32[]{:S(2)}) %collective-permute-start.4) | collective-permute-done | bytes 163872 | tf_op jit(solution)/shard_map/ppermute | solution.py:257
  49.0 2.1 %shard_map.96 = bf16[1,120,8,128]{3,2,1,0:T(8,128)(2,1)} custom-call(s32[2]{0:T(128)S(1)} %add_convert_fusion.refs_0_, bf16[5,128,128]{2,1,0:T(8,128)(2,1)S(1)} %collective-permute-done.4.refs_1_, f32[5,128,128]{2,1,0:T(8,128)S(1)} %get-tuple-element.46.refs_2_, bf16[3,384,128]{2,1,0:T(8,128)(2,1)S(1)} %get-tuple-element.47.refs_3_, ...), custom_call_target="tpu_custom_call" | custom-call | tf_op jit(solution)/shard_map/pallas_call | solution.py:229
  (7 shorter events, 0.1 us)
Async XLA Ops:
  0.0 10.6 %collective-permute-start = (bf16[1,120,8,128]{3,2,1,0:T(8,128)(2,1)}, bf16[1,120,8,128]{3,2,1,0:T(8,128)(2,1)S(1)}, u32[]{:S(2)}, u32[]{:S(2)}) collective-permute-start(bf16[1,120,8,128]{3,2,1,0:T(8,128)(2,1)} %refs_0_.1), channel_id=1, source_target_pairs={{0,1},{1,0},{2,3},{3,2},{4,5},{5,4},{6,7},{7,6},{8,9},{9,8},{10,11... | collective-permute-start | bytes 737288 | tf_op jit(solution)/shard_map/ppermute | solution.py:257
  1.6 1.1 %copy-start = (bf16[2,9,120,120]{3,2,1,0:T(8,128)(2,1)S(1)}, bf16[2,9,120,120]{3,2,1,0:T(8,128)(2,1)}, u32[]{:S(2)}) copy-start(bf16[2,9,120,120]{3,2,1,0:T(8,128)(2,1)} %conv.1) | copy-start | bytes 1555204
  2.6 0.9 %copy-start.2 = (bf16[2,120,360]{2,1,0:T(8,128)(2,1)S(1)}, bf16[2,120,360]{2,1,0:T(8,128)(2,1)}, u32[]{:S(2)}) copy-start(bf16[2,120,360]{2,1,0:T(8,128)(2,1)} %qkv.1) | copy-start | bytes 518404
  3.6 0.9 %copy-start.3 = (bf16[2,120,240]{2,1,0:T(8,128)(2,1)S(1)}, bf16[2,120,240]{2,1,0:T(8,128)(2,1)}, u32[]{:S(2)}) copy-start(bf16[2,120,240]{2,1,0:T(8,128)(2,1)} %gate.1) | copy-start | bytes 345604
  4.5 0.9 %copy-start.4 = (bf16[2,120,240]{2,1,0:T(8,128)(2,1)S(1)}, bf16[2,120,240]{2,1,0:T(8,128)(2,1)}, u32[]{:S(2)}) copy-start(bf16[2,120,240]{2,1,0:T(8,128)(2,1)} %upw.1) | copy-start | bytes 345604
  5.4 0.9 %copy-start.5 = (bf16[2,240,120]{2,1,0:T(8,128)(2,1)S(1)}, bf16[2,240,120]{2,1,0:T(8,128)(2,1)}, u32[]{:S(2)}) copy-start(bf16[2,240,120]{2,1,0:T(8,128)(2,1)} %down.1) | copy-start | bytes 345604
  6.3 0.8 %copy-start.6 = (bf16[2,120,120]{2,1,0:T(8,128)(2,1)S(1)}, bf16[2,120,120]{2,1,0:T(8,128)(2,1)}, u32[]{:S(2)}) copy-start(bf16[2,120,120]{2,1,0:T(8,128)(2,1)} %out.1) | copy-start | bytes 172804
  7.1 0.7 %copy-start.7 = (f32[2,2,120]{2,1,0:T(2,128)S(1)}, f32[2,2,120]{2,1,0:T(2,128)}, u32[]{:S(2)}) copy-start(f32[2,2,120]{2,1,0:T(2,128)} %gain.1) | copy-start | bytes 5764
  7.8 0.7 %copy-start.8 = (f32[2,120]{1,0:T(2,128)S(1)}, f32[2,120]{1,0:T(2,128)}, u32[]{:S(2)}) copy-start(f32[2,120]{1,0:T(2,128)} %bias.1) | copy-start | bytes 2884
  8.8 0.9 %copy-start.1 = (bf16[1,120,8,128]{3,2,1,0:T(8,128)(2,1)S(1)}, bf16[1,120,8,128]{3,2,1,0:T(8,128)(2,1)}, u32[]{:S(2)}) copy-start(bf16[1,120,8,128]{3,2,1,0:T(8,128)(2,1)} %refs_0_.1) | copy-start | bytes 737284
  18.0 3.5 %collective-permute-start.3 = (bf16[5,128,128]{2,1,0:T(8,128)(2,1)S(1)}, bf16[5,128,128]{2,1,0:T(8,128)(2,1)S(1)}, u32[]{:S(2)}, u32[]{:S(2)}) collective-permute-start(bf16[5,128,128]{2,1,0:T(8,128)(2,1)S(1)} %get-tuple-element.37), channel_id=1, source_target_pairs={{0,12},{1,13},{2,14},{3,15},{4,0},{5,1},{6,2},{7,3},{8,4},{9,5},{1... | collective-permute-start | bytes 491528 | tf_op jit(solution)/shard_map/ppermute | solution.py:257
  18.7 17.0 %collective-permute-start.2 = (bf16[5,128,128]{2,1,0:T(8,128)(2,1)S(1)}, bf16[5,128,128]{2,1,0:T(8,128)(2,1)S(1)}, u32[]{:S(2)}, u32[]{:S(2)}) collective-permute-start(bf16[5,128,128]{2,1,0:T(8,128)(2,1)S(1)} %get-tuple-element.37), channel_id=1, source_target_pairs={{0,15},{1,14},{2,13},{3,12},{4,3},{5,2},{6,1},{7,0},{8,7},{9,6},{1... | collective-permute-start | bytes 491528 | tf_op jit(solution)/shard_map/ppermute | solution.py:257
  18.7 17.0 %collective-permute-start.1 = (bf16[5,128,128]{2,1,0:T(8,128)(2,1)S(1)}, bf16[5,128,128]{2,1,0:T(8,128)(2,1)S(1)}, u32[]{:S(2)}, u32[]{:S(2)}) collective-permute-start(bf16[5,128,128]{2,1,0:T(8,128)(2,1)S(1)} %get-tuple-element.36), channel_id=1, source_target_pairs={{0,3},{1,2},{2,1},{3,0},{4,7},{5,6},{6,5},{7,4},{8,11},{9,10},{10,... | collective-permute-start | bytes 491528 | tf_op jit(solution)/shard_map/ppermute | solution.py:257
  44.2 4.8 %collective-permute-start.4 = (bf16[5,128,128]{2,1,0:T(8,128)(2,1)S(1)}, bf16[5,128,128]{2,1,0:T(8,128)(2,1)S(1)}, u32[]{:S(2)}, u32[]{:S(2)}) collective-permute-start(bf16[5,128,128]{2,1,0:T(8,128)(2,1)S(1)} %get-tuple-element.45), channel_id=1, source_target_pairs={{0,4},{1,5},{2,6},{3,7},{4,8},{5,9},{6,10},{7,11},{8,12},{9,13},{1... | collective-permute-start | bytes 491528 | tf_op jit(solution)/shard_map/ppermute | solution.py:257
where the time goes:
time: 51.5 us; the launch traced here: 51.2 us
  Pallas kernels  21.3 us (41%)
  waiting for transfers between devices  17.1 us (33%)
  local copies, waits for them, and re-layouts  7.88 us (15%)
  starting transfers between devices  4.75 us (9%)
    pallas_call x6, Pallas kernels, call(): pl.pallas_call(body, out_shape=[jax.ShapeDtypeStruct(s, d) for s, d in ou...  21.3 us
    ppermute x5, waiting for transfers between devices, send(): return lax.ppermute(x, axes, pairs)  17.1 us
    unnamed x18, local copies, waits for them, and re-layouts  7.78 us
    ppermute x5, starting transfers between devices, send(): return lax.ppermute(x, axes, pairs)  4.75 us
  transfers between devices with their start and end apart: 5, of which 3 were waited for; matrix products, arithmetic and copies ran while one was open for 0% of the time, Pallas kernels for 6%

commit v1 on v0

v1 whole, which is shorter than its diff:
```python
import jax
import jax.numpy as jnp
from jax import lax
from jax.experimental import pallas as pl
from jax.experimental.pallas import tpu as pltpu
from jax.sharding import PartitionSpec as P


HEADS = 6
HD = 20
WIN = 8
LANES = 128
GROUP = 4
BF = jnp.bfloat16
F32 = jnp.float32
NT = (((1,), (1,)), ((), ()))


def up(n):
    return -(-n // LANES) * LANES


def dot(a, b):
    return jnp.dot(a, b, preferred_element_type=F32)


def dot_nt(a, b):
    return lax.dot_general(a, b, NT, preferred_element_type=F32)


def norm(x, gain, channels):
    lane = lax.broadcasted_iota(jnp.int32, x.shape, x.ndim - 1)
    mean = jnp.sum(x, axis=-1, keepdims=True) * (1.0 / channels)
    center = jnp.where(lane < channels, x - mean, 0.0)
    spread = jnp.sum(center * center, axis=-1, keepdims=True) * (1.0 / channels)
    return center * lax.rsqrt(spread + 1e-05) * gain


def to_positions(ref):
    x = ref[0].astype(F32)
    channels, rows, cols = x.shape
    x = jnp.concatenate([x, jnp.zeros((LANES - channels, rows, cols), F32)], axis=0)
    x = jnp.swapaxes(x, 0, 1)
    return jnp.stack([x[r].T for r in range(rows)], axis=0)


def windows(x):
    rows, cols, lanes = x.shape
    x = x.reshape(rows, cols // WIN, WIN, lanes)
    return jnp.swapaxes(x, 0, 1).reshape(cols // WIN, rows * WIN, lanes)


def unwindows(x, rows):
    count, _, lanes = x.shape
    x = jnp.swapaxes(x.reshape(count, rows, WIN, lanes), 0, 1)
    return x.reshape(rows, count * WIN, lanes)


def pad2(x, rows, cols):
    x = x.astype(F32)
    if x.shape[1] < cols:
        x = jnp.concatenate([x, jnp.zeros((x.shape[0], cols - x.shape[1]), F32)], axis=1)
    if x.shape[0] < rows:
        x = jnp.concatenate([x, jnp.zeros((rows - x.shape[0], cols), F32)], axis=0)
    return x


def norm_body(channels, gain_hbm, x_hbm, o_x, o_a, o_b, gain, x_ref, sems):
    copies = [pltpu.make_async_copy(x_hbm, x_ref, sems.at[0]), pltpu.make_async_copy(gain_hbm, gain, sems.at[1])]
    for copy in copies:
        copy.start()
    for copy in copies:
        copy.wait()
    x = windows(to_positions(x_ref))
    o_x[...] = x
    xn = norm(x, pad2(gain[0], 2, LANES)[:1], channels).astype(BF)
    first = o_a.shape[0]
    o_a[...] = xn[:first]
    o_b[...] = xn[first:]


def weights_body(channels, *refs):
    hbm, (xa, xb) = refs[:8], refs[8:10]
    o_q, o_k = refs[10:12]
    layers = hbm[2].shape[0]
    outs = refs[12 : 12 + 8 * layers]
    local, sems = refs[12 + 8 * layers : -1], refs[-1]
    copies = [pltpu.make_async_copy(a, b, sems.at[i]) for i, (a, b) in enumerate(zip(hbm, local))]
    for copy in copies:
        copy.start()
    for copy in copies:
        copy.wait()
    gain, qkv, out, gate, upw, down, conv, bias = local
    hp = up(gate.shape[2])
    for l in range(layers):
        o_gain, o_qk, o_vt, o_out, o_gu, o_down, o_conv, o_bias = outs[8 * l : 8 * l + 8]
        o_gain[...] = pad2(gain[l], 2, LANES)
        o_bias[...] = pad2(bias[l : l + 1], 1, LANES)
        w = qkv[l].astype(F32)
        wq = pad2(w[:, :channels], LANES, LANES).astype(BF)
        wk = pad2(w[:, channels : 2 * channels], LANES, LANES).astype(BF)
        o_qk[:, :LANES] = wq
        o_qk[:, LANES:] = wk
        o_vt[...] = pad2(w[:, 2 * channels :], LANES, LANES).T.astype(BF)
        o_out[...] = pad2(out[l], LANES, LANES).astype(BF)
        o_gu[:, :hp] = pad2(gate[l], LANES, hp).astype(BF)
        o_gu[:, hp:] = pad2(upw[l], LANES, hp).astype(BF)
        o_down[...] = pad2(down[l], hp, LANES).astype(BF)
        for tap in range(9):
            a, b = divmod(tap, 3)
            o_conv[a, b * LANES : (b + 1) * LANES, :] = pad2(conv[l, tap], LANES, LANES).astype(BF)
        if l == 0:
            project(jnp.concatenate([xa[...], xb[...]], axis=0), jnp.concatenate([wq, wk], axis=1), o_q, o_k)


def project(xn, qk, o_q, o_k):
    count, size, _ = xn.shape
    both = dot(xn.reshape(count * size, LANES), qk).astype(BF)
    o_q[...] = both[:, :LANES].reshape(count, size, LANES)
    o_k[...] = both[:, LANES:].reshape(count, size, LANES)


def mutual(channels, base, fn, own, x_ref, q_ref, k_ref, gain, qk, vt, wo, wgu, wd, emit):
    count, size, _ = fn.shape
    hp = wd.shape[0]
    fk = dot(fn.reshape(count * size, LANES), qk[:, LANES:]).astype(BF).reshape(count, size, LANES)
    head_of = lax.broadcasted_iota(jnp.int32, (size, LANES), 1) // HD
    sub = lax.broadcasted_iota(jnp.int32, (LANES, LANES), 0) // HD
    half = lax.broadcasted_iota(jnp.int32, (LANES, LANES), 1) // size
    pick = [sub == 2 * j + half for j in range(HEADS // 2)]
    scale = HD ** (-0.5) * 1.4426950408889634
    group = next(g for g in range(min(GROUP, count), 0, -1) if count % g == 0)
    if group < 3:
        group = count

    def scores(g, _):
        out = []
        for w in range(g * group, (g + 1) * group):
            keys = jnp.concatenate([k_ref[base + w], fk[w]], axis=0)
            xall = jnp.concatenate([own[w], fn[w]], axis=0)
            vals = dot_nt(vt[...], xall).astype(BF)
            q = q_ref[base + w]
            qm = jnp.concatenate([jnp.where(head_of == h, q, jnp.zeros_like(q)) for h in range(HEADS)], axis=0)
            out.append((vals, dot_nt(keys, qm)))
        return out

    def attend(g, state):
        out = []
        for vals, s in state:
            top = jnp.max(s, axis=0, keepdims=True)
            p = jnp.exp2((s - top) * scale)
            p = (p * (1.0 / jnp.sum(p, axis=0, keepdims=True))).astype(BF)
            out.append(dot(vals, p))
        return out

    def merge(g, state):
        mixed = []
        for o in state:
            r = jnp.where(pick[0], o[:, :LANES], 0.0)
            for j in range(1, HEADS // 2):
                r = jnp.where(pick[j], o[:, j * LANES : (j + 1) * LANES], r)
            r = r.T
            mixed.append(r[:size] + r[size:])
        mixed = jnp.concatenate(mixed, axis=0).astype(BF)
        return x_ref[base + g * group : base + (g + 1) * group].reshape(group * size, LANES) + dot(mixed, wo[...])

    def widen(g, att):
        nf = norm(att, gain[1:2], channels).astype(BF)
        return att, dot(nf, wgu[...])

    def narrow(g, state):
        att, gu = state
        gate = gu[:, :hp]
        act = 0.5 * gate * (1.0 + lax.erf(gate * (0.5**0.5))) * gu[:, hp:]
        fed = att + dot(act.astype(BF), wd[...])
        emit(g * group, fed.reshape(group, size, LANES))

    stages = [scores, attend, merge, widen, narrow]
    total = count // group
    held = [None] * (len(stages) + 1)
    for step in range(total + len(stages) - 1):
        for i in reversed(range(len(stages))):
            if 0 <= step - i < total:
                held[i + 1] = stages[i](step - i, held[i])


def conv_rows(x, shift, origin, drop, wc, bias):
    cols = x.shape[1]
    taps = [pltpu.roll(x, (shift + 1 - b) % cols, 1) if (shift + 1 - b) % cols else x for b in range(3)]
    return conv_taps(taps, origin, cols, drop, wc, bias)


def conv_cols(x, skip, origin, cols, drop, wc, bias):
    n = x.shape[1] - 2 * skip
    taps = [x[:, skip - 1 + b : skip - 1 + b + n] for b in range(3)]
    return conv_taps(taps, origin, cols, drop, wc, bias)


def conv_taps(taps, origin, cols, drop, wc, bias):
    center = taps[1]
    rows, width = center.shape[0] - 2, center.shape[1]
    col = (lax.broadcasted_iota(jnp.int32, (width, 1), 0) + origin) % cols
    parts = []
    for b, moved in enumerate(taps):
        if b != 1:
            moved = jnp.where(col == (0 if b == 0 else cols - 1), 0.0, moved)
        parts.append(moved.astype(BF))
    cat = jnp.concatenate(parts, axis=2)
    total = (center[1 : 1 + rows] + bias[...]).reshape(rows * width, LANES)
    for a in range(3):
        part = drop(a, cat[a : a + rows])
        total = total + dot(part.reshape(rows * width, 3 * LANES), wc[a])
    return total.reshape(rows, width, LANES)


def wrap_drop(last, edge):
    def drop(a, part):
        if a == 1:
            return part
        at = edge if a == 0 else edge - 1
        row = jnp.where(last, 0.0, part[at : at + 1].astype(F32)).astype(BF)
        return jnp.concatenate([part[:at], row, part[at + 1 :]], axis=0)

    return drop


def collect(buf):
    def emit(at, fed):
        buf[:, at * WIN : (at + fed.shape[0]) * WIN, :] = unwindows(fed, buf.shape[0])

    return emit


def layer0_first(channels, far, own, x_ref, q_ref, k_ref, gain, qk, vt, wo, wgu, wd, o_fed, o_low, o_high, buf):
    rows, keep = buf.shape[0], o_low.shape[0]
    mutual(channels, 0, far[...], own[...], x_ref, q_ref, k_ref, gain, qk, vt, wo, wgu, wd, collect(buf))
    o_fed[...] = buf[rows - keep :]
    o_low[...] = buf[:keep].astype(BF)
    o_high[...] = buf[rows - keep :].astype(BF)


def layer0_second(channels, far, own, x_ref, q_ref, k_ref, gain, qk, vt, wo, wgu, wd, low_a, o_fed, o_low, o_high, o_whole, buf):
    rows, keep = buf.shape[0], o_low.shape[0]
    base = x_ref.shape[0] - far.shape[0]
    mutual(channels, base, far[...], own[...], x_ref, q_ref, k_ref, gain, qk, vt, wo, wgu, wd, collect(buf))
    o_fed[...] = buf[rows - keep :]
    low = buf[:keep].astype(BF)
    o_low[...] = low
    o_high[...] = buf[rows - keep :].astype(BF)
    first = base * WIN
    o_whole[:, :first, :] = low_a[...]
    o_whole[:, first:, :] = low


def own1_body(channels, ends, fed_a, fed_b, low, wc, bias, gain, qk, o_x, o_xn, o_q, o_k):
    high = jnp.concatenate([fed_a[...], fed_b[...]], axis=1)
    x = jnp.concatenate([high, low[...].astype(F32)], axis=0)
    x = windows(conv_rows(x, -(WIN // 2), WIN // 2, wrap_drop(ends[0] == 1, WIN // 2), wc, bias))
    o_x[...] = x
    xn = norm(x, gain[0:1], channels).astype(BF)
    o_xn[...] = xn
    project(xn, qk[...], o_q, o_k)


def far_normed(channels, ends, x, base, cols, wc, bias, gain):
    x = conv_cols(x, WIN // 2, base + WIN // 2, cols, wrap_drop(ends[0] == 1, WIN // 2), wc, bias)
    return norm(windows(x), gain[0:1], channels).astype(BF)


def layer1_first(channels, ends, high, low, xn_ref, x_ref, q_ref, k_ref, wc, bias, gain0, gain, qk, vt, wo, wgu, wd, o_own, o_send, buf):
    x = jnp.concatenate([high[...], low[...]], axis=0).astype(F32)
    rows, keep = buf.shape[0], o_own.shape[0]
    count = buf.shape[1] // WIN
    fn = far_normed(channels, ends, x, 0, 2 * buf.shape[1], wc, bias, gain)
    mutual(channels, 0, fn, xn_ref[:count], x_ref, q_ref, k_ref, gain, qk, vt, wo, wgu, wd, collect(buf))
    o_own[...] = buf[:keep]
    o_send[...] = buf[rows - keep :].astype(BF)


def layer1_second(channels, ends, high_a, low_a, high_b, low_b, xn_ref, x_ref, q_ref, k_ref, wc, bias, gain0, gain, qk, vt, wo, wgu, wd, send_a, o_own, o_send, buf):
    xa = jnp.concatenate([high_a[...], low_a[...]], axis=0).astype(F32)
    xb = jnp.concatenate([high_b[...], low_b[...]], axis=0).astype(F32)
    half = buf.shape[1]
    x = jnp.concatenate([xa[:, half:], xb, xa[:, :WIN]], axis=1)
    rows, keep = buf.shape[0], o_own.shape[0]
    count = half // WIN
    fn = far_normed(channels, ends, x, half, 2 * half, wc, bias, gain)
    mutual(channels, count, fn, xn_ref[count:], x_ref, q_ref, k_ref, gain, qk, vt, wo, wgu, wd, collect(buf))
    o_own[...] = buf[:keep]
    o_send[:, :half, :] = send_a[...]
    o_send[:, half:, :] = buf[rows - keep :].astype(BF)


def final_body(channels, ends, high, own_a, own_b, wc, bias, o_ref):
    first, last = ends[1] == 1, ends[0] == 1
    high = high[...].astype(F32)
    own = jnp.concatenate([own_a[...], own_b[...]], axis=1)
    top = jnp.where(first, 0.0, high[:1])
    low = jnp.where(last, 0.0, own[-1:])
    x = jnp.concatenate([top, high[1:], own[:-1], low], axis=0)
    y = conv_rows(x, WIN // 2, 0, lambda a, part: part, wc, bias)
    y = jnp.stack([y[r].T for r in range(y.shape[0])], axis=0)
    y = jnp.swapaxes(y, 0, 1)[:channels]
    o_ref[0] = y.astype(BF)


def call(body, outs, *args, scratch=(), scalars=0, remote=0, work=0):
    vm = pl.BlockSpec(memory_space=pltpu.VMEM)
    sm = pl.BlockSpec(memory_space=pltpu.SMEM)
    hbm = pl.BlockSpec(memory_space=pltpu.HBM)
    specs = [sm] * scalars + [hbm] * remote
    cost = pl.CostEstimate(flops=work, bytes_accessed=1024, transcendentals=0) if work else None
    run = pl.pallas_call(
        body,
        out_shape=[jax.ShapeDtypeStruct(s, d) for s, d in outs],
        in_specs=specs + [vm] * (len(args) - len(specs)),
        out_specs=[vm] * len(outs),
        scratch_shapes=list(scratch),
        cost_estimate=cost,
        compiler_params=pltpu.CompilerParams(vmem_limit_bytes=24 * 1024 * 1024),
    )
    args = [pltpu.with_memory_space_constraint(a, pltpu.HBM) if i < scalars + remote and i >= scalars else a for i, a in enumerate(args)]
    return run(*args)


def section(frames, *params):
    ln_gain, gate_weight = params[0], params[3]
    _, channels, rows, cols = frames.shape
    layers = ln_gain.shape[0]
    hp = up(gate_weight.shape[2])
    tiles, depth = lax.axis_size("tile"), lax.axis_size("tm")
    where = lax.axis_index("tile")
    ends = jnp.stack([where == tiles - 1, where == 0]).astype(jnp.int32)
    axes = ("tile", "tm")

    def odd(f):
        return (f + 1) % depth if f % 2 else (f - 1) % depth

    def send(x, target):
        pairs = []
        for t in range(tiles):
            for f in range(depth):
                to_t, to_f = target(t, f)
                pairs.append((t * depth + f, to_t * depth + to_f))
        return lax.ppermute(x, axes, pairs)

    def bind(body):
        def wrapped(*refs):
            return body(channels, *refs)

        wrapped.__name__ = body.__name__
        return wrapped

    count = cols // WIN
    first = count // 2 + 1
    rest = count - first
    keep = rows // 2 + 1
    size = rows * WIN
    dma = pltpu.SemaphoreType.DMA
    x, xa, xb = call(bind(norm_body),
        [((count, size, LANES), F32), ((first, size, LANES), BF), ((rest, size, LANES), BF)],
        ln_gain, frames,
        scratch=[pltpu.VMEM(ln_gain.shape, F32), pltpu.VMEM(frames.shape, BF), dma((2,))],
        remote=2,
    )
    far_a = send(xa, lambda t, f: (t, f ^ 1))
    far_b = send(xb, lambda t, f: (t, f ^ 1))
    q, k, *sets = call(bind(weights_body),
        [((count, size, LANES), BF), ((count, size, LANES), BF)]
        + [
            ((2, LANES), F32),
            ((LANES, 2 * LANES), BF),
            ((LANES, LANES), BF),
            ((LANES, LANES), BF),
            ((LANES, 2 * hp), BF),
            ((hp, LANES), BF),
            ((3, 3 * LANES, LANES), BF),
            ((1, LANES), F32),
        ]
        * layers,
        *params, xa, xb,
        scratch=[pltpu.VMEM(p.shape, p.dtype) for p in params] + [dma((len(params),))],
        remote=len(params),
    )

    gain, qk, vt, wo, wgu, wd, wc, bias = zip(*[sets[8 * l : 8 * l + 8] for l in range(layers)])

    def buf(n):
        return pltpu.VMEM((rows, n * WIN, LANES), F32)

    def piece(n, dtype=BF):
        return ((keep, n * WIN, LANES), dtype)

    inner = (gain[0], qk[0], vt[0], wo[0], wgu[0], wd[0])
    fed_a, low_a, high_a = call(bind(layer0_first), [piece(first, F32), piece(first), piece(first)],
        far_a, xa, x, q, k, *inner, scratch=[buf(first)],
    )
    far_high_a = send(high_a, lambda t, f: (t, odd(f)))
    far_low_a = send(low_a, lambda t, f: ((t - 1) % tiles, odd(f)))
    fed_b, low_b, high_b, low = call(bind(layer0_second), [piece(rest, F32), piece(rest), piece(rest), piece(count)],
        far_b, xb, x, q, k, *inner, low_a, scratch=[buf(rest)],
    )
    below = send(low, lambda t, f: ((t - 1) % tiles, f))
    far_high_b = send(high_b, lambda t, f: (t, odd(f)))
    far_low_b = send(low_b, lambda t, f: ((t - 1) % tiles, odd(f)))
    whole = (count, size, LANES)
    x, xn, q, k = call(bind(own1_body), [(whole, F32), (whole, BF), (whole, BF), (whole, BF)],
        ends, fed_a, fed_b, below, wc[0], bias[0], gain[1], qk[1], scalars=1,
    )
    inner = (wc[0], bias[0], gain[0], gain[1], qk[1], vt[1], wo[1], wgu[1], wd[1])
    half = count // 2
    own_a, send_a = call(bind(layer1_first), [piece(half, F32), piece(half)],
        ends, far_high_a, far_low_a, xn, x, q, k, *inner, scratch=[buf(half)], scalars=1,
    )
    own_b, down = call(bind(layer1_second), [piece(half, F32), piece(count)],
        ends, far_high_a, far_low_a, far_high_b, far_low_b, xn, x, q, k, *inner, send_a, scratch=[buf(half)], scalars=1,
    )
    above = send(down, lambda t, f: ((t + 1) % tiles, f))
    (out,) = call(bind(final_body), [((1, channels, rows, cols), BF)], ends, above, own_a, own_b, wc[1], bias[1], scalars=1)
    return out


def solution(mesh):
    in_specs = (P(("clips", "tm"), None, "tile", None), P(), P(), P(), P(), P(), P(), P(), P())
    out_specs = P(("clips", "tm"), None, "tile", None)
    return jax.shard_map(section, mesh=mesh, in_specs=in_specs, out_specs=out_specs, check_vma=False)
```

time: 51.5 us -> 41.3 us (0.80)
  local copies, waits for them, and re-layouts: 7.88 us -> 0 us
  Pallas kernels: 21.3 us -> 18 us
  starting transfers between devices: 4.75 us -> 6.4 us
    unnamed x18 -> x0, local copies, waits for them, and re-layouts: 7.78 us -> none
    pallas_call x6 -> x8, Pallas kernels: 21.3 us -> 18 us  [call(): return run(*args)]
    ppermute x5 -> x8, starting transfers between devices: 4.75 us -> 6.4 us  [send(): return lax.ppermute(x, axes, pairs)]
    ppermute x5 -> x8, waiting for transfers between devices: 17.1 us -> 16.6 us  [send(): return lax.ppermute(x, axes, pairs)]
  transfers between devices with their start and end apart: 5 -> 8, of which waited for: 3 -> 3; matrix products, arithmetic and copies ran while one was open for 0% -> 0% of each run, Pallas kernels for 6% -> 23%
where the time goes in v1:
time: 41.3 us; the launch traced here: 41.1 us
  Pallas kernels  18 us (44%)
  waiting for transfers between devices  16.6 us (40%)
  starting transfers between devices  6.4 us (15%)
    pallas_call x8, Pallas kernels, call(): return run(*args)  18 us
    ppermute x8, waiting for transfers between devices, send(): return lax.ppermute(x, axes, pairs)  16.6 us
    ppermute x8, starting transfers between devices, send(): return lax.ppermute(x, axes, pairs)  6.4 us
  transfers between devices with their start and end apart: 8, of which 3 were waited for; matrix products, arithmetic and copies ran while one was open for 0% of the time, Pallas kernels for 23%

profile of v1, /device:TPU:16, one launch (start us, length us, event | category | flops | bytes accessed | tf_op | source)
XLA Modules:
  0.0 41.1 jit_solution(1951380185995131505)
XLA Ops:
  0.0 1.5 %shard_map.91 = (f32[16,64,128]{2,1,0:T(8,128)S(1)}, bf16[9,64,128]{2,1,0:T(8,128)(2,1)S(1)}, bf16[7,64,128]{2,1,0:T(8,128)(2,1)S(1)}) custom-call(f32[2,2,120]{2,1,0:T(2,128)} %refs_0_.3, bf16[1,120,8,128]{3,2,1,0:T(8,128)(2,1)} %refs_1_.2), custom_call_target="tpu_custom_call" | custom-call | tf_op jit(solution)/shard_map/pallas_call | solution.py:323
  1.5 1.6 %collective-permute-start = (bf16[9,64,128]{2,1,0:T(8,128)(2,1)S(1)}, bf16[9,64,128]{2,1,0:T(8,128)(2,1)S(1)}, u32[]{:S(2)}, u32[]{:S(2)}) collective-permute-start(bf16[9,64,128]{2,1,0:T(8,128)(2,1)S(1)} %get-tuple-element.41.refs_8_.refs_1_), channel_id=1, source_target_pairs={{0,1},{1,0},{2,3},{3,2},{4,5},{5,4},{6,7},{7,6},{8,9},{9,8},{10,11... | collective-permute-start | bytes 442376 | tf_op jit(solution)/shard_map/ppermute | solution.py:345
  3.2 0.4 %collective-permute-start.3 = (bf16[7,64,128]{2,1,0:T(8,128)(2,1)S(1)}, bf16[7,64,128]{2,1,0:T(8,128)(2,1)S(1)}, u32[]{:S(2)}, u32[]{:S(2)}) collective-permute-start(bf16[7,64,128]{2,1,0:T(8,128)(2,1)S(1)} %get-tuple-element.43.refs_9_.refs_1_), channel_id=1, source_target_pairs={{0,1},{1,0},{2,3},{3,2},{4,5},{5,4},{6,7},{7,6},{8,9},{9,8},{10,11... | collective-permute-start | bytes 344072 | tf_op jit(solution)/shard_map/ppermute | solution.py:345
  3.6 1.9 %shard_map.92 = (bf16[16,64,128]{2,1,0:T(8,128)(2,1)S(1)}, bf16[16,64,128]{2,1,0:T(8,128)(2,1)S(1)}, f32[2,128]{1,0:T(2,128)S(1)}, bf16[128,256]{1,0:T(8,128)(2,...) custom-call(f32[2,2,120]{2,1,0:T(2,128)} %refs_0_.3, ...), custom_call_target="tpu_custom_call" | custom-call | tf_op jit(solution)/shard_map/pallas_call | solution.py:323
  5.5 2.8 %collective-permute-done.refs_0_ = bf16[9,64,128]{2,1,0:T(8,128)(2,1)S(1)} collective-permute-done((bf16[9,64,128]{2,1,0:T(8,128)(2,1)S(1)}, bf16[9,64,128]{2,1,0:T(8,128)(2,1)S(1)}, u32[]{:S(2)}, u32[]{:S(2)}) %collective-permute-start) | collective-permute-done | bytes 147488 | tf_op jit(solution)/shard_map/ppermute | solution.py:345
  8.3 2.3 %shard_map.93 = (f32[5,72,128]{2,1,0:T(8,128)S(1)}, bf16[5,72,128]{2,1,0:T(8,128)(2,1)S(1)}, bf16[5,72,128]{2,1,0:T(8,128)(2,1)S(1)}) custom-call(bf16[9,64,128]{2,1,0:T(8,128)(2,1)S(1)} %collective-permute-done.refs_0_, bf16[9,64,128]{2,1,0:T(8,128)(2,1)S(1)} %get-tuple-element.41.refs_8_.refs_1_, f32[16,64,128]{2,1,0:T(8,128)S(1)} %get-tuple-element.42.refs_2_, ...), custom_call_target="tpu_custom_call" | custom-call | tf_op jit(solution)/shard_map/pallas_call | solution.py:323
  10.5 0.0 collective-permute-done.3.refs_0_
  10.6 1.6 %shard_map.94 = (f32[5,56,128]{2,1,0:T(8,128)S(1)}, bf16[5,56,128]{2,1,0:T(8,128)(2,1)S(1)}, bf16[5,56,128]{2,1,0:T(8,128)(2,1)S(1)}, bf16[5,128,128]{2,1,0:T(8,128)(2,1)S(1)}) custom-call(bf16[7,64,128]{2,1,0:T(8,128)(2,1)S(1)} %collective-permute-done.3.refs_0_, bf16[7,64,128]{2,1,0:T(8,128)(2,1)S(1)} %get-tuple-element.43.refs_9_.refs_1_, ...), custom_call_target="tpu_custom_call" | custom-call | tf_op jit(solution)/shard_map/pallas_call | solution.py:323
  12.2 0.1 collective-permute-start.6
  12.3 1.5 %collective-permute-start.2 = (bf16[5,72,128]{2,1,0:T(8,128)(2,1)S(1)}, bf16[5,72,128]{2,1,0:T(8,128)(2,1)S(1)}, u32[]{:S(2)}, u32[]{:S(2)}) collective-permute-start(bf16[5,72,128]{2,1,0:T(8,128)(2,1)S(1)} %get-tuple-element.53.refs_11_), channel_id=1, source_target_pairs={{0,15},{1,14},{2,13},{3,12},{4,3},{5,2},{6,1},{7,0},{8,7},{9,6},{1... | collective-permute-start | bytes 276488 | tf_op jit(solution)/shard_map/ppermute | solution.py:345
  13.7 1.6 %collective-permute-start.1 = (bf16[5,72,128]{2,1,0:T(8,128)(2,1)S(1)}, bf16[5,72,128]{2,1,0:T(8,128)(2,1)S(1)}, u32[]{:S(2)}, u32[]{:S(2)}) collective-permute-start(bf16[5,72,128]{2,1,0:T(8,128)(2,1)S(1)} %get-tuple-element.52), channel_id=1, source_target_pairs={{0,3},{1,2},{2,1},{3,0},{4,7},{5,6},{6,5},{7,4},{8,11},{9,10},{10,... | collective-permute-start | bytes 276488 | tf_op jit(solution)/shard_map/ppermute | solution.py:345
  15.3 0.4 %collective-permute-start.4 = (bf16[5,56,128]{2,1,0:T(8,128)(2,1)S(1)}, bf16[5,56,128]{2,1,0:T(8,128)(2,1)S(1)}, u32[]{:S(2)}, u32[]{:S(2)}) collective-permute-start(bf16[5,56,128]{2,1,0:T(8,128)(2,1)S(1)} %get-tuple-element.54), channel_id=1, source_target_pairs={{0,3},{1,2},{2,1},{3,0},{4,7},{5,6},{6,5},{7,4},{8,11},{9,10},{10,... | collective-permute-start | bytes 215048 | tf_op jit(solution)/shard_map/ppermute | solution.py:345
  15.8 0.7 %collective-permute-start.5 = (bf16[5,56,128]{2,1,0:T(8,128)(2,1)S(1)}, bf16[5,56,128]{2,1,0:T(8,128)(2,1)S(1)}, u32[]{:S(2)}, u32[]{:S(2)}) collective-permute-start(bf16[5,56,128]{2,1,0:T(8,128)(2,1)S(1)} %get-tuple-element.55), channel_id=1, source_target_pairs={{0,15},{1,14},{2,13},{3,12},{4,3},{5,2},{6,1},{7,0},{8,7},{9,6},{1... | collective-permute-start | bytes 215048 | tf_op jit(solution)/shard_map/ppermute | solution.py:345
  16.4 0.1 add_convert_fusion.refs_0_
  16.5 0.0 collective-permute-done.6.refs_3_
  16.5 2.2 %shard_map.95 = (f32[16,64,128]{2,1,0:T(8,128)S(1)}, bf16[16,64,128]{2,1,0:T(8,128)(2,1)S(1)}, bf16[16,64,128]{2,1,0:T(8,128)(2,1)S(1)}, bf16[16,64,128]{2,1,0:T(8,128)(2,1)S(1)}) custom-call(s32[2]{0:T(128)S(1)} %add_convert_fusion.refs_0_, f32[5,72,128]{2,1,0:T(8,128)S(1)} %get-tuple-element.56.refs_1_, f32[5,56,128]{2,1,0:T(8,128)S(1)} %get-tuple-element.57.refs_2_, ...), custom_call_target="tpu_custom_call" | custom-call | tf_op jit(solution)/shard_map/pallas_call | solution.py:323
  18.7 9.1 %collective-permute-done.1.refs_1_ = bf16[5,72,128]{2,1,0:T(8,128)(2,1)S(1)} collective-permute-done((bf16[5,72,128]{2,1,0:T(8,128)(2,1)S(1)}, bf16[5,72,128]{2,1,0:T(8,128)(2,1)S(1)}, u32[]{:S(2)}, u32[]{:S(2)}) %collective-permute-start.1) | collective-permute-done | bytes 92192 | tf_op jit(solution)/shard_map/ppermute | solution.py:345
  27.8 0.0 collective-permute-done.2.refs_2_
  27.8 3.2 %shard_map.96 = (f32[5,64,128]{2,1,0:T(8,128)S(1)}, bf16[5,64,128]{2,1,0:T(8,128)(2,1)S(1)}) custom-call(s32[2]{0:T(128)S(1)} %add_convert_fusion.refs_0_, bf16[5,72,128]{2,1,0:T(8,128)(2,1)S(1)} %collective-permute-done.1.refs_1_, bf16[5,72,128]{2,1,0:T(8,128)(2,1)S(1)} %collective-permute-done.2.refs_2_, ...), custom_call_target="tpu_custom_call" | custom-call | tf_op jit(solution)/shard_map/pallas_call | solution.py:323
  31.0 0.0 collective-permute-done.4.refs_3_
  31.0 0.0 collective-permute-done.5.refs_4_
  31.0 3.2 %shard_map.97 = (f32[5,64,128]{2,1,0:T(8,128)S(1)}, bf16[5,128,128]{2,1,0:T(8,128)(2,1)S(1)}) custom-call(s32[2]{0:T(128)S(1)} %add_convert_fusion.refs_0_, bf16[5,72,128]{2,1,0:T(8,128)(2,1)S(1)} %collective-permute-done.1.refs_1_, bf16[5,72,128]{2,1,0:T(8,128)(2,1)S(1)} %collective-permute-done.2.refs_2_, ...), custom_call_target="tpu_custom_call" | custom-call | tf_op jit(solution)/shard_map/pallas_call | solution.py:323
  34.2 0.1 collective-permute-start.7
  34.3 4.7 %collective-permute-done.7.refs_1_ = bf16[5,128,128]{2,1,0:T(8,128)(2,1)S(1)} collective-permute-done((bf16[5,128,128]{2,1,0:T(8,128)(2,1)S(1)}, bf16[5,128,128]{2,1,0:T(8,128)(2,1)S(1)}, u32[]{:S(2)}, u32[]{:S(2)}) %collective-permute-start.7) | collective-permute-done | bytes 163872 | tf_op jit(solution)/shard_map/ppermute | solution.py:345
  39.0 2.1 %shard_map.98 = bf16[1,120,8,128]{3,2,1,0:T(8,128)(2,1)} custom-call(s32[2]{0:T(128)S(1)} %add_convert_fusion.refs_0_, bf16[5,128,128]{2,1,0:T(8,128)(2,1)S(1)} %collective-permute-done.7.refs_1_, f32[5,64,128]{2,1,0:T(8,128)S(1)} %get-tuple-element.73.refs_2_, f32[5,64,128]{2,1,0:T(8,128)S(1)} %get-tuple-element.74.refs_3_, ...), custom_call_target="tpu_custom_call" | custom-call | tf_op jit(solution)/shard_map/pallas_call | solution.py:323
Async XLA Ops:
  1.5 6.8 %collective-permute-start = (bf16[9,64,128]{2,1,0:T(8,128)(2,1)S(1)}, bf16[9,64,128]{2,1,0:T(8,128)(2,1)S(1)}, u32[]{:S(2)}, u32[]{:S(2)}) collective-permute-start(bf16[9,64,128]{2,1,0:T(8,128)(2,1)S(1)} %get-tuple-element.41.refs_8_.refs_1_), channel_id=1, source_target_pairs={{0,1},{1,0},{2,3},{3,2},{4,5},{5,4},{6,7},{7,6},{8,9},{9,8},{10,11... | collective-permute-start | bytes 442376 | tf_op jit(solution)/shard_map/ppermute | solution.py:345
  3.2 7.4 %collective-permute-start.3 = (bf16[7,64,128]{2,1,0:T(8,128)(2,1)S(1)}, bf16[7,64,128]{2,1,0:T(8,128)(2,1)S(1)}, u32[]{:S(2)}, u32[]{:S(2)}) collective-permute-start(bf16[7,64,128]{2,1,0:T(8,128)(2,1)S(1)} %get-tuple-element.43.refs_9_.refs_1_), channel_id=1, source_target_pairs={{0,1},{1,0},{2,3},{3,2},{4,5},{5,4},{6,7},{7,6},{8,9},{9,8},{10,11... | collective-permute-start | bytes 344072 | tf_op jit(solution)/shard_map/ppermute | solution.py:345
  12.2 4.3 %collective-permute-start.6 = (bf16[5,128,128]{2,1,0:T(8,128)(2,1)S(1)}, bf16[5,128,128]{2,1,0:T(8,128)(2,1)S(1)}, u32[]{:S(2)}, u32[]{:S(2)}) collective-permute-start(bf16[5,128,128]{2,1,0:T(8,128)(2,1)S(1)} %get-tuple-element.58), channel_id=1, source_target_pairs={{0,12},{1,13},{2,14},{3,15},{4,0},{5,1},{6,2},{7,3},{8,4},{9,5},{1... | collective-permute-start | bytes 491528 | tf_op jit(solution)/shard_map/ppermute | solution.py:345
  12.3 15.6 %collective-permute-start.2 = (bf16[5,72,128]{2,1,0:T(8,128)(2,1)S(1)}, bf16[5,72,128]{2,1,0:T(8,128)(2,1)S(1)}, u32[]{:S(2)}, u32[]{:S(2)}) collective-permute-start(bf16[5,72,128]{2,1,0:T(8,128)(2,1)S(1)} %get-tuple-element.53.refs_11_), channel_id=1, source_target_pairs={{0,15},{1,14},{2,13},{3,12},{4,3},{5,2},{6,1},{7,0},{8,7},{9,6},{1... | collective-permute-start | bytes 276488 | tf_op jit(solution)/shard_map/ppermute | solution.py:345
  13.7 14.1 %collective-permute-start.1 = (bf16[5,72,128]{2,1,0:T(8,128)(2,1)S(1)}, bf16[5,72,128]{2,1,0:T(8,128)(2,1)S(1)}, u32[]{:S(2)}, u32[]{:S(2)}) collective-permute-start(bf16[5,72,128]{2,1,0:T(8,128)(2,1)S(1)} %get-tuple-element.52), channel_id=1, source_target_pairs={{0,3},{1,2},{2,1},{3,0},{4,7},{5,6},{6,5},{7,4},{8,11},{9,10},{10,... | collective-permute-start | bytes 276488 | tf_op jit(solution)/shard_map/ppermute | solution.py:345
  15.3 15.7 %collective-permute-start.4 = (bf16[5,56,128]{2,1,0:T(8,128)(2,1)S(1)}, bf16[5,56,128]{2,1,0:T(8,128)(2,1)S(1)}, u32[]{:S(2)}, u32[]{:S(2)}) collective-permute-start(bf16[5,56,128]{2,1,0:T(8,128)(2,1)S(1)} %get-tuple-element.54), channel_id=1, source_target_pairs={{0,3},{1,2},{2,1},{3,0},{4,7},{5,6},{6,5},{7,4},{8,11},{9,10},{10,... | collective-permute-start | bytes 215048 | tf_op jit(solution)/shard_map/ppermute | solution.py:345
  15.8 15.2 %collective-permute-start.5 = (bf16[5,56,128]{2,1,0:T(8,128)(2,1)S(1)}, bf16[5,56,128]{2,1,0:T(8,128)(2,1)S(1)}, u32[]{:S(2)}, u32[]{:S(2)}) collective-permute-start(bf16[5,56,128]{2,1,0:T(8,128)(2,1)S(1)} %get-tuple-element.55), channel_id=1, source_target_pairs={{0,15},{1,14},{2,13},{3,12},{4,3},{5,2},{6,1},{7,0},{8,7},{9,6},{1... | collective-permute-start | bytes 215048 | tf_op jit(solution)/shard_map/ppermute | solution.py:345
  34.2 4.8 %collective-permute-start.7 = (bf16[5,128,128]{2,1,0:T(8,128)(2,1)S(1)}, bf16[5,128,128]{2,1,0:T(8,128)(2,1)S(1)}, u32[]{:S(2)}, u32[]{:S(2)}) collective-permute-start(bf16[5,128,128]{2,1,0:T(8,128)(2,1)S(1)} %get-tuple-element.72), channel_id=1, source_target_pairs={{0,4},{1,5},{2,6},{3,7},{4,8},{5,9},{6,10},{7,11},{8,12},{9,13},{1... | collective-permute-start | bytes 491528 | tf_op jit(solution)/shard_map/ppermute | solution.py:345

commit v2 on v1

v2 whole, which is shorter than its diff:
```python
import jax
import jax.numpy as jnp
from jax import lax
from jax.experimental import pallas as pl
from jax.experimental.pallas import tpu as pltpu
from jax.sharding import PartitionSpec as P


HEADS = 6
HD = 20
WIN = 8
LANES = 128
GROUP = 8
BF = jnp.bfloat16
F32 = jnp.float32
NT = (((1,), (1,)), ((), ()))


def up(n):
    return -(-n // LANES) * LANES


def dot(a, b):
    return jnp.dot(a, b, preferred_element_type=F32)


def dot_nt(a, b):
    return lax.dot_general(a, b, NT, preferred_element_type=F32)


def norm(x, gain, channels):
    lane = lax.broadcasted_iota(jnp.int32, x.shape, x.ndim - 1)
    mean = jnp.sum(x, axis=-1, keepdims=True) * (1.0 / channels)
    center = jnp.where(lane < channels, x - mean, 0.0)
    spread = jnp.sum(center * center, axis=-1, keepdims=True) * (1.0 / channels)
    return center * lax.rsqrt(spread + 1e-05) * gain


def to_positions(ref):
    x = ref[0].astype(F32)
    channels, rows, cols = x.shape
    x = jnp.concatenate([x, jnp.zeros((LANES - channels, rows, cols), F32)], axis=0)
    x = jnp.swapaxes(x, 0, 1)
    return jnp.stack([x[r].T for r in range(rows)], axis=0)


def windows(x):
    rows, cols, lanes = x.shape
    x = x.reshape(rows, cols // WIN, WIN, lanes)
    return jnp.swapaxes(x, 0, 1).reshape(cols // WIN, rows * WIN, lanes)


def unwindows(x, rows):
    count, _, lanes = x.shape
    x = jnp.swapaxes(x.reshape(count, rows, WIN, lanes), 0, 1)
    return x.reshape(rows, count * WIN, lanes)


def pad2(x, rows, cols):
    x = x.astype(F32)
    if x.shape[1] < cols:
        x = jnp.concatenate([x, jnp.zeros((x.shape[0], cols - x.shape[1]), F32)], axis=1)
    if x.shape[0] < rows:
        x = jnp.concatenate([x, jnp.zeros((rows - x.shape[0], cols), F32)], axis=0)
    return x


def norm_body(channels, gain_hbm, x_hbm, o_x, *refs):
    o_parts, (gain, x_ref, sems) = refs[:-3], refs[-3:]
    copies = [pltpu.make_async_copy(x_hbm, x_ref, sems.at[0]), pltpu.make_async_copy(gain_hbm, gain, sems.at[1])]
    for copy in copies:
        copy.start()
    for copy in copies:
        copy.wait()
    x = windows(to_positions(x_ref))
    o_x[...] = x
    xn = norm(x, pad2(gain[0], 2, LANES)[:1], channels).astype(BF)
    at = 0
    for part in o_parts:
        part[...] = xn[at : at + part.shape[0]]
        at += part.shape[0]


def weights_body(channels, *refs):
    hbm, layers = refs[:8], refs[2].shape[0]
    local, sems = refs[-9:-1], refs[-1]
    xs, (o_q, o_k), outs = refs[8 : -11 - 8 * layers], refs[-11 - 8 * layers : -9 - 8 * layers], refs[-9 - 8 * layers : -9]
    copies = [pltpu.make_async_copy(a, b, sems.at[i]) for i, (a, b) in enumerate(zip(hbm, local))]
    for copy in copies:
        copy.start()
    for copy in copies:
        copy.wait()
    gain, qkv, out, gate, upw, down, conv, bias = local
    hp = up(gate.shape[2])
    for l in range(layers):
        o_gain, o_qk, o_vt, o_out, o_gu, o_down, o_conv, o_bias = outs[8 * l : 8 * l + 8]
        o_gain[...] = pad2(gain[l], 2, LANES)
        o_bias[...] = pad2(bias[l : l + 1], 1, LANES)
        w = qkv[l].astype(F32)
        wq = pad2(w[:, :channels], LANES, LANES).astype(BF)
        wk = pad2(w[:, channels : 2 * channels], LANES, LANES).astype(BF)
        o_qk[:, :LANES] = wq
        o_qk[:, LANES:] = wk
        o_vt[...] = pad2(w[:, 2 * channels :], LANES, LANES).T.astype(BF)
        o_out[...] = pad2(out[l], LANES, LANES).astype(BF)
        o_gu[:, :hp] = pad2(gate[l], LANES, hp).astype(BF)
        o_gu[:, hp:] = pad2(upw[l], LANES, hp).astype(BF)
        o_down[...] = pad2(down[l], hp, LANES).astype(BF)
        blank = jnp.zeros((3 * LANES, LANES), BF)
        o_conv[3 * 3 * LANES :, :LANES] = blank
        o_conv[: 3 * LANES, LANES:] = blank
        for tap in range(9):
            a, b = divmod(tap, 3)
            piece = pad2(conv[l, tap], LANES, LANES).astype(BF)
            for v in range(2):
                at = ((a + v) * 3 + b) * LANES
                o_conv[at : at + LANES, v * LANES : (v + 1) * LANES] = piece
        if l == 0:
            project(jnp.concatenate([part[...] for part in xs], axis=0), jnp.concatenate([wq, wk], axis=1), o_q, o_k)


def project(xn, qk, o_q, o_k):
    count, size, _ = xn.shape
    both = dot(xn.reshape(count * size, LANES), qk).astype(BF)
    o_q[...] = both[:, :LANES].reshape(count, size, LANES)
    o_k[...] = both[:, LANES:].reshape(count, size, LANES)


def pieces(count):
    n = -(-count // GROUP)
    edges = [count * i // n for i in range(n + 1)]
    return [(a, b - a) for a, b in zip(edges, edges[1:])]


def pipeline(stages, total):
    held = [None] * (len(stages) + 1)
    for step in range(total + len(stages) - 1):
        for i in reversed(range(len(stages))):
            if 0 <= step - i < total:
                held[i + 1] = stages[i](step - i, held[i])


def mutual(channels, base, count, far, own, x_ref, q_ref, k_ref, gain, qk, vt, wo, wgu, wd, emit):
    size = x_ref.shape[1]
    hp = wd.shape[0]
    head_of = lax.broadcasted_iota(jnp.int32, (size, LANES), 1) // HD
    sub = lax.broadcasted_iota(jnp.int32, (LANES, LANES), 0) // HD
    half = lax.broadcasted_iota(jnp.int32, (LANES, LANES), 1) // size
    pick = [sub == 2 * j + half for j in range(HEADS // 2)]
    scale = HD ** (-0.5) * 1.4426950408889634
    cuts = pieces(count)

    def fetch(g, _):
        at, n = cuts[g]
        fn = far(at, n)
        return fn, dot(fn.reshape(n * size, LANES), qk[:, LANES:]).astype(BF).reshape(n, size, LANES)

    def scores(g, state):
        fn, fk = state
        at, n = cuts[g]
        out = []
        for i in range(n):
            w = at + i
            keys = jnp.concatenate([k_ref[base + w], fk[i]], axis=0)
            xall = jnp.concatenate([own[w], fn[i]], axis=0)
            vals = dot_nt(vt[...], xall).astype(BF)
            q = q_ref[base + w]
            qm = jnp.concatenate([jnp.where(head_of == h, q, jnp.zeros_like(q)) for h in range(HEADS)], axis=0)
            out.append((vals, dot_nt(keys, qm)))
        return out

    def attend(g, state):
        out = []
        for vals, s in state:
            top = jnp.max(s, axis=0, keepdims=True)
            p = jnp.exp2((s - top) * scale)
            p = (p * (1.0 / jnp.sum(p, axis=0, keepdims=True))).astype(BF)
            out.append(dot(vals, p))
        return out

    def merge(g, state):
        mixed = []
        for o in state:
            r = jnp.where(pick[0], o[:, :LANES], 0.0)
            for j in range(1, HEADS // 2):
                r = jnp.where(pick[j], o[:, j * LANES : (j + 1) * LANES], r)
            r = r.T
            mixed.append(r[:size] + r[size:])
        mixed = jnp.concatenate(mixed, axis=0).astype(BF)
        at, n = cuts[g]
        return x_ref[base + at : base + at + n].reshape(n * size, LANES) + dot(mixed, wo[...])

    def widen(g, att):
        nf = norm(att, gain[1:2], channels).astype(BF)
        return att, dot(nf, wgu[...])

    def narrow(g, state):
        att, gu = state
        gate = gu[:, :hp]
        act = 0.5 * gate * (1.0 + lax.erf(gate * (0.5**0.5))) * gu[:, hp:]
        fed = att + dot(act.astype(BF), wd[...])
        at, n = cuts[g]
        emit(at, fed.reshape(n, size, LANES))

    pipeline([fetch, scores, attend, merge, widen, narrow], len(cuts))


def conv_rows(x, shift, origin, edge, wc, bias):
    cols = x.shape[1]
    taps = [pltpu.roll(x, (shift + 1 - b) % cols, 1) if (shift + 1 - b) % cols else x for b in range(3)]
    return conv_taps(taps, origin, cols, edge, wc, bias)


def conv_cols(x, skip, origin, cols, edge, wc, bias):
    n = x.shape[1] - 2 * skip
    taps = [x[:, skip - 1 + b : skip - 1 + b + n] for b in range(3)]
    return conv_taps(taps, origin, cols, edge, wc, bias)


def conv_taps(taps, origin, cols, edge, wc, bias):
    center = taps[1]
    rows, width = center.shape[0] - 2, center.shape[1]
    col = (lax.broadcasted_iota(jnp.int32, (width, 1), 0) + origin) % cols
    parts = []
    for b, moved in enumerate(taps):
        if b != 1:
            moved = jnp.where(col == (0 if b == 0 else cols - 1), 0.0, moved)
        parts.append(moved)
    lines = [jnp.concatenate([p[r] for p in parts], axis=1) for r in range(rows + 2)]
    packed = [line.astype(BF) for line in lines]
    blocks = []
    for j in range(rows // 2):
        four = packed[2 * j : 2 * j + 4]
        if edge is not None:
            last, at = edge
            if 2 * j + 1 == at - 1:
                four[3] = jnp.where(last, 0.0, lines[2 * j + 3]).astype(BF)
            if 2 * j == at:
                four[0] = jnp.where(last, 0.0, lines[2 * j]).astype(BF)
        blocks.append(jnp.concatenate(four, axis=1))
    mid = len(blocks) // 2
    both = [dot(jnp.concatenate(b, axis=0), wc[...]) for b in (blocks[:mid], blocks[mid:])]
    both = jnp.concatenate(both, axis=0)
    out = []
    for r in range(rows):
        j, v = divmod(r, 2)
        part = both[j * width : (j + 1) * width, v * LANES : (v + 1) * LANES]
        out.append(center[1 + r] + bias[...] + part)
    return jnp.stack(out, axis=0)


def collect(buf):
    def emit(at, fed):
        buf[:, at * WIN : (at + fed.shape[0]) * WIN, :] = unwindows(fed, buf.shape[0])

    return emit


def layer0_body(channels, base, far, own, x_ref, q_ref, k_ref, gain, qk, vt, wo, wgu, wd, *refs):
    buf = refs[-1]
    earlier = refs[: len(refs) - 4]
    outs = refs[len(earlier) : -1]
    rows, keep = buf.shape[0], outs[0].shape[0]
    mutual(channels, base, far.shape[0], lambda at, n: far[at : at + n], own, x_ref, q_ref, k_ref, gain, qk, vt, wo, wgu, wd, collect(buf))
    fresh = (buf[rows - keep :], buf[:keep].astype(BF), buf[rows - keep :].astype(BF))
    for out, now, old in zip(outs, fresh, earlier or (None,) * 3):
        edge = out.shape[1] - now.shape[1]
        if edge:
            out[:, :edge, :] = old[...]
        out[:, edge:, :] = now


def layer0_last(channels, base, far, own, x_ref, q_ref, k_ref, gain, qk, vt, wo, wgu, wd, low_a, o_fed, o_low, o_high, o_whole, buf):
    rows, keep = buf.shape[0], o_low.shape[0]
    mutual(channels, base, far.shape[0], lambda at, n: far[at : at + n], own, x_ref, q_ref, k_ref, gain, qk, vt, wo, wgu, wd, collect(buf))
    o_fed[...] = buf[rows - keep :]
    low = buf[:keep].astype(BF)
    o_low[...] = low
    o_high[...] = buf[rows - keep :].astype(BF)
    first = base * WIN
    o_whole[:, :first, :] = low_a[...]
    o_whole[:, first:, :] = low


def own1_body(channels, ends, fed_a, fed_b, low, wc, bias, gain, qk, o_x, o_xn, o_q, o_k):
    high = jnp.concatenate([fed_a[...], fed_b[...]], axis=1)
    x = jnp.concatenate([high, low[...].astype(F32)], axis=0)
    cols = x.shape[1]
    x = jnp.concatenate([x, x[:, :WIN]], axis=1)
    cuts = pieces(cols // WIN)

    def mix(g, _):
        at, n = cuts[g]
        part = x[:, at * WIN : (at + n + 1) * WIN]
        return windows(conv_cols(part, WIN // 2, at * WIN + WIN // 2, cols, (ends[0] == 1, WIN // 2), wc, bias))

    def finish(g, part):
        at, n = cuts[g]
        o_x[at : at + n] = part
        xn = norm(part, gain[0:1], channels).astype(BF)
        o_xn[at : at + n] = xn
        project(xn, qk[...], o_q.at[at : at + n], o_k.at[at : at + n])

    pipeline([mix, finish], len(cuts))


def far_normed(channels, ends, x, base, cols, wc, bias, gain):
    def far(at, n):
        part = x[:, at * WIN : (at + n + 1) * WIN]
        part = conv_cols(part, WIN // 2, base + at * WIN + WIN // 2, cols, (ends[0] == 1, WIN // 2), wc, bias)
        return norm(windows(part), gain[0:1], channels).astype(BF)

    return far


def layer1_first(channels, ends, high, low, xn_ref, x_ref, q_ref, k_ref, wc, bias, gain0, gain, qk, vt, wo, wgu, wd, o_own, o_send, buf):
    x = jnp.concatenate([high[...], low[...]], axis=0).astype(F32)
    rows, keep = buf.shape[0], o_own.shape[0]
    count = buf.shape[1] // WIN
    far = far_normed(channels, ends, x, 0, 2 * buf.shape[1], wc, bias, gain)
    mutual(channels, 0, count, far, xn_ref, x_ref, q_ref, k_ref, gain, qk, vt, wo, wgu, wd, collect(buf))
    o_own[...] = buf[:keep]
    o_send[...] = buf[rows - keep :].astype(BF)


def layer1_second(channels, ends, high_a, low_a, high_b, low_b, xn_ref, x_ref, q_ref, k_ref, wc, bias, gain0, gain, qk, vt, wo, wgu, wd, o_own, o_send, buf):
    xa = jnp.concatenate([high_a[...], low_a[...]], axis=0).astype(F32)
    xb = jnp.concatenate([high_b[...], low_b[...]], axis=0).astype(F32)
    half = buf.shape[1]
    x = jnp.concatenate([xa[:, half:], xb, xa[:, :WIN]], axis=1)
    rows, keep = buf.shape[0], o_own.shape[0]
    count = half // WIN
    far = far_normed(channels, ends, x, half, 2 * half, wc, bias, gain)
    mutual(channels, count, count, far, xn_ref.at[count:], x_ref, q_ref, k_ref, gain, qk, vt, wo, wgu, wd, collect(buf))
    o_own[...] = buf[:keep]
    o_send[...] = buf[rows - keep :].astype(BF)


def final_body(channels, ends, high_a, high_b, own_a, own_b, wc, bias, o_ref):
    first, last = ends[1] == 1, ends[0] == 1
    high = jnp.concatenate([high_a[...], high_b[...]], axis=1).astype(F32)
    own = jnp.concatenate([own_a[...], own_b[...]], axis=1)
    top = jnp.where(first, 0.0, high[:1])
    low = jnp.where(last, 0.0, own[-1:])
    x = jnp.concatenate([top, high[1:], own[:-1], low], axis=0)
    y = conv_rows(x, WIN // 2, 0, None, wc, bias)
    y = jnp.stack([y[r].T for r in range(y.shape[0])], axis=0)
    y = jnp.swapaxes(y, 0, 1)[:channels]
    o_ref[0] = y.astype(BF)


def call(body, outs, *args, scratch=(), scalars=0, remote=0, work=0):
    vm = pl.BlockSpec(memory_space=pltpu.VMEM)
    sm = pl.BlockSpec(memory_space=pltpu.SMEM)
    hbm = pl.BlockSpec(memory_space=pltpu.HBM)
    specs = [sm] * scalars + [hbm] * remote
    cost = pl.CostEstimate(flops=work, bytes_accessed=1024, transcendentals=0) if work else None
    run = pl.pallas_call(
        body,
        out_shape=[jax.ShapeDtypeStruct(s, d) for s, d in outs],
        in_specs=specs + [vm] * (len(args) - len(specs)),
        out_specs=[vm] * len(outs),
        scratch_shapes=list(scratch),
        cost_estimate=cost,
        compiler_params=pltpu.CompilerParams(vmem_limit_bytes=24 * 1024 * 1024),
    )
    args = [pltpu.with_memory_space_constraint(a, pltpu.HBM) if i < scalars + remote and i >= scalars else a for i, a in enumerate(args)]
    return run(*args)


def section(frames, *params):
    ln_gain, gate_weight = params[0], params[3]
    _, channels, rows, cols = frames.shape
    layers = ln_gain.shape[0]
    hp = up(gate_weight.shape[2])
    tiles, depth = lax.axis_size("tile"), lax.axis_size("tm")
    where = lax.axis_index("tile")
    ends = jnp.stack([where == tiles - 1, where == 0]).astype(jnp.int32)
    axes = ("tile", "tm")

    def odd(f):
        return (f + 1) % depth if f % 2 else (f - 1) % depth

    def send(x, target):
        pairs = []
        for t in range(tiles):
            for f in range(depth):
                to_t, to_f = target(t, f)
                pairs.append((t * depth + f, to_t * depth + to_f))
        return lax.ppermute(x, axes, pairs)

    def bind(body, *extra):
        def wrapped(*refs):
            return body(channels, *extra, *refs)

        wrapped.__name__ = body.__name__
        return wrapped

    count = cols // WIN
    first = count // 2 + 1
    rest = count - first
    keep = rows // 2 + 1
    size = rows * WIN
    dma = pltpu.SemaphoreType.DMA
    parts = [-(-first // 2), first // 2, rest]
    x, *xs = call(
        bind(norm_body),
        [((count, size, LANES), F32)] + [((n, size, LANES), BF) for n in parts],
        ln_gain, frames,
        scratch=[pltpu.VMEM(ln_gain.shape, F32), pltpu.VMEM(frames.shape, BF), dma((2,))],
        remote=2,
    )
    far = [send(part, lambda t, f: (t, f ^ 1)) for part in xs]
    q, k, *sets = call(bind(weights_body),
        [((count, size, LANES), BF), ((count, size, LANES), BF)]
        + [
            ((2, LANES), F32),
            ((LANES, 2 * LANES), BF),
            ((LANES, LANES), BF),
            ((LANES, LANES), BF),
            ((LANES, 2 * hp), BF),
            ((hp, LANES), BF),
            ((12 * LANES, 2 * LANES), BF),
            ((1, LANES), F32),
        ]
        * layers,
        *params, *xs,
        scratch=[pltpu.VMEM(p.shape, p.dtype) for p in params] + [dma((len(params),))],
        remote=len(params),
    )

    gain, qk, vt, wo, wgu, wd, wc, bias = zip(*[sets[8 * l : 8 * l + 8] for l in range(layers)])

    def buf(n):
        return pltpu.VMEM((rows, n * WIN, LANES), F32)

    def piece(n, dtype=BF):
        return ((keep, n * WIN, LANES), dtype)

    inner = (gain[0], qk[0], vt[0], wo[0], wgu[0], wd[0])
    early = call(
        bind(layer0_body, 0), [piece(parts[0], F32), piece(parts[0]), piece(parts[0])],
        far[0], xs[0], x, q, k, *inner, scratch=[buf(parts[0])],
    )
    fed_a, low_a, high_a = call(
        bind(layer0_body, parts[0]), [piece(first, F32), piece(first), piece(first)],
        far[1], xs[1], x, q, k, *inner, *early, scratch=[buf(parts[1])],
    )
    far_high_a = send(high_a, lambda t, f: (t, odd(f)))
    far_low_a = send(low_a, lambda t, f: ((t - 1) % tiles, odd(f)))
    fed_b, low_b, high_b, low = call(bind(layer0_last, first), [piece(rest, F32), piece(rest), piece(rest), piece(count)],
        far[2], xs[2], x, q, k, *inner, low_a, scratch=[buf(rest)],
    )
    below = send(low, lambda t, f: ((t - 1) % tiles, f))
    far_high_b = send(high_b, lambda t, f: (t, odd(f)))
    far_low_b = send(low_b, lambda t, f: ((t - 1) % tiles, odd(f)))
    whole = (count, size, LANES)
    x, xn, q, k = call(bind(own1_body), [(whole, F32), (whole, BF), (whole, BF), (whole, BF)],
        ends, fed_a, fed_b, below, wc[0], bias[0], gain[1], qk[1], scalars=1,
    )
    inner = (wc[0], bias[0], gain[0], gain[1], qk[1], vt[1], wo[1], wgu[1], wd[1])
    half = count // 2
    own_a, send_a = call(bind(layer1_first), [piece(half, F32), piece(half)],
        ends, far_high_a, far_low_a, xn, x, q, k, *inner, scratch=[buf(half)], scalars=1,
    )
    above_a = send(send_a, lambda t, f: ((t + 1) % tiles, f))
    own_b, send_b = call(bind(layer1_second), [piece(half, F32), piece(half)],
        ends, far_high_a, far_low_a, far_high_b, far_low_b, xn, x, q, k, *inner, scratch=[buf(half)], scalars=1,
    )
    above_b = send(send_b, lambda t, f: ((t + 1) % tiles, f))
    (out,) = call(bind(final_body), [((1, channels, rows, cols), BF)], ends, above_a, above_b, own_a, own_b, wc[1], bias[1], scalars=1)
    return out


def solution(mesh):
    in_specs = (P(("clips", "tm"), None, "tile", None), P(), P(), P(), P(), P(), P(), P(), P())
    out_specs = P(("clips", "tm"), None, "tile", None)
    return jax.shard_map(section, mesh=mesh, in_specs=in_specs, out_specs=out_specs, check_vma=False)
```

time: 41.3 us -> 43.1 us (1.044)
  starting transfers between devices: 6.4 us -> 9.79 us
  waiting for transfers between devices: 16.6 us -> 15.2 us
    ppermute x8 -> x10, starting transfers between devices: 6.4 us -> 9.79 us  [send(): return lax.ppermute(x, axes, pairs)]
    ppermute x8 -> x10, waiting for transfers between devices: 16.6 us -> 15.2 us  [send(): return lax.ppermute(x, axes, pairs)]
    pallas_call x8 -> x9, Pallas kernels: 18 us -> 17.8 us  [call(): return run(*args)]
  transfers between devices with their start and end apart: 8 -> 10, of which waited for: 3 -> 4; matrix products, arithmetic and copies ran while one was open for 0% -> 0% of each run, Pallas kernels for 23% -> 23%
where the time goes in v2:
time: 43.1 us; the launch traced here: 43 us
  Pallas kernels  17.8 us (41%)
  waiting for transfers between devices  15.2 us (35%)
  starting transfers between devices  9.79 us (23%)
    pallas_call x9, Pallas kernels, call(): return run(*args)  17.8 us
    ppermute x10, waiting for transfers between devices, send(): return lax.ppermute(x, axes, pairs)  15.2 us
    ppermute x10, starting transfers between devices, send(): return lax.ppermute(x, axes, pairs)  9.79 us
  transfers between devices with their start and end apart: 10, of which 4 were waited for; matrix products, arithmetic and copies ran while one was open for 0% of the time, Pallas kernels for 23%

profile of v2, /device:TPU:16, one launch (start us, length us, event | category | flops | bytes accessed | tf_op | source)
XLA Modules:
  0.0 43.0 jit_solution(12774555092751528913)
XLA Ops:
  0.0 1.5 %shard_map.91 = (f32[16,64,128]{2,1,0:T(8,128)S(1)}, bf16[5,64,128]{2,1,0:T(8,128)(2,1)S(1)}, bf16[4,64,128]{2,1,0:T(8,128)(2,1)S(1)}, bf16[7,64,128]{2,1,0:T(8,128)(2,1)S(1)}) custom-call(f32[2,2,120]{2,1,0:T(2,128)} %refs_0_.3, bf16[1,120,8,128]{3,2,1,0:T(8,128)(2,1)} %refs_1_.2), custom_call_target="tpu_custom_call" | custom-call | tf_op jit(solution)/shard_map/pallas_call | solution.py:368
  1.5 1.6 %collective-permute-start.4 = (bf16[7,64,128]{2,1,0:T(8,128)(2,1)S(1)}, bf16[7,64,128]{2,1,0:T(8,128)(2,1)S(1)}, u32[]{:S(2)}, u32[]{:S(2)}) collective-permute-start(bf16[7,64,128]{2,1,0:T(8,128)(2,1)S(1)} %get-tuple-element.48.refs_10_.refs_1_), channel_id=1, source_target_pairs={{0,1},{1,0},{2,3},{3,2},{4,5},{5,4},{6,7},{7,6},{8,9},{9,8},{10,11... | collective-permute-start | bytes 344072 | tf_op jit(solution)/shard_map/ppermute | solution.py:390
  3.1 0.4 %collective-permute-start.1 = (bf16[5,64,128]{2,1,0:T(8,128)(2,1)S(1)}, bf16[5,64,128]{2,1,0:T(8,128)(2,1)S(1)}, u32[]{:S(2)}, u32[]{:S(2)}) collective-permute-start(bf16[5,64,128]{2,1,0:T(8,128)(2,1)S(1)} %get-tuple-element.47.refs_8_.refs_1_), channel_id=1, source_target_pairs={{0,1},{1,0},{2,3},{3,2},{4,5},{5,4},{6,7},{7,6},{8,9},{9,8},{10,11... | collective-permute-start | bytes 245768 | tf_op jit(solution)/shard_map/ppermute | solution.py:390
  3.6 1.6 %collective-permute-start = (bf16[4,64,128]{2,1,0:T(8,128)(2,1)S(1)}, bf16[4,64,128]{2,1,0:T(8,128)(2,1)S(1)}, u32[]{:S(2)}, u32[]{:S(2)}) collective-permute-start(bf16[4,64,128]{2,1,0:T(8,128)(2,1)S(1)} %get-tuple-element.45.refs_9_.refs_1_), channel_id=1, source_target_pairs={{0,1},{1,0},{2,3},{3,2},{4,5},{5,4},{6,7},{7,6},{8,9},{9,8},{10,11... | collective-permute-start | bytes 196616 | tf_op jit(solution)/shard_map/ppermute | solution.py:390
  5.2 2.1 %shard_map.92 = (bf16[16,64,128]{2,1,0:T(8,128)(2,1)S(1)}, bf16[16,64,128]{2,1,0:T(8,128)(2,1)S(1)}, f32[2,128]{1,0:T(2,128)S(1)}, bf16[128,256]{1,0:T(8,128)(2,...) custom-call(f32[2,2,120]{2,1,0:T(2,128)} %refs_0_.3, ...), custom_call_target="tpu_custom_call" | custom-call | tf_op jit(solution)/shard_map/pallas_call | solution.py:368
  7.3 1.7 %collective-permute-done.1.refs_0_ = bf16[5,64,128]{2,1,0:T(8,128)(2,1)S(1)} collective-permute-done((bf16[5,64,128]{2,1,0:T(8,128)(2,1)S(1)}, bf16[5,64,128]{2,1,0:T(8,128)(2,1)S(1)}, u32[]{:S(2)}, u32[]{:S(2)}) %collective-permute-start.1) | collective-permute-done | bytes 81952 | tf_op jit(solution)/shard_map/ppermute | solution.py:390
  8.9 1.4 %shard_map.93 = (f32[5,40,128]{2,1,0:T(8,128)S(1)}, bf16[5,40,128]{2,1,0:T(8,128)(2,1)S(1)}, bf16[5,40,128]{2,1,0:T(8,128)(2,1)S(1)}) custom-call(bf16[5,64,128]{2,1,0:T(8,128)(2,1)S(1)} %collective-permute-done.1.refs_0_, bf16[5,64,128]{2,1,0:T(8,128)(2,1)S(1)} %get-tuple-element.47.refs_8_.refs_1_, f32[16,64,128]{2,1,0:T(8,128)S(1)} %get-tuple-element.46.refs_2_, ...), custom_call_target="tpu_custom_call" | custom-call | tf_op jit(solution)/shard_map/pallas_call | solution.py:368
  10.3 0.0 collective-permute-done.refs_0_
  10.4 1.3 %shard_map.94 = (f32[5,72,128]{2,1,0:T(8,128)S(1)}, bf16[5,72,128]{2,1,0:T(8,128)(2,1)S(1)}, bf16[5,72,128]{2,1,0:T(8,128)(2,1)S(1)}) custom-call(bf16[4,64,128]{2,1,0:T(8,128)(2,1)S(1)} %collective-permute-done.refs_0_, bf16[4,64,128]{2,1,0:T(8,128)(2,1)S(1)} %get-tuple-element.45.refs_9_.refs_1_, f32[16,64,128]{2,1,0:T(8,128)S(1)} %get-tuple-element.46.refs_2_, ...), custom_call_target="tpu_custom_call" | custom-call | tf_op jit(solution)/shard_map/pallas_call | solution.py:368
  11.7 0.0 collective-permute-done.4.refs_0_
  11.7 1.6 %shard_map.95 = (f32[5,56,128]{2,1,0:T(8,128)S(1)}, bf16[5,56,128]{2,1,0:T(8,128)(2,1)S(1)}, bf16[5,56,128]{2,1,0:T(8,128)(2,1)S(1)}, bf16[5,128,128]{2,1,0:T(8,128)(2,1)S(1)}) custom-call(bf16[7,64,128]{2,1,0:T(8,128)(2,1)S(1)} %collective-permute-done.4.refs_0_, bf16[7,64,128]{2,1,0:T(8,128)(2,1)S(1)} %get-tuple-element.48.refs_10_.refs_1_, ...), custom_call_target="tpu_custom_call" | custom-call | tf_op jit(solution)/shard_map/pallas_call | solution.py:368
  13.3 0.1 collective-permute-start.5
  13.4 1.5 %collective-permute-start.3 = (bf16[5,72,128]{2,1,0:T(8,128)(2,1)S(1)}, bf16[5,72,128]{2,1,0:T(8,128)(2,1)S(1)}, u32[]{:S(2)}, u32[]{:S(2)}) collective-permute-start(bf16[5,72,128]{2,1,0:T(8,128)(2,1)S(1)} %get-tuple-element.61.refs_11_), channel_id=1, source_target_pairs={{0,15},{1,14},{2,13},{3,12},{4,3},{5,2},{6,1},{7,0},{8,7},{9,6},{1... | collective-permute-start | bytes 276488 | tf_op jit(solution)/shard_map/ppermute | solution.py:390
  14.8 1.6 %collective-permute-start.2 = (bf16[5,72,128]{2,1,0:T(8,128)(2,1)S(1)}, bf16[5,72,128]{2,1,0:T(8,128)(2,1)S(1)}, u32[]{:S(2)}, u32[]{:S(2)}) collective-permute-start(bf16[5,72,128]{2,1,0:T(8,128)(2,1)S(1)} %get-tuple-element.60), channel_id=1, source_target_pairs={{0,3},{1,2},{2,1},{3,0},{4,7},{5,6},{6,5},{7,4},{8,11},{9,10},{10,... | collective-permute-start | bytes 276488 | tf_op jit(solution)/shard_map/ppermute | solution.py:390
  16.4 0.5 %collective-permute-start.7 = (bf16[5,56,128]{2,1,0:T(8,128)(2,1)S(1)}, bf16[5,56,128]{2,1,0:T(8,128)(2,1)S(1)}, u32[]{:S(2)}, u32[]{:S(2)}) collective-permute-start(bf16[5,56,128]{2,1,0:T(8,128)(2,1)S(1)} %get-tuple-element.78), channel_id=1, source_target_pairs={{0,3},{1,2},{2,1},{3,0},{4,7},{5,6},{6,5},{7,4},{8,11},{9,10},{10,... | collective-permute-start | bytes 215048 | tf_op jit(solution)/shard_map/ppermute | solution.py:390
  16.9 0.7 %collective-permute-start.8 = (bf16[5,56,128]{2,1,0:T(8,128)(2,1)S(1)}, bf16[5,56,128]{2,1,0:T(8,128)(2,1)S(1)}, u32[]{:S(2)}, u32[]{:S(2)}) collective-permute-start(bf16[5,56,128]{2,1,0:T(8,128)(2,1)S(1)} %get-tuple-element.79), channel_id=1, source_target_pairs={{0,15},{1,14},{2,13},{3,12},{4,3},{5,2},{6,1},{7,0},{8,7},{9,6},{1... | collective-permute-start | bytes 215048 | tf_op jit(solution)/shard_map/ppermute | solution.py:390
  17.6 0.1 add_convert_fusion.refs_0_
  17.6 0.0 collective-permute-done.5.refs_3_
  17.6 2.1 %shard_map.96 = (f32[16,64,128]{2,1,0:T(8,128)S(1)}, bf16[16,64,128]{2,1,0:T(8,128)(2,1)S(1)}, bf16[16,64,128]{2,1,0:T(8,128)(2,1)S(1)}, bf16[16,64,128]{2,1,0:T(8,128)(2,1)S(1)}) custom-call(s32[2]{0:T(128)S(1)} %add_convert_fusion.refs_0_, f32[5,72,128]{2,1,0:T(8,128)S(1)} %get-tuple-element.62.refs_1_, f32[5,56,128]{2,1,0:T(8,128)S(1)} %get-tuple-element.63.refs_2_, ...), custom_call_target="tpu_custom_call" | custom-call | tf_op jit(solution)/shard_map/pallas_call | solution.py:368
  19.8 9.1 %collective-permute-done.2.refs_1_ = bf16[5,72,128]{2,1,0:T(8,128)(2,1)S(1)} collective-permute-done((bf16[5,72,128]{2,1,0:T(8,128)(2,1)S(1)}, bf16[5,72,128]{2,1,0:T(8,128)(2,1)S(1)}, u32[]{:S(2)}, u32[]{:S(2)}) %collective-permute-start.2) | collective-permute-done | bytes 92192 | tf_op jit(solution)/shard_map/ppermute | solution.py:390
  28.9 0.0 collective-permute-done.3.refs_2_
  28.9 0.8 %collective-permute-done.7.refs_3_ = bf16[5,56,128]{2,1,0:T(8,128)(2,1)S(1)} collective-permute-done((bf16[5,56,128]{2,1,0:T(8,128)(2,1)S(1)}, bf16[5,56,128]{2,1,0:T(8,128)(2,1)S(1)}, u32[]{:S(2)}, u32[]{:S(2)}) %collective-permute-start.7) | collective-permute-done | bytes 71712 | tf_op jit(solution)/shard_map/ppermute | solution.py:390
  29.7 0.0 collective-permute-done.8.refs_4_
  29.7 2.9 %shard_map.98 = (f32[5,64,128]{2,1,0:T(8,128)S(1)}, bf16[5,64,128]{2,1,0:T(8,128)(2,1)S(1)}) custom-call(s32[2]{0:T(128)S(1)} %add_convert_fusion.refs_0_, bf16[5,72,128]{2,1,0:T(8,128)(2,1)S(1)} %collective-permute-done.2.refs_1_, bf16[5,72,128]{2,1,0:T(8,128)(2,1)S(1)} %collective-permute-done.3.refs_2_, ...), custom_call_target="tpu_custom_call" | custom-call | tf_op jit(solution)/shard_map/pallas_call | solution.py:368
  32.6 1.6 %collective-permute-start.9 = (bf16[5,64,128]{2,1,0:T(8,128)(2,1)S(1)}, bf16[5,64,128]{2,1,0:T(8,128)(2,1)S(1)}, u32[]{:S(2)}, u32[]{:S(2)}) collective-permute-start(bf16[5,64,128]{2,1,0:T(8,128)(2,1)S(1)} %get-tuple-element.80), channel_id=1, source_target_pairs={{0,4},{1,5},{2,6},{3,7},{4,8},{5,9},{6,10},{7,11},{8,12},{9,13},{1... | collective-permute-start | bytes 245768 | tf_op jit(solution)/shard_map/ppermute | solution.py:390
  34.1 2.9 %shard_map.97 = (f32[5,64,128]{2,1,0:T(8,128)S(1)}, bf16[5,64,128]{2,1,0:T(8,128)(2,1)S(1)}) custom-call(s32[2]{0:T(128)S(1)} %add_convert_fusion.refs_0_, bf16[5,72,128]{2,1,0:T(8,128)(2,1)S(1)} %collective-permute-done.2.refs_1_, bf16[5,72,128]{2,1,0:T(8,128)(2,1)S(1)} %collective-permute-done.3.refs_2_, ...), custom_call_target="tpu_custom_call" | custom-call | tf_op jit(solution)/shard_map/pallas_call | solution.py:368
  37.0 0.3 collective-permute-start.6
  37.4 0.0 collective-permute-done.9.refs_2_
  37.4 3.6 %collective-permute-done.6.refs_1_ = bf16[5,64,128]{2,1,0:T(8,128)(2,1)S(1)} collective-permute-done((bf16[5,64,128]{2,1,0:T(8,128)(2,1)S(1)}, bf16[5,64,128]{2,1,0:T(8,128)(2,1)S(1)}, u32[]{:S(2)}, u32[]{:S(2)}) %collective-permute-start.6) | collective-permute-done | bytes 81952 | tf_op jit(solution)/shard_map/ppermute | solution.py:390
  41.0 2.0 %shard_map.99 = bf16[1,120,8,128]{3,2,1,0:T(8,128)(2,1)} custom-call(s32[2]{0:T(128)S(1)} %add_convert_fusion.refs_0_, bf16[5,64,128]{2,1,0:T(8,128)(2,1)S(1)} %collective-permute-done.6.refs_1_, bf16[5,64,128]{2,1,0:T(8,128)(2,1)S(1)} %collective-permute-done.9.refs_2_, f32[5,64,128]{2,1,0:T(8,128)S(1)} %get-tuple-element.81.refs_3_, ...), custom_call_target="tpu_custom_call" | custom-call | tf_op jit(solution)/shard_map/pallas_call | solution.py:368
Async XLA Ops:
  1.5 10.2 %collective-permute-start.4 = (bf16[7,64,128]{2,1,0:T(8,128)(2,1)S(1)}, bf16[7,64,128]{2,1,0:T(8,128)(2,1)S(1)}, u32[]{:S(2)}, u32[]{:S(2)}) collective-permute-start(bf16[7,64,128]{2,1,0:T(8,128)(2,1)S(1)} %get-tuple-element.48.refs_10_.refs_1_), channel_id=1, source_target_pairs={{0,1},{1,0},{2,3},{3,2},{4,5},{5,4},{6,7},{7,6},{8,9},{9,8},{10,11... | collective-permute-start | bytes 344072 | tf_op jit(solution)/shard_map/ppermute | solution.py:390
  3.1 5.8 %collective-permute-start.1 = (bf16[5,64,128]{2,1,0:T(8,128)(2,1)S(1)}, bf16[5,64,128]{2,1,0:T(8,128)(2,1)S(1)}, u32[]{:S(2)}, u32[]{:S(2)}) collective-permute-start(bf16[5,64,128]{2,1,0:T(8,128)(2,1)S(1)} %get-tuple-element.47.refs_8_.refs_1_), channel_id=1, source_target_pairs={{0,1},{1,0},{2,3},{3,2},{4,5},{5,4},{6,7},{7,6},{8,9},{9,8},{10,11... | collective-permute-start | bytes 245768 | tf_op jit(solution)/shard_map/ppermute | solution.py:390
  3.6 6.7 %collective-permute-start = (bf16[4,64,128]{2,1,0:T(8,128)(2,1)S(1)}, bf16[4,64,128]{2,1,0:T(8,128)(2,1)S(1)}, u32[]{:S(2)}, u32[]{:S(2)}) collective-permute-start(bf16[4,64,128]{2,1,0:T(8,128)(2,1)S(1)} %get-tuple-element.45.refs_9_.refs_1_), channel_id=1, source_target_pairs={{0,1},{1,0},{2,3},{3,2},{4,5},{5,4},{6,7},{7,6},{8,9},{9,8},{10,11... | collective-permute-start | bytes 196616 | tf_op jit(solution)/shard_map/ppermute | solution.py:390
  13.3 4.3 %collective-permute-start.5 = (bf16[5,128,128]{2,1,0:T(8,128)(2,1)S(1)}, bf16[5,128,128]{2,1,0:T(8,128)(2,1)S(1)}, u32[]{:S(2)}, u32[]{:S(2)}) collective-permute-start(bf16[5,128,128]{2,1,0:T(8,128)(2,1)S(1)} %get-tuple-element.64), channel_id=1, source_target_pairs={{0,12},{1,13},{2,14},{3,15},{4,0},{5,1},{6,2},{7,3},{8,4},{9,5},{1... | collective-permute-start | bytes 491528 | tf_op jit(solution)/shard_map/ppermute | solution.py:390
  13.4 15.6 %collective-permute-start.3 = (bf16[5,72,128]{2,1,0:T(8,128)(2,1)S(1)}, bf16[5,72,128]{2,1,0:T(8,128)(2,1)S(1)}, u32[]{:S(2)}, u32[]{:S(2)}) collective-permute-start(bf16[5,72,128]{2,1,0:T(8,128)(2,1)S(1)} %get-tuple-element.61.refs_11_), channel_id=1, source_target_pairs={{0,15},{1,14},{2,13},{3,12},{4,3},{5,2},{6,1},{7,0},{8,7},{9,6},{1... | collective-permute-start | bytes 276488 | tf_op jit(solution)/shard_map/ppermute | solution.py:390
  14.8 14.1 %collective-permute-start.2 = (bf16[5,72,128]{2,1,0:T(8,128)(2,1)S(1)}, bf16[5,72,128]{2,1,0:T(8,128)(2,1)S(1)}, u32[]{:S(2)}, u32[]{:S(2)}) collective-permute-start(bf16[5,72,128]{2,1,0:T(8,128)(2,1)S(1)} %get-tuple-element.60), channel_id=1, source_target_pairs={{0,3},{1,2},{2,1},{3,0},{4,7},{5,6},{6,5},{7,4},{8,11},{9,10},{10,... | collective-permute-start | bytes 276488 | tf_op jit(solution)/shard_map/ppermute | solution.py:390
  16.4 13.3 %collective-permute-start.7 = (bf16[5,56,128]{2,1,0:T(8,128)(2,1)S(1)}, bf16[5,56,128]{2,1,0:T(8,128)(2,1)S(1)}, u32[]{:S(2)}, u32[]{:S(2)}) collective-permute-start(bf16[5,56,128]{2,1,0:T(8,128)(2,1)S(1)} %get-tuple-element.78), channel_id=1, source_target_pairs={{0,3},{1,2},{2,1},{3,0},{4,7},{5,6},{6,5},{7,4},{8,11},{9,10},{10,... | collective-permute-start | bytes 215048 | tf_op jit(solution)/shard_map/ppermute | solution.py:390
  16.9 12.8 %collective-permute-start.8 = (bf16[5,56,128]{2,1,0:T(8,128)(2,1)S(1)}, bf16[5,56,128]{2,1,0:T(8,128)(2,1)S(1)}, u32[]{:S(2)}, u32[]{:S(2)}) collective-permute-start(bf16[5,56,128]{2,1,0:T(8,128)(2,1)S(1)} %get-tuple-element.79), channel_id=1, source_target_pairs={{0,15},{1,14},{2,13},{3,12},{4,3},{5,2},{6,1},{7,0},{8,7},{9,6},{1... | collective-permute-start | bytes 215048 | tf_op jit(solution)/shard_map/ppermute | solution.py:390
  32.6 4.8 %collective-permute-start.9 = (bf16[5,64,128]{2,1,0:T(8,128)(2,1)S(1)}, bf16[5,64,128]{2,1,0:T(8,128)(2,1)S(1)}, u32[]{:S(2)}, u32[]{:S(2)}) collective-permute-start(bf16[5,64,128]{2,1,0:T(8,128)(2,1)S(1)} %get-tuple-element.80), channel_id=1, source_target_pairs={{0,4},{1,5},{2,6},{3,7},{4,8},{5,9},{6,10},{7,11},{8,12},{9,13},{1... | collective-permute-start | bytes 245768 | tf_op jit(solution)/shard_map/ppermute | solution.py:390
  37.0 3.9 %collective-permute-start.6 = (bf16[5,64,128]{2,1,0:T(8,128)(2,1)S(1)}, bf16[5,64,128]{2,1,0:T(8,128)(2,1)S(1)}, u32[]{:S(2)}, u32[]{:S(2)}) collective-permute-start(bf16[5,64,128]{2,1,0:T(8,128)(2,1)S(1)} %get-tuple-element.77), channel_id=1, source_target_pairs={{0,4},{1,5},{2,6},{3,7},{4,8},{5,9},{6,10},{7,11},{8,12},{9,13},{1... | collective-permute-start | bytes 245768 | tf_op jit(solution)/shard_map/ppermute | solution.py:390

commit v3 on v2

--- a/solution.py
+++ b/solution.py
@@ -10,7 +10,8 @@
 HD = 20
 WIN = 8
 LANES = 128
-GROUP = 8
+GROUP = 12
+LEAD = 2
 BF = jnp.bfloat16
 F32 = jnp.float32
 NT = (((1,), (1,)), ((), ()))
@@ -65,32 +66,31 @@
     return x
 
 
-def norm_body(channels, gain_hbm, x_hbm, o_x, *refs):
-    o_parts, (gain, x_ref, sems) = refs[:-3], refs[-3:]
-    copies = [pltpu.make_async_copy(x_hbm, x_ref, sems.at[0]), pltpu.make_async_copy(gain_hbm, gain, sems.at[1])]
-    for copy in copies:
+def norm_body(channels, x_hbm, *refs):
+    x_ref, sems = refs[-2:]
+    n = sems.shape[0] - 1
+    params, o_x, o_parts, local = refs[:n], refs[n], refs[n + 1 : -2 - n], refs[-2 - n : -2]
+    first = [pltpu.make_async_copy(x_hbm, x_ref, sems.at[n]), pltpu.make_async_copy(params[0], local[0], sems.at[0])]
+    later = [pltpu.make_async_copy(params[i], local[i], sems.at[i]) for i in range(1, n)]
+    for copy in first + later:
         copy.start()
-    for copy in copies:
+    for copy in first:
         copy.wait()
     x = windows(to_positions(x_ref))
     o_x[...] = x
-    xn = norm(x, pad2(gain[0], 2, LANES)[:1], channels).astype(BF)
+    xn = norm(x, pad2(local[0][0], 2, LANES)[:1], channels).astype(BF)
     at = 0
     for part in o_parts:
         part[...] = xn[at : at + part.shape[0]]
         at += part.shape[0]
+    for copy in later:
+        copy.wait()
 
 
 def weights_body(channels, *refs):
-    hbm, layers = refs[:8], refs[2].shape[0]
-    local, sems = refs[-9:-1], refs[-1]
-    xs, (o_q, o_k), outs = refs[8 : -11 - 8 * layers], refs[-11 - 8 * layers : -9 - 8 * layers], refs[-9 - 8 * layers : -9]
-    copies = [pltpu.make_async_copy(a, b, sems.at[i]) for i, (a, b) in enumerate(zip(hbm, local))]
-    for copy in copies:
-        copy.start()
-    for copy in copies:
-        copy.wait()
-    gain, qkv, out, gate, upw, down, conv, bias = local
+    gain, qkv, out, gate, upw, down, conv, bias = refs[:8]
+    layers = out.shape[0]
+    xs, (o_q, o_k), outs = refs[8 : -2 - 8 * layers], refs[-2 - 8 * layers : -8 * layers], refs[-8 * layers :]
     hp = up(gate.shape[2])
     for l in range(layers):
         o_gain, o_qk, o_vt, o_out, o_gu, o_down, o_conv, o_bias = outs[8 * l : 8 * l + 8]
@@ -146,7 +146,7 @@
     head_of = lax.broadcasted_iota(jnp.int32, (size, LANES), 1) // HD
     sub = lax.broadcasted_iota(jnp.int32, (LANES, LANES), 0) // HD
     half = lax.broadcasted_iota(jnp.int32, (LANES, LANES), 1) // size
-    pick = [sub == 2 * j + half for j in range(HEADS // 2)]
+    valid = (sub % 2 == half) & (sub < HEADS)
     scale = HD ** (-0.5) * 1.4426950408889634
     cuts = pieces(count)
 
@@ -158,15 +158,18 @@
     def scores(g, state):
         fn, fk = state
         at, n = cuts[g]
+        both = [jnp.concatenate([own[at + i], fn[i]], axis=0) for i in range(n)]
+        vals = []
+        for i in range(0, n, 2):
+            pair = both[i : i + 2]
+            v = dot_nt(vt[...], jnp.concatenate(pair, axis=0)).astype(BF)
+            vals += [v[:, 2 * size * j : 2 * size * (j + 1)] for j in range(len(pair))]
         out = []
         for i in range(n):
-            w = at + i
-            keys = jnp.concatenate([k_ref[base + w], fk[i]], axis=0)
-            xall = jnp.concatenate([own[w], fn[i]], axis=0)
-            vals = dot_nt(vt[...], xall).astype(BF)
-            q = q_ref[base + w]
+            keys = jnp.concatenate([k_ref[base + at + i], fk[i]], axis=0)
+            q = q_ref[base + at + i]
             qm = jnp.concatenate([jnp.where(head_of == h, q, jnp.zeros_like(q)) for h in range(HEADS)], axis=0)
-            out.append((vals, dot_nt(keys, qm)))
+            out.append((vals[i], dot_nt(keys, qm)))
         return out
 
     def attend(g, state):
@@ -175,16 +178,16 @@
             top = jnp.max(s, axis=0, keepdims=True)
             p = jnp.exp2((s - top) * scale)
             p = (p * (1.0 / jnp.sum(p, axis=0, keepdims=True))).astype(BF)
-            out.append(dot(vals, p))
+            cut = 4 * HD
+            out.append((dot(vals[:cut], p[:, : 4 * size]), dot(vals[cut:], p[:, 4 * size :])))
         return out
 
     def merge(g, state):
         mixed = []
-        for o in state:
-            r = jnp.where(pick[0], o[:, :LANES], 0.0)
-            for j in range(1, HEADS // 2):
-                r = jnp.where(pick[j], o[:, j * LANES : (j + 1) * LANES], r)
-            r = r.T
+        for front, back in state:
+            two = 2 * HD
+            r = jnp.concatenate([front[:two, :LANES], front[two:, LANES:], back], axis=0)
+            r = jnp.where(valid, r, 0.0).T
             mixed.append(r[:size] + r[size:])
         mixed = jnp.concatenate(mixed, axis=0).astype(BF)
         at, n = cuts[g]
@@ -238,9 +241,14 @@
             if 2 * j == at:
                 four[0] = jnp.where(last, 0.0, lines[2 * j]).astype(BF)
         blocks.append(jnp.concatenate(four, axis=1))
-    mid = len(blocks) // 2
-    both = [dot(jnp.concatenate(b, axis=0), wc[...]) for b in (blocks[:mid], blocks[mid:])]
-    both = jnp.concatenate(both, axis=0)
+    if width == cols:
+        lhs = jnp.concatenate(blocks, axis=0)
+        mid = lhs.shape[1] // 2
+        both = dot(lhs[:, :mid], wc[:mid, :]) + dot(lhs[:, mid:], wc[mid:, :])
+    else:
+        mid = len(blocks) // 2
+        both = [dot(jnp.concatenate(b, axis=0), wc[...]) for b in (blocks[:mid], blocks[mid:])]
+        both = jnp.concatenate(both, axis=0)
     out = []
     for r in range(rows):
         j, v = divmod(r, 2)
@@ -249,6 +257,58 @@
     return jnp.stack(out, axis=0)
 
 
+def packing(groups, channels):
+    spare = LANES - channels
+    if spare == 0 or channels % spare:
+        return 0, 1
+    per = channels // spare
+    return groups // (per + 1), per
+
+
+def packed_rows(shape, channels):
+    groups = shape[0] * shape[1] // WIN
+    return ((groups - packing(groups, channels)[0]) * WIN, LANES)
+
+
+def pack(x, channels):
+    groups = x.shape[0] * x.shape[1] // WIN
+    extra, per = packing(groups, channels)
+    x = x.reshape(groups, WIN, LANES)
+    lane = lax.broadcasted_iota(jnp.int32, (WIN, LANES), 1)
+    out = []
+    for c in range(groups - extra):
+        e, i = divmod(c, per)
+        line = x[c]
+        if e < extra:
+            turn = (channels - (LANES - channels) * i) % LANES
+            moved = pltpu.roll(x[groups - extra + e], turn, 1) if turn else x[groups - extra + e]
+            line = jnp.where(lane < channels, line, moved)
+        out.append(line)
+    return jnp.concatenate(out, axis=0).astype(BF)
+
+
+def unpack(y, rows, channels):
+    y = y.astype(F32).reshape(-1, WIN, LANES)
+    groups = next(g for g in range(y.shape[0], 2 * y.shape[0] + 1) if g - packing(g, channels)[0] == y.shape[0] and g % rows == 0)
+    extra, per = packing(groups, channels)
+    spare = LANES - channels
+    lane = lax.broadcasted_iota(jnp.int32, (WIN, LANES), 1)
+    out, tails = [], []
+    for c in range(groups - extra):
+        e, i = divmod(c, per)
+        if e >= extra:
+            out.append(y[c])
+            continue
+        out.append(jnp.where(lane < channels, y[c], 0.0))
+        turn = (spare * i - channels) % LANES
+        moved = pltpu.roll(y[c], turn, 1) if turn else y[c]
+        if i == 0:
+            tails.append(jnp.where(lane < spare, moved, 0.0))
+        else:
+            tails[e] = jnp.where((lane >= spare * i) & (lane < spare * (i + 1)), moved, tails[e])
+    return jnp.stack(out + tails, axis=0).reshape(rows, groups // rows * WIN, LANES)
+
+
 def collect(buf):
     def emit(at, fed):
         buf[:, at * WIN : (at + fed.shape[0]) * WIN, :] = unwindows(fed, buf.shape[0])
@@ -256,30 +316,34 @@
     return emit
 
 
-def layer0_body(channels, base, far, own, x_ref, q_ref, k_ref, gain, qk, vt, wo, wgu, wd, *refs):
-    buf = refs[-1]
-    earlier = refs[: len(refs) - 4]
-    outs = refs[len(earlier) : -1]
-    rows, keep = buf.shape[0], outs[0].shape[0]
-    mutual(channels, base, far.shape[0], lambda at, n: far[at : at + n], own, x_ref, q_ref, k_ref, gain, qk, vt, wo, wgu, wd, collect(buf))
-    fresh = (buf[rows - keep :], buf[:keep].astype(BF), buf[rows - keep :].astype(BF))
-    for out, now, old in zip(outs, fresh, earlier or (None,) * 3):
-        edge = out.shape[1] - now.shape[1]
-        if edge:
-            out[:, :edge, :] = old[...]
-        out[:, edge:, :] = now
-
-
-def layer0_last(channels, base, far, own, x_ref, q_ref, k_ref, gain, qk, vt, wo, wgu, wd, low_a, o_fed, o_low, o_high, o_whole, buf):
+def layer0_first(channels, far, own, x_ref, q_ref, k_ref, gain, qk, vt, wo, wgu, wd, o_fed, o_low, buf):
+    rows, keep = buf.shape[0], o_low.shape[0]
+    mutual(channels, 0, far.shape[0], lambda at, n: far[at : at + n], own, x_ref, q_ref, k_ref, gain, qk, vt, wo, wgu, wd, collect(buf))
+    o_fed[...] = buf[rows - keep :]
+    o_low[...] = buf[:keep].astype(BF)
+
+
+def layer0_middle(channels, base, far, own, x_ref, q_ref, k_ref, gain, qk, vt, wo, wgu, wd, fed_a, low_a, o_fed, o_low, o_plow, o_phigh, buf):
     rows, keep = buf.shape[0], o_low.shape[0]
     mutual(channels, base, far.shape[0], lambda at, n: far[at : at + n], own, x_ref, q_ref, k_ref, gain, qk, vt, wo, wgu, wd, collect(buf))
-    o_fed[...] = buf[rows - keep :]
-    low = buf[:keep].astype(BF)
-    o_low[...] = low
-    o_high[...] = buf[rows - keep :].astype(BF)
+    fed = jnp.concatenate([fed_a[...], buf[rows - keep :]], axis=1)
+    low = jnp.concatenate([low_a[...].astype(F32), buf[:keep]], axis=1)
+    o_fed[...] = fed
+    o_low[...] = low.astype(BF)
+    o_plow[...] = pack(low, channels)
+    o_phigh[...] = pack(fed, channels)
+
+
+def layer0_last(channels, base, far, own, x_ref, q_ref, k_ref, gain, qk, vt, wo, wgu, wd, low_a, o_fed, o_plow, o_phigh, o_low, buf):
+    rows, keep = buf.shape[0], o_low.shape[0]
+    mutual(channels, base, far.shape[0], lambda at, n: far[at : at + n], own, x_ref, q_ref, k_ref, gain, qk, vt, wo, wgu, wd, collect(buf))
+    fed, low = buf[rows - keep :], buf[:keep]
+    o_fed[...] = fed
+    o_plow[...] = pack(low, channels)
+    o_phigh[...] = pack(fed, channels)
     first = base * WIN
-    o_whole[:, :first, :] = low_a[...]
-    o_whole[:, first:, :] = low
+    o_low[:, :first, :] = low_a[...]
+    o_low[:, first:, :] = low.astype(BF)
 
 
 def own1_body(channels, ends, fed_a, fed_b, low, wc, bias, gain, qk, o_x, o_xn, o_q, o_k):
@@ -287,7 +351,7 @@
     x = jnp.concatenate([high, low[...].astype(F32)], axis=0)
     cols = x.shape[1]
     x = jnp.concatenate([x, x[:, :WIN]], axis=1)
-    cuts = pieces(cols // WIN)
+    cuts = [(0, cols // WIN)]
 
     def mix(g, _):
         at, n = cuts[g]
@@ -314,29 +378,30 @@
 
 
 def layer1_first(channels, ends, high, low, xn_ref, x_ref, q_ref, k_ref, wc, bias, gain0, gain, qk, vt, wo, wgu, wd, o_own, o_send, buf):
-    x = jnp.concatenate([high[...], low[...]], axis=0).astype(F32)
     rows, keep = buf.shape[0], o_own.shape[0]
+    x = jnp.concatenate([unpack(high[...], keep, channels), unpack(low[...], keep, channels)], axis=0)
     count = buf.shape[1] // WIN
-    far = far_normed(channels, ends, x, 0, 2 * buf.shape[1], wc, bias, gain)
+    far = far_normed(channels, ends, x, 0, x_ref.shape[0] * WIN, wc, bias, gain)
     mutual(channels, 0, count, far, xn_ref, x_ref, q_ref, k_ref, gain, qk, vt, wo, wgu, wd, collect(buf))
     o_own[...] = buf[:keep]
     o_send[...] = buf[rows - keep :].astype(BF)
 
 
 def layer1_second(channels, ends, high_a, low_a, high_b, low_b, xn_ref, x_ref, q_ref, k_ref, wc, bias, gain0, gain, qk, vt, wo, wgu, wd, o_own, o_send, buf):
-    xa = jnp.concatenate([high_a[...], low_a[...]], axis=0).astype(F32)
-    xb = jnp.concatenate([high_b[...], low_b[...]], axis=0).astype(F32)
-    half = buf.shape[1]
-    x = jnp.concatenate([xa[:, half:], xb, xa[:, :WIN]], axis=1)
-    rows, keep = buf.shape[0], o_own.shape[0]
-    count = half // WIN
-    far = far_normed(channels, ends, x, half, 2 * half, wc, bias, gain)
-    mutual(channels, count, count, far, xn_ref.at[count:], x_ref, q_ref, k_ref, gain, qk, vt, wo, wgu, wd, collect(buf))
+    keep = o_own.shape[0]
+    xa = jnp.concatenate([unpack(part[...], keep, channels) for part in (high_a, low_a)], axis=0)
+    xb = jnp.concatenate([unpack(part[...], keep, channels) for part in (high_b, low_b)], axis=0)
+    cols = x_ref.shape[0] * WIN
+    base = cols - buf.shape[1]
+    x = jnp.concatenate([xa[:, base:], xb, xa[:, :WIN]], axis=1)
+    rows, at, count = buf.shape[0], base // WIN, buf.shape[1] // WIN
+    far = far_normed(channels, ends, x, base, cols, wc, bias, gain)
+    mutual(channels, at, count, far, xn_ref.at[at:], x_ref, q_ref, k_ref, gain, qk, vt, wo, wgu, wd, collect(buf))
     o_own[...] = buf[:keep]
     o_send[...] = buf[rows - keep :].astype(BF)
 
 
-def final_body(channels, ends, high_a, high_b, own_a, own_b, wc, bias, o_ref):
+def final_body(channels, ends, high_a, high_b, own_a, own_b, wc, bias, o_hbm, out, sems):
     first, last = ends[1] == 1, ends[0] == 1
     high = jnp.concatenate([high_a[...], high_b[...]], axis=1).astype(F32)
     own = jnp.concatenate([own_a[...], own_b[...]], axis=1)
@@ -345,23 +410,30 @@
     x = jnp.concatenate([top, high[1:], own[:-1], low], axis=0)
     y = conv_rows(x, WIN // 2, 0, None, wc, bias)
     y = jnp.stack([y[r].T for r in range(y.shape[0])], axis=0)
-    y = jnp.swapaxes(y, 0, 1)[:channels]
-    o_ref[0] = y.astype(BF)
-
-
-def call(body, outs, *args, scratch=(), scalars=0, remote=0, work=0):
+    copies = []
+    n = sems.shape[0]
+    step = channels // n
+    for i in range(n):
+        at = i * step
+        out[0, at : at + step] = jnp.swapaxes(y[:, at : at + step], 0, 1).astype(BF)
+        copy = pltpu.make_async_copy(out.at[0, at : at + step], o_hbm.at[0, at : at + step], sems.at[i])
+        copy.start()
+        copies.append(copy)
+    for copy in copies:
+        copy.wait()
+
+
+def call(body, outs, *args, scratch=(), scalars=0, remote=0, away=False):
     vm = pl.BlockSpec(memory_space=pltpu.VMEM)
     sm = pl.BlockSpec(memory_space=pltpu.SMEM)
     hbm = pl.BlockSpec(memory_space=pltpu.HBM)
     specs = [sm] * scalars + [hbm] * remote
-    cost = pl.CostEstimate(flops=work, bytes_accessed=1024, transcendentals=0) if work else None
     run = pl.pallas_call(
         body,
         out_shape=[jax.ShapeDtypeStruct(s, d) for s, d in outs],
         in_specs=specs + [vm] * (len(args) - len(specs)),
-        out_specs=[vm] * len(outs),
+        out_specs=[hbm if away else vm] * len(outs),
         scratch_shapes=list(scratch),
-        cost_estimate=cost,
         compiler_params=pltpu.CompilerParams(vmem_limit_bytes=24 * 1024 * 1024),
     )
     args = [pltpu.with_memory_space_constraint(a, pltpu.HBM) if i < scalars + remote and i >= scalars else a for i, a in enumerate(args)]
@@ -397,7 +469,7 @@
         return wrapped
 
     count = cols // WIN
-    first = count // 2 + 1
+    first = count // 2 + LEAD
     rest = count - first
     keep = rows // 2 + 1
     size = rows * WIN
@@ -405,11 +477,12 @@
     parts = [-(-first // 2), first // 2, rest]
     x, *xs = call(
         bind(norm_body),
-        [((count, size, LANES), F32)] + [((n, size, LANES), BF) for n in parts],
-        ln_gain, frames,
-        scratch=[pltpu.VMEM(ln_gain.shape, F32), pltpu.VMEM(frames.shape, BF), dma((2,))],
-        remote=2,
-    )
+        [((count, size, LANES), F32)] + [((n, size, LANES), BF) for n in parts] + [(p.shape, p.dtype) for p in params],
+        frames, *params,
+        scratch=[pltpu.VMEM(frames.shape, BF), dma((1 + len(params),))],
+        remote=1 + len(params),
+    )
+    xs, params = xs[: len(parts)], xs[len(parts) :]
     far = [send(part, lambda t, f: (t, f ^ 1)) for part in xs]
     q, k, *sets = call(bind(weights_body),
         [((count, size, LANES), BF), ((count, size, LANES), BF)]
@@ -425,8 +498,6 @@
         ]
         * layers,
         *params, *xs,
-        scratch=[pltpu.VMEM(p.shape, p.dtype) for p in params] + [dma((len(params),))],
-        remote=len(params),
     )
 
     gain, qk, vt, wo, wgu, wd, wc, bias = zip(*[sets[8 * l : 8 * l + 8] for l in range(layers)])
@@ -438,18 +509,22 @@
         return ((keep, n * WIN, LANES), dtype)
 
     inner = (gain[0], qk[0], vt[0], wo[0], wgu[0], wd[0])
+
+    def thin(n):
+        return (packed_rows(piece(n)[0], channels), BF)
+
     early = call(
-        bind(layer0_body, 0), [piece(parts[0], F32), piece(parts[0]), piece(parts[0])],
+        bind(layer0_first), [piece(parts[0], F32), piece(parts[0])],
         far[0], xs[0], x, q, k, *inner, scratch=[buf(parts[0])],
     )
-    fed_a, low_a, high_a = call(
-        bind(layer0_body, parts[0]), [piece(first, F32), piece(first), piece(first)],
+    fed_a, low, low_a, high_a = call(
+        bind(layer0_middle, parts[0]), [piece(first, F32), piece(first), thin(first), thin(first)],
         far[1], xs[1], x, q, k, *inner, *early, scratch=[buf(parts[1])],
     )
     far_high_a = send(high_a, lambda t, f: (t, odd(f)))
     far_low_a = send(low_a, lambda t, f: ((t - 1) % tiles, odd(f)))
-    fed_b, low_b, high_b, low = call(bind(layer0_last, first), [piece(rest, F32), piece(rest), piece(rest), piece(count)],
-        far[2], xs[2], x, q, k, *inner, low_a, scratch=[buf(rest)],
+    fed_b, low_b, high_b, low = call(bind(layer0_last, first), [piece(rest, F32), thin(rest), thin(rest), piece(count)],
+        far[2], xs[2], x, q, k, *inner, low, scratch=[buf(rest)],
     )
     below = send(low, lambda t, f: ((t - 1) % tiles, f))
     far_high_b = send(high_b, lambda t, f: (t, odd(f)))
@@ -459,16 +534,18 @@
         ends, fed_a, fed_b, below, wc[0], bias[0], gain[1], qk[1], scalars=1,
     )
     inner = (wc[0], bias[0], gain[0], gain[1], qk[1], vt[1], wo[1], wgu[1], wd[1])
-    half = count // 2
+    half = first - 1
     own_a, send_a = call(bind(layer1_first), [piece(half, F32), piece(half)],
         ends, far_high_a, far_low_a, xn, x, q, k, *inner, scratch=[buf(half)], scalars=1,
     )
     above_a = send(send_a, lambda t, f: ((t + 1) % tiles, f))
-    own_b, send_b = call(bind(layer1_second), [piece(half, F32), piece(half)],
-        ends, far_high_a, far_low_a, far_high_b, far_low_b, xn, x, q, k, *inner, scratch=[buf(half)], scalars=1,
+    own_b, send_b = call(bind(layer1_second), [piece(count - half, F32), piece(count - half)],
+        ends, far_high_a, far_low_a, far_high_b, far_low_b, xn, x, q, k, *inner, scratch=[buf(count - half)], scalars=1,
     )
     above_b = send(send_b, lambda t, f: ((t + 1) % tiles, f))
-    (out,) = call(bind(final_body), [((1, channels, rows, cols), BF)], ends, above_a, above_b, own_a, own_b, wc[1], bias[1], scalars=1)
+    (out,) = call(bind(final_body), [((1, channels, rows, cols), BF)], ends, above_a, above_b, own_a, own_b, wc[1], bias[1],
+        scratch=[pltpu.VMEM(frames.shape, BF), dma((5,))], scalars=1, away=True,
+    )
     return out
 
 

time: 43.1 us -> 40.4 us (0.937)
  waiting for transfers between devices: 15.2 us -> 13.5 us
  Pallas kernels: 17.8 us -> 16.3 us
    ppermute x10, waiting for transfers between devices: 15.2 us -> 13.5 us  [send(): return lax.ppermute(x, axes, pairs)]
    pallas_call x9, Pallas kernels: 17.8 us -> 16.3 us  [call(): return run(*args)]
  transfers between devices with their start and end apart: 10 -> 10, of which waited for: 4 -> 4; matrix products, arithmetic and copies ran while one was open for 0% -> 0% of each run, Pallas kernels for 23% -> 28%
where the time goes in v3:
time: 40.4 us; the launch traced here: 40.2 us
  Pallas kernels  16.3 us (40%)
  waiting for transfers between devices  13.5 us (33%)
  starting transfers between devices  10.2 us (25%)
    pallas_call x9, Pallas kernels, call(): return run(*args)  16.3 us
    ppermute x10, waiting for transfers between devices, send(): return lax.ppermute(x, axes, pairs)  13.5 us
    ppermute x10, starting transfers between devices, send(): return lax.ppermute(x, axes, pairs)  10.2 us
  transfers between devices with their start and end apart: 10, of which 4 were waited for; matrix products, arithmetic and copies ran while one was open for 0% of the time, Pallas kernels for 28%

profile of v3, /device:TPU:16, one launch (start us, length us, event | category | flops | bytes accessed | tf_op | source)
XLA Modules:
  0.0 40.2 jit_solution(7714277235270945285)
XLA Ops:
  0.0 1.6 %shard_map.91 = (f32[16,64,128]{2,1,0:T(8,128)S(1)}, bf16[5,64,128]{2,1,0:T(8,128)(2,1)S(1)}, bf16[5,64,128]{2,1,0:T(8,128)(2,1)S(1)}, bf16[6,64,128]{2,1,0:T(8,...) custom-call(bf16[1,120,8,128]{3,2,1,0:T(8,128)(2,1)} %refs_0_.1, ...), custom_call_target="tpu_custom_call" | custom-call | tf_op jit(solution)/shard_map/pallas_call | solution.py:440
  1.6 1.6 %collective-permute-start.4 = (bf16[6,64,128]{2,1,0:T(8,128)(2,1)S(1)}, bf16[6,64,128]{2,1,0:T(8,128)(2,1)S(1)}, u32[]{:S(2)}, u32[]{:S(2)}) collective-permute-start(bf16[6,64,128]{2,1,0:T(8,128)(2,1)S(1)} %get-tuple-element.64.refs_10_.refs_1_), channel_id=1, source_target_pairs={{0,1},{1,0},{2,3},{3,2},{4,5},{5,4},{6,7},{7,6},{8,9},{9,8},{10,11... | collective-permute-start | bytes 294920 | tf_op jit(solution)/shard_map/ppermute | solution.py:462
  3.2 0.4 %collective-permute-start.1 = (bf16[5,64,128]{2,1,0:T(8,128)(2,1)S(1)}, bf16[5,64,128]{2,1,0:T(8,128)(2,1)S(1)}, u32[]{:S(2)}, u32[]{:S(2)}) collective-permute-start(bf16[5,64,128]{2,1,0:T(8,128)(2,1)S(1)} %get-tuple-element.63.refs_8_.refs_1_), channel_id=1, source_target_pairs={{0,1},{1,0},{2,3},{3,2},{4,5},{5,4},{6,7},{7,6},{8,9},{9,8},{10,11... | collective-permute-start | bytes 245768 | tf_op jit(solution)/shard_map/ppermute | solution.py:462
  3.7 1.6 %collective-permute-start = (bf16[5,64,128]{2,1,0:T(8,128)(2,1)S(1)}, bf16[5,64,128]{2,1,0:T(8,128)(2,1)S(1)}, u32[]{:S(2)}, u32[]{:S(2)}) collective-permute-start(bf16[5,64,128]{2,1,0:T(8,128)(2,1)S(1)} %get-tuple-element.53.refs_9_.refs_1_), channel_id=1, source_target_pairs={{0,1},{1,0},{2,3},{3,2},{4,5},{5,4},{6,7},{7,6},{8,9},{9,8},{10,11... | collective-permute-start | bytes 245768 | tf_op jit(solution)/shard_map/ppermute | solution.py:462
  5.2 0.6 %shard_map.92 = (bf16[16,64,128]{2,1,0:T(8,128)(2,1)S(1)}, bf16[16,64,128]{2,1,0:T(8,128)(2,1)S(1)}, f32[2,128]{1,0:T(2,128)S(1)}, bf16[128,256]{1,0:T(8,128)(2,...) custom-call(f32[2,2,120]{2,1,0:T(2,128)S(1)} %get-tuple-element.55.r, ...), custom_call_target="tpu_custom_call" | custom-call | tf_op jit(solution)/shard_map/pallas_call | solution.py:440
  5.9 3.0 %collective-permute-done.1.refs_0_ = bf16[5,64,128]{2,1,0:T(8,128)(2,1)S(1)} collective-permute-done((bf16[5,64,128]{2,1,0:T(8,128)(2,1)S(1)}, bf16[5,64,128]{2,1,0:T(8,128)(2,1)S(1)}, u32[]{:S(2)}, u32[]{:S(2)}) %collective-permute-start.1) | collective-permute-done | bytes 81952 | tf_op jit(solution)/shard_map/ppermute | solution.py:462
  8.9 1.4 %shard_map.93 = (f32[5,40,128]{2,1,0:T(8,128)S(1)}, bf16[5,40,128]{2,1,0:T(8,128)(2,1)S(1)}) custom-call(bf16[5,64,128]{2,1,0:T(8,128)(2,1)S(1)} %collective-permute-done.1.refs_0_, bf16[5,64,128]{2,1,0:T(8,128)(2,1)S(1)} %get-tuple-element.63.refs_8_.refs_1_, f32[16,64,128]{2,1,0:T(8,128)S(1)} %get-tuple-element.54.refs_2_, ...), custom_call_target="tpu_custom_call" | custom-call | tf_op jit(solution)/shard_map/pallas_call | solution.py:440
  10.3 0.0 collective-permute-done.refs_0_
  10.3 1.5 %shard_map.94 = (f32[5,80,128]{2,1,0:T(8,128)S(1)}, bf16[5,80,128]{2,1,0:T(8,128)(2,1)S(1)}, bf16[376,128]{1,0:T(8,128)(2,1)S(1)}, bf16[376,128]{1,0:T(8,128)(2,1)S(1)}) custom-call(bf16[5,64,128]{2,1,0:T(8,128)(2,1)S(1)} %collective-permute-done.refs_0_, bf16[5,64,128]{2,1,0:T(8,128)(2,1)S(1)} %get-tuple-element.53.refs_9_.refs_1_, ...), custom_call_target="tpu_custom_call" | custom-call | tf_op jit(solution)/shard_map/pallas_call | solution.py:440
  11.8 0.0 collective-permute-done.4.refs_0_
  11.8 1.6 %shard_map.95 = (f32[5,48,128]{2,1,0:T(8,128)S(1)}, bf16[232,128]{1,0:T(8,128)(2,1)S(1)}, bf16[232,128]{1,0:T(8,128)(2,1)S(1)}, bf16[5,128,128]{2,1,0:T(8,128)(2,1)S(1)}) custom-call(bf16[6,64,128]{2,1,0:T(8,128)(2,1)S(1)} %collective-permute-done.4.refs_0_, bf16[6,64,128]{2,1,0:T(8,128)(2,1)S(1)} %get-tuple-element.64.refs_10_.refs_1_, ...), custom_call_target="tpu_custom_call" | custom-call | tf_op jit(solution)/shard_map/pallas_call | solution.py:440
  13.4 0.1 collective-permute-start.5
  13.4 0.4 %collective-permute-start.2 = (bf16[376,128]{1,0:T(8,128)(2,1)S(1)}, bf16[376,128]{1,0:T(8,128)(2,1)S(1)}, u32[]{:S(2)}, u32[]{:S(2)}) collective-permute-start(bf16[376,128]{1,0:T(8,128)(2,1)S(1)} %get-tuple-element.75), channel_id=1, source_target_pairs={{0,3},{1,2},{2,1},{3,0},{4,7},{5,6},{6,5},{7,4},{8,11},{9,10},{10,... | collective-permute-start | bytes 288776 | tf_op jit(solution)/shard_map/ppermute | solution.py:462
  13.9 2.3 %collective-permute-start.3 = (bf16[376,128]{1,0:T(8,128)(2,1)S(1)}, bf16[376,128]{1,0:T(8,128)(2,1)S(1)}, u32[]{:S(2)}, u32[]{:S(2)}) collective-permute-start(bf16[376,128]{1,0:T(8,128)(2,1)S(1)} %get-tuple-element.76), channel_id=1, source_target_pairs={{0,15},{1,14},{2,13},{3,12},{4,3},{5,2},{6,1},{7,0},{8,7},{9,6},{1... | collective-permute-start | bytes 288776 | tf_op jit(solution)/shard_map/ppermute | solution.py:462
  16.2 0.4 collective-permute-start.7
  16.6 1.3 %collective-permute-start.8 = (bf16[232,128]{1,0:T(8,128)(2,1)S(1)}, bf16[232,128]{1,0:T(8,128)(2,1)S(1)}, u32[]{:S(2)}, u32[]{:S(2)}) collective-permute-start(bf16[232,128]{1,0:T(8,128)(2,1)S(1)} %get-tuple-element.95), channel_id=1, source_target_pairs={{0,15},{1,14},{2,13},{3,12},{4,3},{5,2},{6,1},{7,0},{8,7},{9,6},{1... | collective-permute-start | bytes 178184 | tf_op jit(solution)/shard_map/ppermute | solution.py:462
  17.9 0.1 add_convert_fusion.refs_0_
  18.0 0.0 collective-permute-done.5.refs_3_
  18.0 2.0 %shard_map.96 = (f32[16,64,128]{2,1,0:T(8,128)S(1)}, bf16[16,64,128]{2,1,0:T(8,128)(2,1)S(1)}, bf16[16,64,128]{2,1,0:T(8,128)(2,1)S(1)}, bf16[16,64,128]{2,1,0:T(8,128)(2,1)S(1)}) custom-call(s32[2]{0:T(128)S(1)} %add_convert_fusion.refs_0_, f32[5,80,128]{2,1,0:T(8,128)S(1)} %get-tuple-element.77.refs_1_, f32[5,48,128]{2,1,0:T(8,128)S(1)} %get-tuple-element.79.refs_2_, ...), custom_call_target="tpu_custom_call" | custom-call | tf_op jit(solution)/shard_map/pallas_call | solution.py:440
  20.0 5.8 %collective-permute-done.2.refs_1_ = bf16[376,128]{1,0:T(8,128)(2,1)S(1)} collective-permute-done((bf16[376,128]{1,0:T(8,128)(2,1)S(1)}, bf16[376,128]{1,0:T(8,128)(2,1)S(1)}, u32[]{:S(2)}, u32[]{:S(2)}) %collective-permute-start.2) | collective-permute-done | bytes 96288 | tf_op jit(solution)/shard_map/ppermute | solution.py:462
  25.8 1.0 %collective-permute-done.3.refs_2_ = bf16[376,128]{1,0:T(8,128)(2,1)S(1)} collective-permute-done((bf16[376,128]{1,0:T(8,128)(2,1)S(1)}, bf16[376,128]{1,0:T(8,128)(2,1)S(1)}, u32[]{:S(2)}, u32[]{:S(2)}) %collective-permute-start.3) | collective-permute-done | bytes 96288 | tf_op jit(solution)/shard_map/ppermute | solution.py:462
  26.8 3.1 %shard_map.97 = (f32[5,72,128]{2,1,0:T(8,128)S(1)}, bf16[5,72,128]{2,1,0:T(8,128)(2,1)S(1)}) custom-call(s32[2]{0:T(128)S(1)} %add_convert_fusion.refs_0_, bf16[376,128]{1,0:T(8,128)(2,1)S(1)} %collective-permute-done.2.refs_1_, bf16[376,128]{1,0:T(8,128)(2,1)S(1)} %collective-permute-done.3.refs_2_, ...), custom_call_target="tpu_custom_call" | custom-call | tf_op jit(solution)/shard_map/pallas_call | solution.py:440
  29.9 1.9 %collective-permute-start.6 = (bf16[5,72,128]{2,1,0:T(8,128)(2,1)S(1)}, bf16[5,72,128]{2,1,0:T(8,128)(2,1)S(1)}, u32[]{:S(2)}, u32[]{:S(2)}) collective-permute-start(bf16[5,72,128]{2,1,0:T(8,128)(2,1)S(1)} %get-tuple-element.93), channel_id=1, source_target_pairs={{0,4},{1,5},{2,6},{3,7},{4,8},{5,9},{6,10},{7,11},{8,12},{9,13},{1... | collective-permute-start | bytes 276488 | tf_op jit(solution)/shard_map/ppermute | solution.py:462
  31.8 0.0 collective-permute-done.7.refs_3_
  31.8 0.0 collective-permute-done.8.refs_4_
  31.8 2.7 %shard_map.98 = (f32[5,56,128]{2,1,0:T(8,128)S(1)}, bf16[5,56,128]{2,1,0:T(8,128)(2,1)S(1)}) custom-call(s32[2]{0:T(128)S(1)} %add_convert_fusion.refs_0_, bf16[376,128]{1,0:T(8,128)(2,1)S(1)} %collective-permute-done.2.refs_1_, bf16[376,128]{1,0:T(8,128)(2,1)S(1)} %collective-permute-done.3.refs_2_, bf16[232,128]{1,0:T(8,128)(2,1)S(1)} %collective-permute-done.7.refs_3_, ...), custom_call_target="tpu_custom_call" | custom-call | tf_op jit(solution)/shard_map/pallas_call | solution.py:440
  34.5 0.1 collective-permute-start.9
  34.6 3.7 %collective-permute-done.9.refs_2_ = bf16[5,56,128]{2,1,0:T(8,128)(2,1)S(1)} collective-permute-done((bf16[5,56,128]{2,1,0:T(8,128)(2,1)S(1)}, bf16[5,56,128]{2,1,0:T(8,128)(2,1)S(1)}, u32[]{:S(2)}, u32[]{:S(2)}) %collective-permute-start.9) | collective-permute-done | bytes 71712 | tf_op jit(solution)/shard_map/ppermute | solution.py:462
  38.3 0.0 collective-permute-done.6.refs_1_
  38.3 1.9 %shard_map.99 = bf16[1,120,8,128]{3,2,1,0:T(8,128)(2,1)} custom-call(s32[2]{0:T(128)S(1)} %add_convert_fusion.refs_0_, bf16[5,72,128]{2,1,0:T(8,128)(2,1)S(1)} %collective-permute-done.6.refs_1_, bf16[5,56,128]{2,1,0:T(8,128)(2,1)S(1)} %collective-permute-done.9.refs_2_, f32[5,72,128]{2,1,0:T(8,128)S(1)} %get-tuple-element.97.refs_3_, ...), custom_call_target="tpu_custom_call" | custom-call | tf_op jit(solution)/shard_map/pallas_call | solution.py:440
Async XLA Ops:
  1.6 10.2 %collective-permute-start.4 = (bf16[6,64,128]{2,1,0:T(8,128)(2,1)S(1)}, bf16[6,64,128]{2,1,0:T(8,128)(2,1)S(1)}, u32[]{:S(2)}, u32[]{:S(2)}) collective-permute-start(bf16[6,64,128]{2,1,0:T(8,128)(2,1)S(1)} %get-tuple-element.64.refs_10_.refs_1_), channel_id=1, source_target_pairs={{0,1},{1,0},{2,3},{3,2},{4,5},{5,4},{6,7},{7,6},{8,9},{9,8},{10,11... | collective-permute-start | bytes 294920 | tf_op jit(solution)/shard_map/ppermute | solution.py:462
  3.2 5.7 %collective-permute-start.1 = (bf16[5,64,128]{2,1,0:T(8,128)(2,1)S(1)}, bf16[5,64,128]{2,1,0:T(8,128)(2,1)S(1)}, u32[]{:S(2)}, u32[]{:S(2)}) collective-permute-start(bf16[5,64,128]{2,1,0:T(8,128)(2,1)S(1)} %get-tuple-element.63.refs_8_.refs_1_), channel_id=1, source_target_pairs={{0,1},{1,0},{2,3},{3,2},{4,5},{5,4},{6,7},{7,6},{8,9},{9,8},{10,11... | collective-permute-start | bytes 245768 | tf_op jit(solution)/shard_map/ppermute | solution.py:462
  3.7 6.6 %collective-permute-start = (bf16[5,64,128]{2,1,0:T(8,128)(2,1)S(1)}, bf16[5,64,128]{2,1,0:T(8,128)(2,1)S(1)}, u32[]{:S(2)}, u32[]{:S(2)}) collective-permute-start(bf16[5,64,128]{2,1,0:T(8,128)(2,1)S(1)} %get-tuple-element.53.refs_9_.refs_1_), channel_id=1, source_target_pairs={{0,1},{1,0},{2,3},{3,2},{4,5},{5,4},{6,7},{7,6},{8,9},{9,8},{10,11... | collective-permute-start | bytes 245768 | tf_op jit(solution)/shard_map/ppermute | solution.py:462
  13.4 4.6 %collective-permute-start.5 = (bf16[5,128,128]{2,1,0:T(8,128)(2,1)S(1)}, bf16[5,128,128]{2,1,0:T(8,128)(2,1)S(1)}, u32[]{:S(2)}, u32[]{:S(2)}) collective-permute-start(bf16[5,128,128]{2,1,0:T(8,128)(2,1)S(1)} %get-tuple-element.80), channel_id=1, source_target_pairs={{0,12},{1,13},{2,14},{3,15},{4,0},{5,1},{6,2},{7,3},{8,4},{9,5},{1... | collective-permute-start | bytes 491528 | tf_op jit(solution)/shard_map/ppermute | solution.py:462
  13.4 12.4 %collective-permute-start.2 = (bf16[376,128]{1,0:T(8,128)(2,1)S(1)}, bf16[376,128]{1,0:T(8,128)(2,1)S(1)}, u32[]{:S(2)}, u32[]{:S(2)}) collective-permute-start(bf16[376,128]{1,0:T(8,128)(2,1)S(1)} %get-tuple-element.75), channel_id=1, source_target_pairs={{0,3},{1,2},{2,1},{3,0},{4,7},{5,6},{6,5},{7,4},{8,11},{9,10},{10,... | collective-permute-start | bytes 288776 | tf_op jit(solution)/shard_map/ppermute | solution.py:462
  13.9 12.9 %collective-permute-start.3 = (bf16[376,128]{1,0:T(8,128)(2,1)S(1)}, bf16[376,128]{1,0:T(8,128)(2,1)S(1)}, u32[]{:S(2)}, u32[]{:S(2)}) collective-permute-start(bf16[376,128]{1,0:T(8,128)(2,1)S(1)} %get-tuple-element.76), channel_id=1, source_target_pairs={{0,15},{1,14},{2,13},{3,12},{4,3},{5,2},{6,1},{7,0},{8,7},{9,6},{1... | collective-permute-start | bytes 288776 | tf_op jit(solution)/shard_map/ppermute | solution.py:462
  16.2 15.5 %collective-permute-start.7 = (bf16[232,128]{1,0:T(8,128)(2,1)S(1)}, bf16[232,128]{1,0:T(8,128)(2,1)S(1)}, u32[]{:S(2)}, u32[]{:S(2)}) collective-permute-start(bf16[232,128]{1,0:T(8,128)(2,1)S(1)} %get-tuple-element.94), channel_id=1, source_target_pairs={{0,3},{1,2},{2,1},{3,0},{4,7},{5,6},{6,5},{7,4},{8,11},{9,10},{10,... | collective-permute-start | bytes 178184 | tf_op jit(solution)/shard_map/ppermute | solution.py:462
  16.6 15.2 %collective-permute-start.8 = (bf16[232,128]{1,0:T(8,128)(2,1)S(1)}, bf16[232,128]{1,0:T(8,128)(2,1)S(1)}, u32[]{:S(2)}, u32[]{:S(2)}) collective-permute-start(bf16[232,128]{1,0:T(8,128)(2,1)S(1)} %get-tuple-element.95), channel_id=1, source_target_pairs={{0,15},{1,14},{2,13},{3,12},{4,3},{5,2},{6,1},{7,0},{8,7},{9,6},{1... | collective-permute-start | bytes 178184 | tf_op jit(solution)/shard_map/ppermute | solution.py:462
  29.9 8.4 %collective-permute-start.6 = (bf16[5,72,128]{2,1,0:T(8,128)(2,1)S(1)}, bf16[5,72,128]{2,1,0:T(8,128)(2,1)S(1)}, u32[]{:S(2)}, u32[]{:S(2)}) collective-permute-start(bf16[5,72,128]{2,1,0:T(8,128)(2,1)S(1)} %get-tuple-element.93), channel_id=1, source_target_pairs={{0,4},{1,5},{2,6},{3,7},{4,8},{5,9},{6,10},{7,11},{8,12},{9,13},{1... | collective-permute-start | bytes 276488 | tf_op jit(solution)/shard_map/ppermute | solution.py:462
  34.5 3.8 %collective-permute-start.9 = (bf16[5,56,128]{2,1,0:T(8,128)(2,1)S(1)}, bf16[5,56,128]{2,1,0:T(8,128)(2,1)S(1)}, u32[]{:S(2)}, u32[]{:S(2)}) collective-permute-start(bf16[5,56,128]{2,1,0:T(8,128)(2,1)S(1)} %get-tuple-element.96), channel_id=1, source_target_pairs={{0,4},{1,5},{2,6},{3,7},{4,8},{5,9},{6,10},{7,11},{8,12},{9,13},{1... | collective-permute-start | bytes 215048 | tf_op jit(solution)/shard_map/ppermute | solution.py:462

commit v4 on v3

--- a/solution.py
+++ b/solution.py
@@ -206,12 +206,6 @@
         emit(at, fed.reshape(n, size, LANES))
 
     pipeline([fetch, scores, attend, merge, widen, narrow], len(cuts))
-
-
-def conv_rows(x, shift, origin, edge, wc, bias):
-    cols = x.shape[1]
-    taps = [pltpu.roll(x, (shift + 1 - b) % cols, 1) if (shift + 1 - b) % cols else x for b in range(3)]
-    return conv_taps(taps, origin, cols, edge, wc, bias)
 
 
 def conv_cols(x, skip, origin, cols, edge, wc, bias):
@@ -401,15 +395,46 @@
     o_send[...] = buf[rows - keep :].astype(BF)
 
 
-def final_body(channels, ends, high_a, high_b, own_a, own_b, wc, bias, o_hbm, out, sems):
-    first, last = ends[1] == 1, ends[0] == 1
+def lines_of(x, shift):
+    cols = x.shape[1]
+    col = lax.broadcasted_iota(jnp.int32, (cols, 1), 0)
+    taps = [pltpu.roll(x, shift + 1 - b, 1) for b in range(3)]
+    edges = (jnp.where(col == 0, 0.0, taps[0]), taps[1], jnp.where(col == cols - 1, 0.0, taps[2]))
+    packed = [jnp.concatenate([t[r] for t in edges], axis=1).astype(BF) for r in range(x.shape[0])]
+    return packed, taps[1]
+
+
+def split_dot(lhs, rhs):
+    mid = lhs.shape[1] // 256 * 128
+    return dot(lhs[:, :mid], rhs[:mid, :]) + dot(lhs[:, mid:], rhs[mid:, :])
+
+
+def settle_body(channels, ends, own_a, own_b, wc, bias, o_first, o_rest):
+    own = jnp.concatenate([own_a[...], own_b[...]], axis=1)
+    low = jnp.where(ends[0] == 1, 0.0, own[-1:])
+    packed, center = lines_of(jnp.concatenate([own[:-1], low], axis=0), WIN // 2)
+    early = dot(jnp.concatenate(packed[:3], axis=1), wc[3 * LANES :, :])
+    late = dot(jnp.concatenate(packed[1:], axis=1), wc[...])
+    parts = [early[:, :LANES], early[:, LANES:], late[:, :LANES], late[:, LANES:]]
+    rows = [center[r] + bias[...] + part for r, part in enumerate(parts)]
+    o_first[...] = rows[0]
+    for r in range(1, 4):
+        o_rest[r - 1] = rows[r].T
+
+
+def final_body(channels, ends, high_a, high_b, own_a, own_b, first_row, rest, wc, bias, o_hbm, out, sems):
     high = jnp.concatenate([high_a[...], high_b[...]], axis=1).astype(F32)
-    own = jnp.concatenate([own_a[...], own_b[...]], axis=1)
-    top = jnp.where(first, 0.0, high[:1])
-    low = jnp.where(last, 0.0, own[-1:])
-    x = jnp.concatenate([top, high[1:], own[:-1], low], axis=0)
-    y = conv_rows(x, WIN // 2, 0, None, wc, bias)
-    y = jnp.stack([y[r].T for r in range(y.shape[0])], axis=0)
+    own = jnp.concatenate([own_a[:1], own_b[:1]], axis=1)
+    top = jnp.where(ends[1] == 1, 0.0, high[:1])
+    packed, center = lines_of(jnp.concatenate([top, high[1:], own], axis=0), WIN // 2)
+    width = center.shape[1]
+    both = split_dot(jnp.concatenate([jnp.concatenate(packed[i : i + 4], axis=1) for i in (0, 2)], axis=0), wc[...])
+    rows = []
+    for r in range(4):
+        j, v = divmod(r, 2)
+        rows.append(center[1 + r] + bias[...] + both[j * width : (j + 1) * width, v * LANES : (v + 1) * LANES])
+    rows.append(first_row[...] + dot(packed[4], wc[: 3 * LANES, :LANES]))
+    y = jnp.stack([row.T for row in rows] + [rest[r] for r in range(3)], axis=0)
     copies = []
     n = sems.shape[0]
     step = channels // n
@@ -474,7 +499,7 @@
     keep = rows // 2 + 1
     size = rows * WIN
     dma = pltpu.SemaphoreType.DMA
-    parts = [-(-first // 2), first // 2, rest]
+    parts = [-(-first // 2) + 1, first // 2 - 1, rest]
     x, *xs = call(
         bind(norm_body),
         [((count, size, LANES), F32)] + [((n, size, LANES), BF) for n in parts] + [(p.shape, p.dtype) for p in params],
@@ -543,7 +568,11 @@
         ends, far_high_a, far_low_a, far_high_b, far_low_b, xn, x, q, k, *inner, scratch=[buf(count - half)], scalars=1,
     )
     above_b = send(send_b, lambda t, f: ((t + 1) % tiles, f))
-    (out,) = call(bind(final_body), [((1, channels, rows, cols), BF)], ends, above_a, above_b, own_a, own_b, wc[1], bias[1],
+    first_row, rest = call(
+        bind(settle_body), [((cols, LANES), F32), ((rows // 2 - 1, LANES, cols), F32)],
+        ends, own_a, own_b, wc[1], bias[1], scalars=1,
+    )
+    (out,) = call(bind(final_body), [((1, channels, rows, cols), BF)], ends, above_a, above_b, own_a, own_b, first_row, rest, wc[1], bias[1],
         scratch=[pltpu.VMEM(frames.shape, BF), dma((5,))], scalars=1, away=True,
     )
     return out

time: 40.4 us -> 41.6 us (1.030)
  Pallas kernels: 16.3 us -> 17.2 us
  waiting for transfers between devices: 13.5 us -> 14.1 us
    pallas_call x9 -> x10, Pallas kernels: 16.3 us -> 17.2 us  [call(): return run(*args)]
    ppermute x10, waiting for transfers between devices: 13.5 us -> 14.1 us  [send(): return lax.ppermute(x, axes, pairs)]
  transfers between devices with their start and end apart: 10 -> 10, of which waited for: 4 -> 5; matrix products, arithmetic and copies ran while one was open for 0% -> 0% of each run, Pallas kernels for 28% -> 30%
where the time goes in v4:
time: 41.6 us; the launch traced here: 41.5 us
  Pallas kernels  17.2 us (41%)
  waiting for transfers between devices  14.1 us (34%)
  starting transfers between devices  10 us (24%)
    pallas_call x10, Pallas kernels, call(): return run(*args)  17.2 us
    ppermute x10, waiting for transfers between devices, send(): return lax.ppermute(x, axes, pairs)  14.1 us
    ppermute x10, starting transfers between devices, send(): return lax.ppermute(x, axes, pairs)  10 us
  transfers between devices with their start and end apart: 10, of which 5 were waited for; matrix products, arithmetic and copies ran while one was open for 0% of the time, Pallas kernels for 30%

profile of v4, /device:TPU:16, one launch (start us, length us, event | category | flops | bytes accessed | tf_op | source)
XLA Modules:
  0.0 41.5 jit_solution(11229260639939199314)
XLA Ops:
  0.0 1.6 %shard_map.91 = (f32[16,64,128]{2,1,0:T(8,128)S(1)}, bf16[6,64,128]{2,1,0:T(8,128)(2,1)S(1)}, bf16[4,64,128]{2,1,0:T(8,128)(2,1)S(1)}, bf16[6,64,128]{2,1,0:T(8,...) custom-call(bf16[1,120,8,128]{3,2,1,0:T(8,128)(2,1)} %refs_0_.1, ...), custom_call_target="tpu_custom_call" | custom-call | tf_op jit(solution)/shard_map/pallas_call | solution.py:465
  1.6 1.6 %collective-permute-start.1 = (bf16[6,64,128]{2,1,0:T(8,128)(2,1)S(1)}, bf16[6,64,128]{2,1,0:T(8,128)(2,1)S(1)}, u32[]{:S(2)}, u32[]{:S(2)}) collective-permute-start(bf16[6,64,128]{2,1,0:T(8,128)(2,1)S(1)} %get-tuple-element.65.refs_8_.refs_1_), channel_id=1, source_target_pairs={{0,1},{1,0},{2,3},{3,2},{4,5},{5,4},{6,7},{7,6},{8,9},{9,8},{10,11... | collective-permute-start | bytes 294920 | tf_op jit(solution)/shard_map/ppermute | solution.py:487
  3.2 0.4 %collective-permute-start.4 = (bf16[6,64,128]{2,1,0:T(8,128)(2,1)S(1)}, bf16[6,64,128]{2,1,0:T(8,128)(2,1)S(1)}, u32[]{:S(2)}, u32[]{:S(2)}) collective-permute-start(bf16[6,64,128]{2,1,0:T(8,128)(2,1)S(1)} %get-tuple-element.66.refs_10_.refs_1_), channel_id=1, source_target_pairs={{0,1},{1,0},{2,3},{3,2},{4,5},{5,4},{6,7},{7,6},{8,9},{9,8},{10,11... | collective-permute-start | bytes 294920 | tf_op jit(solution)/shard_map/ppermute | solution.py:487
  3.7 1.6 %collective-permute-start = (bf16[4,64,128]{2,1,0:T(8,128)(2,1)S(1)}, bf16[4,64,128]{2,1,0:T(8,128)(2,1)S(1)}, u32[]{:S(2)}, u32[]{:S(2)}) collective-permute-start(bf16[4,64,128]{2,1,0:T(8,128)(2,1)S(1)} %get-tuple-element.55.refs_9_.refs_1_), channel_id=1, source_target_pairs={{0,1},{1,0},{2,3},{3,2},{4,5},{5,4},{6,7},{7,6},{8,9},{9,8},{10,11... | collective-permute-start | bytes 196616 | tf_op jit(solution)/shard_map/ppermute | solution.py:487
  5.2 0.6 %shard_map.92 = (bf16[16,64,128]{2,1,0:T(8,128)(2,1)S(1)}, bf16[16,64,128]{2,1,0:T(8,128)(2,1)S(1)}, f32[2,128]{1,0:T(2,128)S(1)}, bf16[128,256]{1,0:T(8,128)(2,...) custom-call(f32[2,2,120]{2,1,0:T(2,128)S(1)} %get-tuple-element.57.r, ...), custom_call_target="tpu_custom_call" | custom-call | tf_op jit(solution)/shard_map/pallas_call | solution.py:465
  5.9 1.3 %collective-permute-done.1.refs_0_ = bf16[6,64,128]{2,1,0:T(8,128)(2,1)S(1)} collective-permute-done((bf16[6,64,128]{2,1,0:T(8,128)(2,1)S(1)}, bf16[6,64,128]{2,1,0:T(8,128)(2,1)S(1)}, u32[]{:S(2)}, u32[]{:S(2)}) %collective-permute-start.1) | collective-permute-done | bytes 98336 | tf_op jit(solution)/shard_map/ppermute | solution.py:487
  7.2 1.5 %shard_map.93 = (f32[5,48,128]{2,1,0:T(8,128)S(1)}, bf16[5,48,128]{2,1,0:T(8,128)(2,1)S(1)}) custom-call(bf16[6,64,128]{2,1,0:T(8,128)(2,1)S(1)} %collective-permute-done.1.refs_0_, bf16[6,64,128]{2,1,0:T(8,128)(2,1)S(1)} %get-tuple-element.65.refs_8_.refs_1_, f32[16,64,128]{2,1,0:T(8,128)S(1)} %get-tuple-element.56.refs_2_, ...), custom_call_target="tpu_custom_call" | custom-call | tf_op jit(solution)/shard_map/pallas_call | solution.py:465
  8.6 1.2 %collective-permute-done.refs_0_ = bf16[4,64,128]{2,1,0:T(8,128)(2,1)S(1)} collective-permute-done((bf16[4,64,128]{2,1,0:T(8,128)(2,1)S(1)}, bf16[4,64,128]{2,1,0:T(8,128)(2,1)S(1)}, u32[]{:S(2)}, u32[]{:S(2)}) %collective-permute-start) | collective-permute-done | bytes 65568 | tf_op jit(solution)/shard_map/ppermute | solution.py:487
  9.8 1.4 %shard_map.94 = (f32[5,80,128]{2,1,0:T(8,128)S(1)}, bf16[5,80,128]{2,1,0:T(8,128)(2,1)S(1)}, bf16[376,128]{1,0:T(8,128)(2,1)S(1)}, bf16[376,128]{1,0:T(8,128)(2,1)S(1)}) custom-call(bf16[4,64,128]{2,1,0:T(8,128)(2,1)S(1)} %collective-permute-done.refs_0_, bf16[4,64,128]{2,1,0:T(8,128)(2,1)S(1)} %get-tuple-element.55.refs_9_.refs_1_, ...), custom_call_target="tpu_custom_call" | custom-call | tf_op jit(solution)/shard_map/pallas_call | solution.py:465
  11.2 0.0 collective-permute-done.4.refs_0_
  11.2 1.6 %shard_map.95 = (f32[5,48,128]{2,1,0:T(8,128)S(1)}, bf16[232,128]{1,0:T(8,128)(2,1)S(1)}, bf16[232,128]{1,0:T(8,128)(2,1)S(1)}, bf16[5,128,128]{2,1,0:T(8,128)(2,1)S(1)}) custom-call(bf16[6,64,128]{2,1,0:T(8,128)(2,1)S(1)} %collective-permute-done.4.refs_0_, bf16[6,64,128]{2,1,0:T(8,128)(2,1)S(1)} %get-tuple-element.66.refs_10_.refs_1_, ...), custom_call_target="tpu_custom_call" | custom-call | tf_op jit(solution)/shard_map/pallas_call | solution.py:465
  12.8 0.4 collective-permute-start.5
  13.1 0.1 collective-permute-start.7
  13.3 2.3 %collective-permute-start.8 = (bf16[232,128]{1,0:T(8,128)(2,1)S(1)}, bf16[232,128]{1,0:T(8,128)(2,1)S(1)}, u32[]{:S(2)}, u32[]{:S(2)}) collective-permute-start(bf16[232,128]{1,0:T(8,128)(2,1)S(1)} %get-tuple-element.97), channel_id=1, source_target_pairs={{0,15},{1,14},{2,13},{3,12},{4,3},{5,2},{6,1},{7,0},{8,7},{9,6},{1... | collective-permute-start | bytes 178184 | tf_op jit(solution)/shard_map/ppermute | solution.py:487
  15.6 0.4 collective-permute-start.2
  16.0 1.4 %collective-permute-start.3 = (bf16[376,128]{1,0:T(8,128)(2,1)S(1)}, bf16[376,128]{1,0:T(8,128)(2,1)S(1)}, u32[]{:S(2)}, u32[]{:S(2)}) collective-permute-start(bf16[376,128]{1,0:T(8,128)(2,1)S(1)} %get-tuple-element.78), channel_id=1, source_target_pairs={{0,15},{1,14},{2,13},{3,12},{4,3},{5,2},{6,1},{7,0},{8,7},{9,6},{1... | collective-permute-start | bytes 288776 | tf_op jit(solution)/shard_map/ppermute | solution.py:487
  17.3 0.1 add_convert_fusion.refs_0_
  17.4 0.0 collective-permute-done.5.refs_3_
  17.4 2.0 %shard_map.96 = (f32[16,64,128]{2,1,0:T(8,128)S(1)}, bf16[16,64,128]{2,1,0:T(8,128)(2,1)S(1)}, bf16[16,64,128]{2,1,0:T(8,128)(2,1)S(1)}, bf16[16,64,128]{2,1,0:T(8,128)(2,1)S(1)}) custom-call(s32[2]{0:T(128)S(1)} %add_convert_fusion.refs_0_, f32[5,80,128]{2,1,0:T(8,128)S(1)} %get-tuple-element.79.refs_1_, f32[5,48,128]{2,1,0:T(8,128)S(1)} %get-tuple-element.81.refs_2_, ...), custom_call_target="tpu_custom_call" | custom-call | tf_op jit(solution)/shard_map/pallas_call | solution.py:465
  19.4 8.4 %collective-permute-done.2.refs_1_ = bf16[376,128]{1,0:T(8,128)(2,1)S(1)} collective-permute-done((bf16[376,128]{1,0:T(8,128)(2,1)S(1)}, bf16[376,128]{1,0:T(8,128)(2,1)S(1)}, u32[]{:S(2)}, u32[]{:S(2)}) %collective-permute-start.2) | collective-permute-done | bytes 96288 | tf_op jit(solution)/shard_map/ppermute | solution.py:487
  27.8 0.8 %collective-permute-done.3.refs_2_ = bf16[376,128]{1,0:T(8,128)(2,1)S(1)} collective-permute-done((bf16[376,128]{1,0:T(8,128)(2,1)S(1)}, bf16[376,128]{1,0:T(8,128)(2,1)S(1)}, u32[]{:S(2)}, u32[]{:S(2)}) %collective-permute-start.3) | collective-permute-done | bytes 96288 | tf_op jit(solution)/shard_map/ppermute | solution.py:487
  28.6 3.1 %shard_map.97 = (f32[5,72,128]{2,1,0:T(8,128)S(1)}, bf16[5,72,128]{2,1,0:T(8,128)(2,1)S(1)}) custom-call(s32[2]{0:T(128)S(1)} %add_convert_fusion.refs_0_, bf16[376,128]{1,0:T(8,128)(2,1)S(1)} %collective-permute-done.2.refs_1_, bf16[376,128]{1,0:T(8,128)(2,1)S(1)} %collective-permute-done.3.refs_2_, ...), custom_call_target="tpu_custom_call" | custom-call | tf_op jit(solution)/shard_map/pallas_call | solution.py:465
  31.7 1.4 %collective-permute-start.6 = (bf16[5,72,128]{2,1,0:T(8,128)(2,1)S(1)}, bf16[5,72,128]{2,1,0:T(8,128)(2,1)S(1)}, u32[]{:S(2)}, u32[]{:S(2)}) collective-permute-start(bf16[5,72,128]{2,1,0:T(8,128)(2,1)S(1)} %get-tuple-element.95), channel_id=1, source_target_pairs={{0,4},{1,5},{2,6},{3,7},{4,8},{5,9},{6,10},{7,11},{8,12},{9,13},{1... | collective-permute-start | bytes 276488 | tf_op jit(solution)/shard_map/ppermute | solution.py:487
  33.1 0.0 collective-permute-done.7.refs_3_
  33.1 0.0 collective-permute-done.8.refs_4_
  33.2 2.7 %shard_map.98 = (f32[5,56,128]{2,1,0:T(8,128)S(1)}, bf16[5,56,128]{2,1,0:T(8,128)(2,1)S(1)}) custom-call(s32[2]{0:T(128)S(1)} %add_convert_fusion.refs_0_, bf16[376,128]{1,0:T(8,128)(2,1)S(1)} %collective-permute-done.2.refs_1_, bf16[376,128]{1,0:T(8,128)(2,1)S(1)} %collective-permute-done.3.refs_2_, bf16[232,128]{1,0:T(8,128)(2,1)S(1)} %collective-permute-done.7.refs_3_, ...), custom_call_target="tpu_custom_call" | custom-call | tf_op jit(solution)/shard_map/pallas_call | solution.py:465
  35.9 0.4 collective-permute-start.9
  36.2 1.0 %shard_map.99 = (f32[128,128]{1,0:T(8,128)S(1)}, f32[3,128,128]{2,1,0:T(8,128)S(1)}) custom-call(s32[2]{0:T(128)S(1)} %add_convert_fusion.refs_0_, f32[5,72,128]{2,1,0:T(8,128)S(1)} %get-tuple-element.99.refs_1_.refs_3_, f32[5,56,128]{2,1,0:T(8,128)S(1)} %get-tuple-element.100.refs_2_.refs_4_, bf16[1536,256]{1,0:T(8,128)(2,1)S(1)} %get-tuple-element.101.refs_3_.refs_7_, ...), custom_call_target="tpu_custom_call" | custom-call | tf_op jit(solution)/shard_map/pallas_call | solution.py:465
  37.2 2.4 %collective-permute-done.9.refs_2_ = bf16[5,56,128]{2,1,0:T(8,128)(2,1)S(1)} collective-permute-done((bf16[5,56,128]{2,1,0:T(8,128)(2,1)S(1)}, bf16[5,56,128]{2,1,0:T(8,128)(2,1)S(1)}, u32[]{:S(2)}, u32[]{:S(2)}) %collective-permute-start.9) | collective-permute-done | bytes 71712 | tf_op jit(solution)/shard_map/ppermute | solution.py:487
  39.7 0.0 collective-permute-done.6.refs_1_
  39.7 1.8 %shard_map.100 = bf16[1,120,8,128]{3,2,1,0:T(8,128)(2,1)} custom-call(s32[2]{0:T(128)S(1)} %add_convert_fusion.refs_0_, bf16[5,72,128]{2,1,0:T(8,128)(2,1)S(1)} %collective-permute-done.6.refs_1_, bf16[5,56,128]{2,1,0:T(8,128)(2,1)S(1)} %collective-permute-done.9.refs_2_, f32[5,72,128]{2,1,0:T(8,128)S(1)} %get-tuple-element.99.refs_1_.refs_3_, ...), custom_call_target="tpu_custom_call" | custom-call | tf_op jit(solution)/shard_map/pallas_call | solution.py:465
Async XLA Ops:
  1.6 5.6 %collective-permute-start.1 = (bf16[6,64,128]{2,1,0:T(8,128)(2,1)S(1)}, bf16[6,64,128]{2,1,0:T(8,128)(2,1)S(1)}, u32[]{:S(2)}, u32[]{:S(2)}) collective-permute-start(bf16[6,64,128]{2,1,0:T(8,128)(2,1)S(1)} %get-tuple-element.65.refs_8_.refs_1_), channel_id=1, source_target_pairs={{0,1},{1,0},{2,3},{3,2},{4,5},{5,4},{6,7},{7,6},{8,9},{9,8},{10,11... | collective-permute-start | bytes 294920 | tf_op jit(solution)/shard_map/ppermute | solution.py:487
  3.2 8.0 %collective-permute-start.4 = (bf16[6,64,128]{2,1,0:T(8,128)(2,1)S(1)}, bf16[6,64,128]{2,1,0:T(8,128)(2,1)S(1)}, u32[]{:S(2)}, u32[]{:S(2)}) collective-permute-start(bf16[6,64,128]{2,1,0:T(8,128)(2,1)S(1)} %get-tuple-element.66.refs_10_.refs_1_), channel_id=1, source_target_pairs={{0,1},{1,0},{2,3},{3,2},{4,5},{5,4},{6,7},{7,6},{8,9},{9,8},{10,11... | collective-permute-start | bytes 294920 | tf_op jit(solution)/shard_map/ppermute | solution.py:487
  3.7 6.1 %collective-permute-start = (bf16[4,64,128]{2,1,0:T(8,128)(2,1)S(1)}, bf16[4,64,128]{2,1,0:T(8,128)(2,1)S(1)}, u32[]{:S(2)}, u32[]{:S(2)}) collective-permute-start(bf16[4,64,128]{2,1,0:T(8,128)(2,1)S(1)} %get-tuple-element.55.refs_9_.refs_1_), channel_id=1, source_target_pairs={{0,1},{1,0},{2,3},{3,2},{4,5},{5,4},{6,7},{7,6},{8,9},{9,8},{10,11... | collective-permute-start | bytes 196616 | tf_op jit(solution)/shard_map/ppermute | solution.py:487
  12.8 4.6 %collective-permute-start.5 = (bf16[5,128,128]{2,1,0:T(8,128)(2,1)S(1)}, bf16[5,128,128]{2,1,0:T(8,128)(2,1)S(1)}, u32[]{:S(2)}, u32[]{:S(2)}) collective-permute-start(bf16[5,128,128]{2,1,0:T(8,128)(2,1)S(1)} %get-tuple-element.82), channel_id=1, source_target_pairs={{0,12},{1,13},{2,14},{3,15},{4,0},{5,1},{6,2},{7,3},{8,4},{9,5},{1... | collective-permute-start | bytes 491528 | tf_op jit(solution)/shard_map/ppermute | solution.py:487
  13.1 20.0 %collective-permute-start.7 = (bf16[232,128]{1,0:T(8,128)(2,1)S(1)}, bf16[232,128]{1,0:T(8,128)(2,1)S(1)}, u32[]{:S(2)}, u32[]{:S(2)}) collective-permute-start(bf16[232,128]{1,0:T(8,128)(2,1)S(1)} %get-tuple-element.96), channel_id=1, source_target_pairs={{0,3},{1,2},{2,1},{3,0},{4,7},{5,6},{6,5},{7,4},{8,11},{9,10},{10,... | collective-permute-start | bytes 178184 | tf_op jit(solution)/shard_map/ppermute | solution.py:487
  13.3 19.9 %collective-permute-start.8 = (bf16[232,128]{1,0:T(8,128)(2,1)S(1)}, bf16[232,128]{1,0:T(8,128)(2,1)S(1)}, u32[]{:S(2)}, u32[]{:S(2)}) collective-permute-start(bf16[232,128]{1,0:T(8,128)(2,1)S(1)} %get-tuple-element.97), channel_id=1, source_target_pairs={{0,15},{1,14},{2,13},{3,12},{4,3},{5,2},{6,1},{7,0},{8,7},{9,6},{1... | collective-permute-start | bytes 178184 | tf_op jit(solution)/shard_map/ppermute | solution.py:487
  15.6 12.2 %collective-permute-start.2 = (bf16[376,128]{1,0:T(8,128)(2,1)S(1)}, bf16[376,128]{1,0:T(8,128)(2,1)S(1)}, u32[]{:S(2)}, u32[]{:S(2)}) collective-permute-start(bf16[376,128]{1,0:T(8,128)(2,1)S(1)} %get-tuple-element.77), channel_id=1, source_target_pairs={{0,3},{1,2},{2,1},{3,0},{4,7},{5,6},{6,5},{7,4},{8,11},{9,10},{10,... | collective-permute-start | bytes 288776 | tf_op jit(solution)/shard_map/ppermute | solution.py:487
  16.0 12.7 %collective-permute-start.3 = (bf16[376,128]{1,0:T(8,128)(2,1)S(1)}, bf16[376,128]{1,0:T(8,128)(2,1)S(1)}, u32[]{:S(2)}, u32[]{:S(2)}) collective-permute-start(bf16[376,128]{1,0:T(8,128)(2,1)S(1)} %get-tuple-element.78), channel_id=1, source_target_pairs={{0,15},{1,14},{2,13},{3,12},{4,3},{5,2},{6,1},{7,0},{8,7},{9,6},{1... | collective-permute-start | bytes 288776 | tf_op jit(solution)/shard_map/ppermute | solution.py:487
  31.7 8.0 %collective-permute-start.6 = (bf16[5,72,128]{2,1,0:T(8,128)(2,1)S(1)}, bf16[5,72,128]{2,1,0:T(8,128)(2,1)S(1)}, u32[]{:S(2)}, u32[]{:S(2)}) collective-permute-start(bf16[5,72,128]{2,1,0:T(8,128)(2,1)S(1)} %get-tuple-element.95), channel_id=1, source_target_pairs={{0,4},{1,5},{2,6},{3,7},{4,8},{5,9},{6,10},{7,11},{8,12},{9,13},{1... | collective-permute-start | bytes 276488 | tf_op jit(solution)/shard_map/ppermute | solution.py:487
  35.9 3.8 %collective-permute-start.9 = (bf16[5,56,128]{2,1,0:T(8,128)(2,1)S(1)}, bf16[5,56,128]{2,1,0:T(8,128)(2,1)S(1)}, u32[]{:S(2)}, u32[]{:S(2)}) collective-permute-start(bf16[5,56,128]{2,1,0:T(8,128)(2,1)S(1)} %get-tuple-element.98), channel_id=1, source_target_pairs={{0,4},{1,5},{2,6},{3,7},{4,8},{5,9},{6,10},{7,11},{8,12},{9,13},{1... | collective-permute-start | bytes 215048 | tf_op jit(solution)/shard_map/ppermute | solution.py:487

commit v5 on v4

--- a/solution.py
+++ b/solution.py
@@ -11,7 +11,7 @@
 WIN = 8
 LANES = 128
 GROUP = 12
-LEAD = 2
+LEAD = 3
 BF = jnp.bfloat16
 F32 = jnp.float32
 NT = (((1,), (1,)), ((), ()))
@@ -340,7 +340,7 @@
     o_low[:, first:, :] = low.astype(BF)
 
 
-def own1_body(channels, ends, fed_a, fed_b, low, wc, bias, gain, qk, o_x, o_xn, o_q, o_k):
+def own1_body(channels, last, fed_a, fed_b, low, wc, bias, gain, qk, o_x, o_xn, o_q, o_k):
     high = jnp.concatenate([fed_a[...], fed_b[...]], axis=1)
     x = jnp.concatenate([high, low[...].astype(F32)], axis=0)
     cols = x.shape[1]
@@ -350,7 +350,7 @@
     def mix(g, _):
         at, n = cuts[g]
         part = x[:, at * WIN : (at + n + 1) * WIN]
-        return windows(conv_cols(part, WIN // 2, at * WIN + WIN // 2, cols, (ends[0] == 1, WIN // 2), wc, bias))
+        return windows(conv_cols(part, WIN // 2, at * WIN + WIN // 2, cols, (lax.axis_index("tile") == last, WIN // 2), wc, bias))
 
     def finish(g, part):
         at, n = cuts[g]
@@ -362,26 +362,26 @@
     pipeline([mix, finish], len(cuts))
 
 
-def far_normed(channels, ends, x, base, cols, wc, bias, gain):
+def far_normed(channels, last, x, base, cols, wc, bias, gain):
     def far(at, n):
         part = x[:, at * WIN : (at + n + 1) * WIN]
-        part = conv_cols(part, WIN // 2, base + at * WIN + WIN // 2, cols, (ends[0] == 1, WIN // 2), wc, bias)
+        part = conv_cols(part, WIN // 2, base + at * WIN + WIN // 2, cols, (lax.axis_index("tile") == last, WIN // 2), wc, bias)
         return norm(windows(part), gain[0:1], channels).astype(BF)
 
     return far
 
 
-def layer1_first(channels, ends, high, low, xn_ref, x_ref, q_ref, k_ref, wc, bias, gain0, gain, qk, vt, wo, wgu, wd, o_own, o_send, buf):
+def layer1_first(channels, last, high, low, xn_ref, x_ref, q_ref, k_ref, wc, bias, gain0, gain, qk, vt, wo, wgu, wd, o_own, o_send, buf):
     rows, keep = buf.shape[0], o_own.shape[0]
     x = jnp.concatenate([unpack(high[...], keep, channels), unpack(low[...], keep, channels)], axis=0)
     count = buf.shape[1] // WIN
-    far = far_normed(channels, ends, x, 0, x_ref.shape[0] * WIN, wc, bias, gain)
+    far = far_normed(channels, last, x, 0, x_ref.shape[0] * WIN, wc, bias, gain)
     mutual(channels, 0, count, far, xn_ref, x_ref, q_ref, k_ref, gain, qk, vt, wo, wgu, wd, collect(buf))
     o_own[...] = buf[:keep]
     o_send[...] = buf[rows - keep :].astype(BF)
 
 
-def layer1_second(channels, ends, high_a, low_a, high_b, low_b, xn_ref, x_ref, q_ref, k_ref, wc, bias, gain0, gain, qk, vt, wo, wgu, wd, o_own, o_send, buf):
+def layer1_second(channels, last, high_a, low_a, high_b, low_b, xn_ref, x_ref, q_ref, k_ref, wc, bias, gain0, gain, qk, vt, wo, wgu, wd, o_own, o_send, buf):
     keep = o_own.shape[0]
     xa = jnp.concatenate([unpack(part[...], keep, channels) for part in (high_a, low_a)], axis=0)
     xb = jnp.concatenate([unpack(part[...], keep, channels) for part in (high_b, low_b)], axis=0)
@@ -389,7 +389,7 @@
     base = cols - buf.shape[1]
     x = jnp.concatenate([xa[:, base:], xb, xa[:, :WIN]], axis=1)
     rows, at, count = buf.shape[0], base // WIN, buf.shape[1] // WIN
-    far = far_normed(channels, ends, x, base, cols, wc, bias, gain)
+    far = far_normed(channels, last, x, base, cols, wc, bias, gain)
     mutual(channels, at, count, far, xn_ref.at[at:], x_ref, q_ref, k_ref, gain, qk, vt, wo, wgu, wd, collect(buf))
     o_own[...] = buf[:keep]
     o_send[...] = buf[rows - keep :].astype(BF)
@@ -409,9 +409,9 @@
     return dot(lhs[:, :mid], rhs[:mid, :]) + dot(lhs[:, mid:], rhs[mid:, :])
 
 
-def settle_body(channels, ends, own_a, own_b, wc, bias, o_first, o_rest):
+def settle_body(channels, last, own_a, own_b, wc, bias, o_first, o_rest):
     own = jnp.concatenate([own_a[...], own_b[...]], axis=1)
-    low = jnp.where(ends[0] == 1, 0.0, own[-1:])
+    low = jnp.where(lax.axis_index("tile") == last, 0.0, own[-1:])
     packed, center = lines_of(jnp.concatenate([own[:-1], low], axis=0), WIN // 2)
     early = dot(jnp.concatenate(packed[:3], axis=1), wc[3 * LANES :, :])
     late = dot(jnp.concatenate(packed[1:], axis=1), wc[...])
@@ -422,10 +422,10 @@
         o_rest[r - 1] = rows[r].T
 
 
-def final_body(channels, ends, high_a, high_b, own_a, own_b, first_row, rest, wc, bias, o_hbm, out, sems):
+def final_body(channels, last, high_a, high_b, own_a, own_b, first_row, rest, wc, bias, o_hbm, out, sems):
     high = jnp.concatenate([high_a[...], high_b[...]], axis=1).astype(F32)
     own = jnp.concatenate([own_a[:1], own_b[:1]], axis=1)
-    top = jnp.where(ends[1] == 1, 0.0, high[:1])
+    top = jnp.where(lax.axis_index("tile") == 0, 0.0, high[:1])
     packed, center = lines_of(jnp.concatenate([top, high[1:], own], axis=0), WIN // 2)
     width = center.shape[1]
     both = split_dot(jnp.concatenate([jnp.concatenate(packed[i : i + 4], axis=1) for i in (0, 2)], axis=0), wc[...])
@@ -471,8 +471,7 @@
     layers = ln_gain.shape[0]
     hp = up(gate_weight.shape[2])
     tiles, depth = lax.axis_size("tile"), lax.axis_size("tm")
-    where = lax.axis_index("tile")
-    ends = jnp.stack([where == tiles - 1, where == 0]).astype(jnp.int32)
+    last_tile = tiles - 1
     axes = ("tile", "tm")
 
     def odd(f):
@@ -555,25 +554,25 @@
     far_high_b = send(high_b, lambda t, f: (t, odd(f)))
     far_low_b = send(low_b, lambda t, f: ((t - 1) % tiles, odd(f)))
     whole = (count, size, LANES)
-    x, xn, q, k = call(bind(own1_body), [(whole, F32), (whole, BF), (whole, BF), (whole, BF)],
-        ends, fed_a, fed_b, below, wc[0], bias[0], gain[1], qk[1], scalars=1,
+    x, xn, q, k = call(bind(own1_body, last_tile), [(whole, F32), (whole, BF), (whole, BF), (whole, BF)],
+        fed_a, fed_b, below, wc[0], bias[0], gain[1], qk[1],
     )
     inner = (wc[0], bias[0], gain[0], gain[1], qk[1], vt[1], wo[1], wgu[1], wd[1])
     half = first - 1
-    own_a, send_a = call(bind(layer1_first), [piece(half, F32), piece(half)],
-        ends, far_high_a, far_low_a, xn, x, q, k, *inner, scratch=[buf(half)], scalars=1,
+    own_a, send_a = call(bind(layer1_first, last_tile), [piece(half, F32), piece(half)],
+        far_high_a, far_low_a, xn, x, q, k, *inner, scratch=[buf(half)],
     )
     above_a = send(send_a, lambda t, f: ((t + 1) % tiles, f))
-    own_b, send_b = call(bind(layer1_second), [piece(count - half, F32), piece(count - half)],
-        ends, far_high_a, far_low_a, far_high_b, far_low_b, xn, x, q, k, *inner, scratch=[buf(count - half)], scalars=1,
+    own_b, send_b = call(bind(layer1_second, last_tile), [piece(count - half, F32), piece(count - half)],
+        far_high_a, far_low_a, far_high_b, far_low_b, xn, x, q, k, *inner, scratch=[buf(count - half)],
     )
     above_b = send(send_b, lambda t, f: ((t + 1) % tiles, f))
     first_row, rest = call(
-        bind(settle_body), [((cols, LANES), F32), ((rows // 2 - 1, LANES, cols), F32)],
-        ends, own_a, own_b, wc[1], bias[1], scalars=1,
-    )
-    (out,) = call(bind(final_body), [((1, channels, rows, cols), BF)], ends, above_a, above_b, own_a, own_b, first_row, rest, wc[1], bias[1],
-        scratch=[pltpu.VMEM(frames.shape, BF), dma((5,))], scalars=1, away=True,
+        bind(settle_body, last_tile), [((cols, LANES), F32), ((rows // 2 - 1, LANES, cols), F32)],
+        own_a, own_b, wc[1], bias[1],
+    )
+    (out,) = call(bind(final_body, last_tile), [((1, channels, rows, cols), BF)], above_a, above_b, own_a, own_b, first_row, rest, wc[1], bias[1],
+        scratch=[pltpu.VMEM(frames.shape, BF), dma((5,))], away=True,
     )
     return out
 

time: 41.6 us -> 38.1 us (0.916)
  Pallas kernels: 17.2 us -> 14.5 us
  waiting for transfers between devices: 14.1 us -> 13.2 us
    pallas_call x10, Pallas kernels: 17.2 us -> 14.5 us  [call(): return run(*args)]
    ppermute x10, waiting for transfers between devices: 14.1 us -> 13.2 us  [send(): return lax.ppermute(x, axes, pairs)]
  transfers between devices with their start and end apart: 10 -> 10, of which waited for: 5 -> 5; matrix products, arithmetic and copies ran while one was open for 0% -> 0% of each run, Pallas kernels for 30% -> 27%
where the time goes in v5:
time: 38.1 us; the launch traced here: 38 us
  Pallas kernels  14.5 us (38%)
  waiting for transfers between devices  13.2 us (35%)
  starting transfers between devices  10.2 us (27%)
    pallas_call x10, Pallas kernels, call(): return run(*args)  14.5 us
    ppermute x10, waiting for transfers between devices, send(): return lax.ppermute(x, axes, pairs)  13.2 us
    ppermute x10, starting transfers between devices, send(): return lax.ppermute(x, axes, pairs)  10.2 us
  transfers between devices with their start and end apart: 10, of which 5 were waited for; matrix products, arithmetic and copies ran while one was open for 0% of the time, Pallas kernels for 27%

profile of v5, /device:TPU:16, one launch (start us, length us, event | category | flops | bytes accessed | tf_op | source)
XLA Modules:
  0.0 38.0 jit_solution(16525388077114622571)
XLA Ops:
  0.0 1.6 %shard_map.91 = (f32[16,64,128]{2,1,0:T(8,128)S(1)}, bf16[7,64,128]{2,1,0:T(8,128)(2,1)S(1)}, bf16[4,64,128]{2,1,0:T(8,128)(2,1)S(1)}, bf16[5,64,128]{2,1,0:T(8,...) custom-call(bf16[1,120,8,128]{3,2,1,0:T(8,128)(2,1)} %refs_0_.1, ...), custom_call_target="tpu_custom_call" | custom-call | tf_op jit(solution)/shard_map/pallas_call | solution.py:465
  1.6 1.6 %collective-permute-start.1 = (bf16[7,64,128]{2,1,0:T(8,128)(2,1)S(1)}, bf16[7,64,128]{2,1,0:T(8,128)(2,1)S(1)}, u32[]{:S(2)}, u32[]{:S(2)}) collective-permute-start(bf16[7,64,128]{2,1,0:T(8,128)(2,1)S(1)} %get-tuple-element.65.refs_8_.refs_1_), channel_id=1, source_target_pairs={{0,1},{1,0},{2,3},{3,2},{4,5},{5,4},{6,7},{7,6},{8,9},{9,8},{10,11... | collective-permute-start | bytes 344072 | tf_op jit(solution)/shard_map/ppermute | solution.py:486
  3.2 0.4 %collective-permute-start.4 = (bf16[5,64,128]{2,1,0:T(8,128)(2,1)S(1)}, bf16[5,64,128]{2,1,0:T(8,128)(2,1)S(1)}, u32[]{:S(2)}, u32[]{:S(2)}) collective-permute-start(bf16[5,64,128]{2,1,0:T(8,128)(2,1)S(1)} %get-tuple-element.66.refs_10_.refs_1_), channel_id=1, source_target_pairs={{0,1},{1,0},{2,3},{3,2},{4,5},{5,4},{6,7},{7,6},{8,9},{9,8},{10,11... | collective-permute-start | bytes 245768 | tf_op jit(solution)/shard_map/ppermute | solution.py:486
  3.7 1.6 %collective-permute-start = (bf16[4,64,128]{2,1,0:T(8,128)(2,1)S(1)}, bf16[4,64,128]{2,1,0:T(8,128)(2,1)S(1)}, u32[]{:S(2)}, u32[]{:S(2)}) collective-permute-start(bf16[4,64,128]{2,1,0:T(8,128)(2,1)S(1)} %get-tuple-element.55.refs_9_.refs_1_), channel_id=1, source_target_pairs={{0,1},{1,0},{2,3},{3,2},{4,5},{5,4},{6,7},{7,6},{8,9},{9,8},{10,11... | collective-permute-start | bytes 196616 | tf_op jit(solution)/shard_map/ppermute | solution.py:486
  5.2 0.6 %shard_map.92 = (bf16[16,64,128]{2,1,0:T(8,128)(2,1)S(1)}, bf16[16,64,128]{2,1,0:T(8,128)(2,1)S(1)}, f32[2,128]{1,0:T(2,128)S(1)}, bf16[128,256]{1,0:T(8,128)(2,...) custom-call(f32[2,2,120]{2,1,0:T(2,128)S(1)} %get-tuple-element.57.r, ...), custom_call_target="tpu_custom_call" | custom-call | tf_op jit(solution)/shard_map/pallas_call | solution.py:465
  5.9 1.8 %collective-permute-done.1.refs_0_ = bf16[7,64,128]{2,1,0:T(8,128)(2,1)S(1)} collective-permute-done((bf16[7,64,128]{2,1,0:T(8,128)(2,1)S(1)}, bf16[7,64,128]{2,1,0:T(8,128)(2,1)S(1)}, u32[]{:S(2)}, u32[]{:S(2)}) %collective-permute-start.1) | collective-permute-done | bytes 114720 | tf_op jit(solution)/shard_map/ppermute | solution.py:486
  7.7 1.6 %shard_map.93 = (f32[5,56,128]{2,1,0:T(8,128)S(1)}, bf16[5,56,128]{2,1,0:T(8,128)(2,1)S(1)}) custom-call(bf16[7,64,128]{2,1,0:T(8,128)(2,1)S(1)} %collective-permute-done.1.refs_0_, bf16[7,64,128]{2,1,0:T(8,128)(2,1)S(1)} %get-tuple-element.65.refs_8_.refs_1_, f32[16,64,128]{2,1,0:T(8,128)S(1)} %get-tuple-element.56.refs_2_, ...), custom_call_target="tpu_custom_call" | custom-call | tf_op jit(solution)/shard_map/pallas_call | solution.py:465
  9.3 0.4 %collective-permute-done.refs_0_ = bf16[4,64,128]{2,1,0:T(8,128)(2,1)S(1)} collective-permute-done((bf16[4,64,128]{2,1,0:T(8,128)(2,1)S(1)}, bf16[4,64,128]{2,1,0:T(8,128)(2,1)S(1)}, u32[]{:S(2)}, u32[]{:S(2)}) %collective-permute-start) | collective-permute-done | bytes 65568 | tf_op jit(solution)/shard_map/ppermute | solution.py:486
  9.7 1.4 %shard_map.94 = (f32[5,88,128]{2,1,0:T(8,128)S(1)}, bf16[5,88,128]{2,1,0:T(8,128)(2,1)S(1)}, bf16[416,128]{1,0:T(8,128)(2,1)S(1)}, bf16[416,128]{1,0:T(8,128)(2,1)S(1)}) custom-call(bf16[4,64,128]{2,1,0:T(8,128)(2,1)S(1)} %collective-permute-done.refs_0_, bf16[4,64,128]{2,1,0:T(8,128)(2,1)S(1)} %get-tuple-element.55.refs_9_.refs_1_, ...), custom_call_target="tpu_custom_call" | custom-call | tf_op jit(solution)/shard_map/pallas_call | solution.py:465
  11.1 0.0 collective-permute-done.4.refs_0_
  11.1 1.5 %shard_map.95 = (f32[5,40,128]{2,1,0:T(8,128)S(1)}, bf16[192,128]{1,0:T(8,128)(2,1)S(1)}, bf16[192,128]{1,0:T(8,128)(2,1)S(1)}, bf16[5,128,128]{2,1,0:T(8,128)(2,1)S(1)}) custom-call(bf16[5,64,128]{2,1,0:T(8,128)(2,1)S(1)} %collective-permute-done.4.refs_0_, bf16[5,64,128]{2,1,0:T(8,128)(2,1)S(1)} %get-tuple-element.66.refs_10_.refs_1_, ...), custom_call_target="tpu_custom_call" | custom-call | tf_op jit(solution)/shard_map/pallas_call | solution.py:465
  12.6 0.1 collective-permute-start.5
  12.7 0.5 %collective-permute-start.2 = (bf16[416,128]{1,0:T(8,128)(2,1)S(1)}, bf16[416,128]{1,0:T(8,128)(2,1)S(1)}, u32[]{:S(2)}, u32[]{:S(2)}) collective-permute-start(bf16[416,128]{1,0:T(8,128)(2,1)S(1)} %get-tuple-element.77), channel_id=1, source_target_pairs={{0,3},{1,2},{2,1},{3,0},{4,7},{5,6},{6,5},{7,4},{8,11},{9,10},{10,... | collective-permute-start | bytes 319496 | tf_op jit(solution)/shard_map/ppermute | solution.py:486
  13.2 2.3 %collective-permute-start.3 = (bf16[416,128]{1,0:T(8,128)(2,1)S(1)}, bf16[416,128]{1,0:T(8,128)(2,1)S(1)}, u32[]{:S(2)}, u32[]{:S(2)}) collective-permute-start(bf16[416,128]{1,0:T(8,128)(2,1)S(1)} %get-tuple-element.78), channel_id=1, source_target_pairs={{0,15},{1,14},{2,13},{3,12},{4,3},{5,2},{6,1},{7,0},{8,7},{9,6},{1... | collective-permute-start | bytes 319496 | tf_op jit(solution)/shard_map/ppermute | solution.py:486
  15.4 0.4 %collective-permute-start.7 = (bf16[192,128]{1,0:T(8,128)(2,1)S(1)}, bf16[192,128]{1,0:T(8,128)(2,1)S(1)}, u32[]{:S(2)}, u32[]{:S(2)}) collective-permute-start(bf16[192,128]{1,0:T(8,128)(2,1)S(1)} %get-tuple-element.96), channel_id=1, source_target_pairs={{0,3},{1,2},{2,1},{3,0},{4,7},{5,6},{6,5},{7,4},{8,11},{9,10},{10,... | collective-permute-start | bytes 147464 | tf_op jit(solution)/shard_map/ppermute | solution.py:486
  15.9 1.3 %collective-permute-start.8 = (bf16[192,128]{1,0:T(8,128)(2,1)S(1)}, bf16[192,128]{1,0:T(8,128)(2,1)S(1)}, u32[]{:S(2)}, u32[]{:S(2)}) collective-permute-start(bf16[192,128]{1,0:T(8,128)(2,1)S(1)} %get-tuple-element.97), channel_id=1, source_target_pairs={{0,15},{1,14},{2,13},{3,12},{4,3},{5,2},{6,1},{7,0},{8,7},{9,6},{1... | collective-permute-start | bytes 147464 | tf_op jit(solution)/shard_map/ppermute | solution.py:486
  17.1 0.0 collective-permute-done.5.refs_2_
  17.2 1.5 %shard_map.96 = (f32[16,64,128]{2,1,0:T(8,128)S(1)}, bf16[16,64,128]{2,1,0:T(8,128)(2,1)S(1)}, bf16[16,64,128]{2,1,0:T(8,128)(2,1)S(1)}, bf16[16,64,128]{2,1,0:T(8,128)(2,1)S(1)}) custom-call(f32[5,88,128]{2,1,0:T(8,128)S(1)} %get-tuple-element.79.refs_0_, f32[5,40,128]{2,1,0:T(8,128)S(1)} %get-tuple-element.81.refs_1_, ...), custom_call_target="tpu_custom_call" | custom-call | tf_op jit(solution)/shard_map/pallas_call | solution.py:465
  18.6 6.6 %collective-permute-done.2.refs_0_ = bf16[416,128]{1,0:T(8,128)(2,1)S(1)} collective-permute-done((bf16[416,128]{1,0:T(8,128)(2,1)S(1)}, bf16[416,128]{1,0:T(8,128)(2,1)S(1)}, u32[]{:S(2)}, u32[]{:S(2)}) %collective-permute-start.2) | collective-permute-done | bytes 106528 | tf_op jit(solution)/shard_map/ppermute | solution.py:486
  25.2 1.2 %collective-permute-done.3.refs_1_ = bf16[416,128]{1,0:T(8,128)(2,1)S(1)} collective-permute-done((bf16[416,128]{1,0:T(8,128)(2,1)S(1)}, bf16[416,128]{1,0:T(8,128)(2,1)S(1)}, u32[]{:S(2)}, u32[]{:S(2)}) %collective-permute-start.3) | collective-permute-done | bytes 106528 | tf_op jit(solution)/shard_map/ppermute | solution.py:486
  26.4 2.6 %shard_map.97 = (f32[5,80,128]{2,1,0:T(8,128)S(1)}, bf16[5,80,128]{2,1,0:T(8,128)(2,1)S(1)}) custom-call(bf16[416,128]{1,0:T(8,128)(2,1)S(1)} %collective-permute-done.2.refs_0_, bf16[416,128]{1,0:T(8,128)(2,1)S(1)} %collective-permute-done.3.refs_1_, bf16[16,64,128]{2,1,0:T(8,128)(2,1)S(1)} %get-tuple-element.87.refs_2_.refs_4_, ...), custom_call_target="tpu_custom_call" | custom-call | tf_op jit(solution)/shard_map/pallas_call | solution.py:465
  29.0 1.9 %collective-permute-start.6 = (bf16[5,80,128]{2,1,0:T(8,128)(2,1)S(1)}, bf16[5,80,128]{2,1,0:T(8,128)(2,1)S(1)}, u32[]{:S(2)}, u32[]{:S(2)}) collective-permute-start(bf16[5,80,128]{2,1,0:T(8,128)(2,1)S(1)} %get-tuple-element.95), channel_id=1, source_target_pairs={{0,4},{1,5},{2,6},{3,7},{4,8},{5,9},{6,10},{7,11},{8,12},{9,13},{1... | collective-permute-start | bytes 307208 | tf_op jit(solution)/shard_map/ppermute | solution.py:486
  30.9 0.0 collective-permute-done.7.refs_2_
  30.9 0.0 collective-permute-done.8.refs_3_
  30.9 2.1 %shard_map.98 = (f32[5,48,128]{2,1,0:T(8,128)S(1)}, bf16[5,48,128]{2,1,0:T(8,128)(2,1)S(1)}) custom-call(bf16[416,128]{1,0:T(8,128)(2,1)S(1)} %collective-permute-done.2.refs_0_, bf16[416,128]{1,0:T(8,128)(2,1)S(1)} %collective-permute-done.3.refs_1_, bf16[192,128]{1,0:T(8,128)(2,1)S(1)} %collective-permute-done.7.refs_2_, ...), custom_call_target="tpu_custom_call" | custom-call | tf_op jit(solution)/shard_map/pallas_call | solution.py:465
  33.1 0.1 collective-permute-start.9
  33.1 0.5 %shard_map.99 = (f32[128,128]{1,0:T(8,128)S(1)}, f32[3,128,128]{2,1,0:T(8,128)S(1)}) custom-call(f32[5,80,128]{2,1,0:T(8,128)S(1)} %get-tuple-element.99.refs_0_.refs_2_, f32[5,48,128]{2,1,0:T(8,128)S(1)} %get-tuple-element.100.refs_1_.refs_3_, bf16[1536,256]{1,0:T(8,128)(2,1)S(1)} %get-tuple-element.101.refs_2_.refs_6_, ...), custom_call_target="tpu_custom_call" | custom-call | tf_op jit(solution)/shard_map/pallas_call | solution.py:465
  33.6 3.2 %collective-permute-done.9.refs_1_ = bf16[5,48,128]{2,1,0:T(8,128)(2,1)S(1)} collective-permute-done((bf16[5,48,128]{2,1,0:T(8,128)(2,1)S(1)}, bf16[5,48,128]{2,1,0:T(8,128)(2,1)S(1)}, u32[]{:S(2)}, u32[]{:S(2)}) %collective-permute-start.9) | collective-permute-done | bytes 61472 | tf_op jit(solution)/shard_map/ppermute | solution.py:486
  36.8 0.0 collective-permute-done.6.refs_0_
  36.8 1.2 %shard_map.100 = bf16[1,120,8,128]{3,2,1,0:T(8,128)(2,1)} custom-call(bf16[5,80,128]{2,1,0:T(8,128)(2,1)S(1)} %collective-permute-done.6.refs_0_, bf16[5,48,128]{2,1,0:T(8,128)(2,1)S(1)} %collective-permute-done.9.refs_1_, f32[5,80,128]{2,1,0:T(8,128)S(1)} %get-tuple-element.99.refs_0_.refs_2_, f32[5,48,128]{2,1,0:T(8,128)S(1)} %get-tuple-element.100.refs_1_.refs_3_, ...), custom_call_target="tpu_custom_call" | custom-call | tf_op jit(solution)/shard_map/pallas_call | solution.py:465
Async XLA Ops:
  1.6 6.1 %collective-permute-start.1 = (bf16[7,64,128]{2,1,0:T(8,128)(2,1)S(1)}, bf16[7,64,128]{2,1,0:T(8,128)(2,1)S(1)}, u32[]{:S(2)}, u32[]{:S(2)}) collective-permute-start(bf16[7,64,128]{2,1,0:T(8,128)(2,1)S(1)} %get-tuple-element.65.refs_8_.refs_1_), channel_id=1, source_target_pairs={{0,1},{1,0},{2,3},{3,2},{4,5},{5,4},{6,7},{7,6},{8,9},{9,8},{10,11... | collective-permute-start | bytes 344072 | tf_op jit(solution)/shard_map/ppermute | solution.py:486
  3.2 7.9 %collective-permute-start.4 = (bf16[5,64,128]{2,1,0:T(8,128)(2,1)S(1)}, bf16[5,64,128]{2,1,0:T(8,128)(2,1)S(1)}, u32[]{:S(2)}, u32[]{:S(2)}) collective-permute-start(bf16[5,64,128]{2,1,0:T(8,128)(2,1)S(1)} %get-tuple-element.66.refs_10_.refs_1_), channel_id=1, source_target_pairs={{0,1},{1,0},{2,3},{3,2},{4,5},{5,4},{6,7},{7,6},{8,9},{9,8},{10,11... | collective-permute-start | bytes 245768 | tf_op jit(solution)/shard_map/ppermute | solution.py:486
  3.7 6.0 %collective-permute-start = (bf16[4,64,128]{2,1,0:T(8,128)(2,1)S(1)}, bf16[4,64,128]{2,1,0:T(8,128)(2,1)S(1)}, u32[]{:S(2)}, u32[]{:S(2)}) collective-permute-start(bf16[4,64,128]{2,1,0:T(8,128)(2,1)S(1)} %get-tuple-element.55.refs_9_.refs_1_), channel_id=1, source_target_pairs={{0,1},{1,0},{2,3},{3,2},{4,5},{5,4},{6,7},{7,6},{8,9},{9,8},{10,11... | collective-permute-start | bytes 196616 | tf_op jit(solution)/shard_map/ppermute | solution.py:486
  12.6 4.6 %collective-permute-start.5 = (bf16[5,128,128]{2,1,0:T(8,128)(2,1)S(1)}, bf16[5,128,128]{2,1,0:T(8,128)(2,1)S(1)}, u32[]{:S(2)}, u32[]{:S(2)}) collective-permute-start(bf16[5,128,128]{2,1,0:T(8,128)(2,1)S(1)} %get-tuple-element.82), channel_id=1, source_target_pairs={{0,12},{1,13},{2,14},{3,15},{4,0},{5,1},{6,2},{7,3},{8,4},{9,5},{1... | collective-permute-start | bytes 491528 | tf_op jit(solution)/shard_map/ppermute | solution.py:486
  12.7 12.5 %collective-permute-start.2 = (bf16[416,128]{1,0:T(8,128)(2,1)S(1)}, bf16[416,128]{1,0:T(8,128)(2,1)S(1)}, u32[]{:S(2)}, u32[]{:S(2)}) collective-permute-start(bf16[416,128]{1,0:T(8,128)(2,1)S(1)} %get-tuple-element.77), channel_id=1, source_target_pairs={{0,3},{1,2},{2,1},{3,0},{4,7},{5,6},{6,5},{7,4},{8,11},{9,10},{10,... | collective-permute-start | bytes 319496 | tf_op jit(solution)/shard_map/ppermute | solution.py:486
  13.2 13.3 %collective-permute-start.3 = (bf16[416,128]{1,0:T(8,128)(2,1)S(1)}, bf16[416,128]{1,0:T(8,128)(2,1)S(1)}, u32[]{:S(2)}, u32[]{:S(2)}) collective-permute-start(bf16[416,128]{1,0:T(8,128)(2,1)S(1)} %get-tuple-element.78), channel_id=1, source_target_pairs={{0,15},{1,14},{2,13},{3,12},{4,3},{5,2},{6,1},{7,0},{8,7},{9,6},{1... | collective-permute-start | bytes 319496 | tf_op jit(solution)/shard_map/ppermute | solution.py:486
  15.4 15.5 %collective-permute-start.7 = (bf16[192,128]{1,0:T(8,128)(2,1)S(1)}, bf16[192,128]{1,0:T(8,128)(2,1)S(1)}, u32[]{:S(2)}, u32[]{:S(2)}) collective-permute-start(bf16[192,128]{1,0:T(8,128)(2,1)S(1)} %get-tuple-element.96), channel_id=1, source_target_pairs={{0,3},{1,2},{2,1},{3,0},{4,7},{5,6},{6,5},{7,4},{8,11},{9,10},{10,... | collective-permute-start | bytes 147464 | tf_op jit(solution)/shard_map/ppermute | solution.py:486
  15.9 15.0 %collective-permute-start.8 = (bf16[192,128]{1,0:T(8,128)(2,1)S(1)}, bf16[192,128]{1,0:T(8,128)(2,1)S(1)}, u32[]{:S(2)}, u32[]{:S(2)}) collective-permute-start(bf16[192,128]{1,0:T(8,128)(2,1)S(1)} %get-tuple-element.97), channel_id=1, source_target_pairs={{0,15},{1,14},{2,13},{3,12},{4,3},{5,2},{6,1},{7,0},{8,7},{9,6},{1... | collective-permute-start | bytes 147464 | tf_op jit(solution)/shard_map/ppermute | solution.py:486
  29.0 7.7 %collective-permute-start.6 = (bf16[5,80,128]{2,1,0:T(8,128)(2,1)S(1)}, bf16[5,80,128]{2,1,0:T(8,128)(2,1)S(1)}, u32[]{:S(2)}, u32[]{:S(2)}) collective-permute-start(bf16[5,80,128]{2,1,0:T(8,128)(2,1)S(1)} %get-tuple-element.95), channel_id=1, source_target_pairs={{0,4},{1,5},{2,6},{3,7},{4,8},{5,9},{6,10},{7,11},{8,12},{9,13},{1... | collective-permute-start | bytes 307208 | tf_op jit(solution)/shard_map/ppermute | solution.py:486
  33.1 3.7 %collective-permute-start.9 = (bf16[5,48,128]{2,1,0:T(8,128)(2,1)S(1)}, bf16[5,48,128]{2,1,0:T(8,128)(2,1)S(1)}, u32[]{:S(2)}, u32[]{:S(2)}) collective-permute-start(bf16[5,48,128]{2,1,0:T(8,128)(2,1)S(1)} %get-tuple-element.98), channel_id=1, source_target_pairs={{0,4},{1,5},{2,6},{3,7},{4,8},{5,9},{6,10},{7,11},{8,12},{9,13},{1... | collective-permute-start | bytes 184328 | tf_op jit(solution)/shard_map/ppermute | solution.py:486
